TPU v7x, 128 devices: a whole 4x4x4 slice. The times are simulated.
128 devices in a mesh: req: 16 (over z, y), kv: 8 (over x, core).
Axes of the slice: x: 4, y: 4, z: 4, core: 2. Of those that a mesh axis runs over, the one named last changes fastest.
Arguments:
- hidden_in: bfloat16 [16384, 2048], P(('req', 'kv')), may hold values from -6 to 6
- slot_tokens: int32 [16384], replicated, may hold values from 0 to 16383, as said below
- cache_len: int32 [128], P('req'), may hold values from 1 to 2048, 65536 in all
- prefill_start: int32 [16], P('req'), may hold values from 0 to 2048
- key_cache: bfloat16 [128, 2048, 1024], P('req', None, 'kv')
- value_cache: bfloat16 [128, 2048, 1024], P('req', None, 'kv'), may hold values from -18 to 18
- key_prefix: bfloat16 [16, 2048, 1024], P('req', None, 'kv')
- value_prefix: bfloat16 [16, 2048, 1024], P('req', None, 'kv'), may hold values from -18 to 18
- attn_gain: float32 [2048], replicated, may hold values from 0.25 to 1.75
- q_proj: bfloat16 [2048, 2048], P(None, 'kv'), may hold values from -0.125 to 0.125
- k_proj: bfloat16 [2048, 1024], P(None, 'kv'), may hold values from -0.125 to 0.125
- v_proj: bfloat16 [2048, 1024], P(None, 'kv'), may hold values from -0.125 to 0.125
- q_gain: float32 [128], replicated, may hold values from 0.25 to 1.75
- k_gain: float32 [128], replicated, may hold values from 0.25 to 1.75
- o_proj: bfloat16 [2048, 2048], P('kv'), may hold values from -0.125 to 0.125
- ffn_gain: float32 [2048], replicated, may hold values from 0.25 to 1.75
- w_gate: bfloat16 [2048, 6144], P(None, 'req'), may hold values from -0.125 to 0.125
- w_up: bfloat16 [2048, 6144], P(None, 'req'), may hold values from -0.125 to 0.125
- w_down: bfloat16 [6144, 2048], P('req'), may hold values from -0.078125 to 0.078125
- final_gain: float32 [2048], replicated, may hold values from 0.25 to 1.75
- lm_head: bfloat16 [2048, 151936], P(None, ('req', 'kv')), may hold values from -0.375 to 0.375
Outputs:
- layer_out: bfloat16 [16384, 2048], P(('req', 'kv'))
- max_logit: float32 [144], replicated
Inputs may be any that keep to these rules, and one draw needn't show every extreme that they name: slot_tokens is a permutation of the batch's tokens; each device's 128 consecutive slots take exactly 1 token from each device's 128 consecutive batch tokens.
All inputs are finite; a program needn't handle non-finite values. No bound on the sum of `cache_len` on one device may be relied on, other than what follows from the above.
Results may differ from a plain program's by a relative error of at most 0.0085.
The roundings to bfloat16 on the way count: a program that leaves them out, or rounds other values in their place, can miss the bound.
Values may be sent and summed in bfloat16 or wider, within the bound.
A program may use at most 128 MiB of HBM per device.

v0:
```python
import jax
import jax.numpy as jnp
from jax import lax
from jax.sharding import PartitionSpec as P

EPS = 1e-06
NEG = -1e30


def spread(value, axis, root):
    mine = lax.axis_index(axis) == root
    return lax.psum(jnp.where(mine, value, jnp.zeros_like(value)), axis)


def norm_rows(values, gain_vec):
    wide = values.astype(jnp.float32)
    return wide * lax.rsqrt(jnp.mean(wide * wide, axis=-1, keepdims=True) + EPS) * gain_vec


def rotate(values, places):
    half_dim = values.shape[-1] // 2
    freqs = 1000000.0 ** (-(jnp.arange(half_dim, dtype=jnp.float32) * 2.0 / values.shape[-1]))
    angles = places[:, None] * freqs[None, :]
    cosine = jnp.cos(angles)[:, None, :]
    sine = jnp.sin(angles)[:, None, :]
    first_half = values[..., :half_dim]
    second_half = values[..., half_dim:]
    return jnp.concatenate(
        [first_half * cosine - second_half * sine, second_half * cosine + first_half * sine],
        axis=-1,
    )


def prefill_full(q_heads, key_old, value_old, key_new, value_new, start_at):
    old_len = key_old.shape[0]
    fresh_rows = q_heads.shape[0]
    factor = q_heads.shape[-1] ** (-0.5)
    all_keys = jnp.concatenate([key_old, key_new], axis=0)
    all_values = jnp.concatenate([value_old, value_new], axis=0)
    scores = (
        jnp.einsum("cgd,kd->gck", q_heads, all_keys, preferred_element_type=jnp.float32) * factor
    )
    key_index = jnp.arange(old_len + fresh_rows, dtype=jnp.int32)[None, :]
    row_index = jnp.arange(fresh_rows, dtype=jnp.int32)[:, None]
    allowed = jnp.where(key_index < old_len, key_index < start_at, key_index - old_len <= row_index)
    scores = jnp.where(allowed[None], scores, NEG)
    row_peak = jnp.max(scores, axis=-1, keepdims=True)
    expd = jnp.exp(scores - row_peak)
    weights = (expd / jnp.sum(expd, axis=-1, keepdims=True)).astype(jnp.bfloat16)
    return jnp.einsum(
        "gck,kd->cgd", weights, all_values, preferred_element_type=jnp.float32
    ).astype(jnp.bfloat16)


def decode_attend(q_heads, key_old, value_old, key_self, value_self, lengths):
    factor = q_heads.shape[-1] ** (-0.5)
    past = jnp.einsum("bgd,bld->bgl", q_heads, key_old, preferred_element_type=jnp.float32) * factor
    slot_index = jnp.arange(key_old.shape[1], dtype=jnp.int32)
    past = jnp.where(slot_index[None, None, :] < lengths[:, None, None], past, NEG)
    own_score = (
        jnp.einsum("bgd,bd->bg", q_heads, key_self, preferred_element_type=jnp.float32) * factor
    )
    row_peak = jnp.maximum(jnp.max(past, axis=-1), own_score)
    past_exp = jnp.exp(past - row_peak[..., None])
    own_exp = jnp.exp(own_score - row_peak)
    row_total = jnp.sum(past_exp, axis=-1) + own_exp
    past_w = (past_exp / row_total[..., None]).astype(jnp.bfloat16)
    own_w = (own_exp / row_total).astype(jnp.bfloat16)
    summed = jnp.einsum("bgl,bld->bgd", past_w, value_old, preferred_element_type=jnp.float32)
    summed = (
        summed + own_w.astype(jnp.float32)[..., None] * value_self.astype(jnp.float32)[:, None, :]
    )
    return summed.astype(jnp.bfloat16)


def regroup(rows_in):
    return lax.all_to_all(rows_in, ("req", "kv"), split_axis=0, concat_axis=0, tiled=True)


def shards(
    hidden_in,
    slot_tokens,
    cache_len,
    prefill_start,
    key_cache,
    value_cache,
    key_prefix,
    value_prefix,
    attn_gain,
    q_proj,
    k_proj,
    v_proj,
    q_gain,
    k_gain,
    o_proj,
    ffn_gain,
    w_gate,
    w_up,
    w_down,
    final_gain,
    lm_head,
):
    req_count = lax.axis_size("req")
    kv_count = lax.axis_size("kv")
    devices = req_count * kv_count
    rows_dev = hidden_in.shape[0]
    per_pair = rows_dev // devices
    self_index = lax.axis_index("req") * kv_count + lax.axis_index("kv")
    slot_table = slot_tokens.reshape(devices, rows_dev)
    from_self = slot_table // rows_dev == self_index
    picked = jnp.argsort(jnp.where(from_self, 0, 1).astype(jnp.int32), axis=1, stable=True)[
        :, :per_pair
    ]
    send_rows = (jnp.take_along_axis(slot_table, picked, axis=1) - self_index * rows_dev).reshape(
        -1
    )
    own_sources = lax.dynamic_index_in_dim(slot_table, self_index, 0, keepdims=False) // rows_dev
    marks = (own_sources[:, None] == jnp.arange(devices, dtype=jnp.int32)[None, :]).astype(
        jnp.int32
    )
    ranks = jnp.sum(marks * (jnp.cumsum(marks, axis=0) - 1), axis=1)
    slot_place = own_sources * per_pair + ranks
    arrived = regroup(hidden_in[send_rows])
    owner_rows = arrived[slot_place]
    normed = norm_rows(owner_rows, attn_gain).astype(jnp.bfloat16)
    q_cols = q_proj.shape[1]
    kv_cols = k_proj.shape[1]
    rows_piece = lax.all_gather(normed, "kv", axis=0, tiled=True)
    projected = jnp.concatenate(
        [
            jnp.dot(rows_piece, q_proj, preferred_element_type=jnp.float32),
            jnp.dot(rows_piece, k_proj, preferred_element_type=jnp.float32),
            jnp.dot(rows_piece, v_proj, preferred_element_type=jnp.float32),
        ],
        axis=1,
    )
    tok_req = projected.shape[0]
    head_dim = q_gain.shape[0]
    dec_count = cache_len.shape[0]
    fresh_count = tok_req - dec_count
    q_raw = projected[:, :q_cols].reshape(tok_req, q_cols // head_dim, head_dim)
    k_raw = projected[:, q_cols : q_cols + kv_cols].reshape(tok_req, kv_cols // head_dim, head_dim)
    v_new = (
        projected[:, q_cols + kv_cols :]
        .astype(jnp.bfloat16)
        .reshape(tok_req, kv_cols // head_dim, head_dim)
    )
    places = jnp.concatenate(
        [prefill_start[0] + jnp.arange(fresh_count, dtype=jnp.int32), cache_len]
    ).astype(jnp.float32)
    queries = rotate(norm_rows(q_raw, q_gain), places).astype(jnp.bfloat16)
    keys_new = rotate(norm_rows(k_raw, k_gain), places).astype(jnp.bfloat16)
    pre_out = prefill_full(
        queries[:fresh_count],
        key_prefix[0, :, 0:head_dim],
        value_prefix[0, :, 0:head_dim],
        keys_new[:fresh_count, 0],
        v_new[:fresh_count, 0],
        prefill_start[0],
    )
    dec_out = decode_attend(
        queries[fresh_count:],
        key_cache,
        value_cache,
        keys_new[fresh_count:, 0],
        v_new[fresh_count:, 0],
        cache_len,
    )
    pieces = jnp.concatenate([pre_out, dec_out], axis=0)
    attended = pieces.reshape(tok_req, q_cols)
    attn_part = lax.psum_scatter(
        jnp.dot(attended, o_proj, preferred_element_type=jnp.float32),
        "kv",
        scatter_dimension=0,
        tiled=True,
    )
    resid = (owner_rows.astype(jnp.float32) + attn_part).astype(jnp.bfloat16)
    ffn_in = norm_rows(resid, ffn_gain).astype(jnp.bfloat16)
    rows_piece = lax.all_gather(ffn_in, "req", axis=0, tiled=True)
    gate_part = jnp.dot(rows_piece, w_gate, preferred_element_type=jnp.float32)
    up_part = jnp.dot(rows_piece, w_up, preferred_element_type=jnp.float32)
    hidden_act = (jax.nn.silu(gate_part) * up_part).astype(jnp.bfloat16)
    ffn_part = lax.psum_scatter(
        jnp.dot(hidden_act, w_down, preferred_element_type=jnp.float32),
        "req",
        scatter_dimension=0,
        tiled=True,
    )
    out_rows = (resid.astype(jnp.float32) + ffn_part).astype(jnp.bfloat16)
    going_back = jnp.zeros_like(out_rows).at[slot_place].set(out_rows)
    returned = regroup(going_back)
    layer_out = jnp.zeros_like(hidden_in).at[send_rows].set(returned)
    tail_rows = norm_rows(out_rows[rows_dev - dec_count - 1 :], final_gain).astype(jnp.bfloat16)
    tail_rows = spread(tail_rows, "kv", kv_count - 1)
    local_peaks = jnp.max(
        jnp.dot(
            lax.all_gather(tail_rows, "req", axis=0, tiled=True),
            lm_head,
            preferred_element_type=jnp.float32,
        ),
        axis=1,
    )
    max_logit = lax.pmax(local_peaks, ("req", "kv"))
    return (layer_out, max_logit)


def solution(mesh):
    placed = (
        P(("req", "kv"), None),
        P(),
        P("req"),
        P("req"),
        P("req", None, "kv"),
        P("req", None, "kv"),
        P("req", None, "kv"),
        P("req", None, "kv"),
        P(),
        P(None, "kv"),
        P(None, "kv"),
        P(None, "kv"),
        P(),
        P(),
        P("kv", None),
        P(),
        P(None, "req"),
        P(None, "req"),
        P("req", None),
        P(),
        P(None, ("req", "kv")),
    )
    return jax.shard_map(
        shards, mesh=mesh, in_specs=placed, out_specs=(P(("req", "kv"), None), P()), check_vma=False
    )
```

profile of v0, /device:TPU:0, one launch (start us, length us, event | category | flops | bytes accessed | tf_op | source)
XLA Modules:
  0.0 539.5 jit_solution(2482450521483599496)
XLA Ops:
  7.2 1.7 fusion.60
  11.1 4.7 sort.19.cloned.1.call-done
  17.0 1.9 gather_fusion.2
  23.6 11.1 %all-to-all-start = ((bf16[128,2,1024]{2,1,0:T(2,128)(2,1)}), bf16[128,2,1024]{2,1,0:T(2,128)(2,1)S(1)}, u32[]{:S(2)}, u32[]{:S(2)}) async-start(bf16[128,2,1024]{2,1,0:T(2,128)(2,1)} %reshape.484), calls=%async_computation | async-start | bytes 1048576 | tf_op jit(solution)/shard_map/all_to_all | solution.py:77
  35.6 12.8 %all-to-all-done = bf16[128,2,1024]{2,1,0:T(2,128)(2,1)S(1)} async-done(((bf16[128,2,1024]{2,1,0:T(2,128)(2,1)}), bf16[128,2,1024]{2,1,0:T(2,128)(2,1)S(1)}, u32[]{:S(2)}, u32[]{:S(2)}) %all-to-all-start) | async-done | bytes 524320 | tf_op jit(solution)/shard_map/all_to_all | solution.py:77
  48.3 1.7 reshape.485
  50.0 1.5 copy.105
  54.9 3.1 multiply_cosine_fusion
  58.0 4.2 fusion.4
  62.2 19.8 %all-gather.4.cloned.1.call-done = bf16[1024,2048]{1,0:T(8,128)(2,1)} async-done(((bf16[128,2048]{1,0:T(8,128)(2,1)}), bf16[1024,2048]{1,0:T(8,128)(2,1)}) %all-gather.4.cloned.1.call-update) | async-done | bytes 4194320 | tf_op jit(solution)/shard_map/all_gather | solution.py:128
  82.0 3.6 convolution_convert_fusion
  86.4 1.5 multiply_reduce_fusion.1
  89.3 2.3 multiply_reduce_fusion
  91.6 1.5 copy.81
  94.5 1.8 subtract_convert_fusion
  98.3 2.9 fusion.43
  101.3 15.9 %fusion.84 = (f32[2,1016]{1,0:T(2,128)S(1)}, f32[2,1016,3064]{2,1,0:T(8,128)}) fusion(pred[1016,3064]{1,0:T(8,128)(4,1)} %fusion.4, bf16[1016,128]{1,0:T(8,128)(2,1)} %copy.80, bf16[2048,128]{1,0:T(8,128)(2,1)} %bitcast.105, bf16[1024,2,64]{2,0,1:T(8,128)(2,1)S(1)} %get-tuple-element.6, bf16[1024,2,64]{2,0,1:T(8,128)(2,1)S(1)} %get-tuple-element.7), kind=kOutput, calls=%fused_computation.161 | convolution fusion | flops 1621384704 | bytes 29334016 | tf_op jit(solution)/shard_map/sub | solution.py:48
  117.2 11.7 %fusion.12 = bf16[1016,2,128]{2,0,1:T(8,128)(2,1)S(1)} fusion(f32[2,1016,3064]{2,1,0:T(8,128)} %get-tuple-element.21, f32[2,1016]{1,0:T(2,128)S(1)} %get-tuple-element.20, bf16[1016,128]{1,0:T(8,128)(2,1)S(1)} %copy-done.5, bf16[2048,128]{1,0:T(8,128)(2,1)} %bitcast.106), kind=kOutput, calls=%fused_computation.28 | convolution fusion | flops 1608149248 | bytes 26216896 | tf_op jit(solution)/shard_map/gck,kd->cgd/dot_general | solution.py:50
  129.2 5.7 %fusion.89 = f32[1024,2048]{1,0:T(8,128)} fusion(bf16[1024,256]{0,1:T(8,128)(2,1)S(1)} %bitcast.94, bf16[256,2048]{1,0:T(8,128)(2,1)} %param.35), kind=kOutput, calls=%fused_computation.162 | convolution fusion | flops 1073741824 | bytes 9961472 | tf_op jit(solution)/shard_map/dot_general | solution.py:172
  135.0 52.5 %reduce-scatter.3.cloned.1.call-done = f32[128,2048]{1,0:T(8,128)} async-done(((f32[1024,2048]{1,0:T(8,128)}), f32[128,2048]{1,0:T(8,128)}) %reduce-scatter.3.cloned.1.call-update) | async-done | bytes 1048592 | tf_op jit(solution)/shard_map/reduce_scatter | solution.py:171
  187.4 1.5 fusion.17
  190.1 70.6 %all-gather.6.cloned.1.call-done = bf16[2048,2048]{1,0:T(8,128)(2,1)} async-done(((bf16[128,2048]{1,0:T(8,128)(2,1)}), bf16[2048,2048]{1,0:T(8,128)(2,1)}) %all-gather.6.cloned.1.call-update) | async-done | bytes 8388624 | tf_op jit(solution)/shard_map/all_gather | solution.py:179
  260.8 10.1 %fusion.90 = f32[2048,384]{1,0:T(8,128)} fusion(bf16[2048,2048]{1,0:T(8,128)(2,1)} %all-gather.6.cloned.1.call-done, bf16[2048,384]{1,0:T(8,128)(2,1)} %param.37), kind=kOutput, calls=%fused_computation.163 | convolution fusion | flops 3221225472 | bytes 13107200 | tf_op jit(solution)/shard_map/dot_general | solution.py:180
  270.8 15.4 %fusion.10 = f32[2048,2048]{1,0:T(8,128)} fusion(bf16[384,2048]{1,0:T(8,128)(2,1)S(1)} %copy-done, f32[2048,384]{1,0:T(8,128)} %fusion.90, bf16[2048,2048]{1,0:T(8,128)(2,1)} %all-gather.6.cloned.1.call-done, bf16[2048,384]{1,0:T(8,128)(2,1)} %param.38), kind=kOutput, calls=%fused_computation.26 | convolution fusion | flops 6447169536 | bytes 31457280 | tf_op jit(solution)/shard_map/dot_general | solution.py:184
  286.3 110.5 %reduce-scatter.5.cloned.1.call-done = f32[128,2048]{1,0:T(8,128)} async-done(((f32[2048,2048]{1,0:T(8,128)}), f32[128,2048]{1,0:T(8,128)}) %reduce-scatter.5.cloned.1.call-update) | async-done | bytes 1048592 | tf_op jit(solution)/shard_map/reduce_scatter | solution.py:183
  398.2 1.5 scatter_custom_fusion
  402.0 25.6 %psum.7 = bf16[9,2048]{1,0:T(8,128)(2,1)S(1)} all-reduce(bf16[9,2048]{1,0:T(8,128)(2,1)S(1)} %fusion.48), channel_id=1, replica_groups=mesh['req'=16,'kv'=8] {'kv'}, use_global_device_ids=true, to_apply=%region_16.17 | all-reduce | flops 18432 | bytes 73728 | tf_op jit(solution)/shard_map/psum | solution.py:12
  427.6 6.1 %all-to-all-start.1 = ((bf16[128,2,1024]{2,1,0:T(2,128)(2,1)}), bf16[128,2,1024]{2,1,0:T(2,128)(2,1)S(1)}, u32[]{:S(2)}, u32[]{:S(2)}) async-start(bf16[128,2,1024]{2,1,0:T(2,128)(2,1)} %reshape.486), calls=%async_computation.3 | async-start | bytes 1048576 | tf_op jit(solution)/shard_map/all_to_all | solution.py:77
  433.7 26.2 %all-gather = bf16[16,9,2048]{2,1,0:T(8,128)(2,1)S(1)} all-gather(bf16[1,9,2048]{2,1,0:T(8,128)(2,1)S(1)} %bitcast.99), channel_id=1, replica_groups=mesh['req'=16,'kv'=8] {'req'}, dimensions={0}, use_global_device_ids=true | all-gather | bytes 626688 | tf_op jit(solution)/shard_map/all_gather | solution.py:197
  461.0 4.4 convolution_reduce_fusion
  465.3 64.6 %pmax.7 = f32[144]{0:T(256)} all-reduce(f32[144]{0:T(256)S(1)} %convolution_reduce_fusion), channel_id=1, replica_groups=mesh['req'=16,'kv'=8] {'req','kv'}, use_global_device_ids=true, to_apply=%region_18.19 | all-reduce | flops 144 | bytes 1152 | tf_op jit(solution)/shard_map/pmax | solution.py:203
  530.4 2.4 scatter_custom_fusion.1
  (102 shorter events, 23.8 us)
Async XLA Ops:
  7.2 263.7 %copy-start = (bf16[384,2048]{1,0:T(8,128)(2,1)S(1)}, bf16[384,2048]{1,0:T(8,128)(2,1)}, u32[]{:S(2)}) copy-start(bf16[384,2048]{1,0:T(8,128)(2,1)} %param.39) | copy-start | bytes 4718596
  7.2 12.8 %copy-start.1 = (bf16[128,2048]{1,0:T(8,128)(2,1)S(1)}, bf16[128,2048]{1,0:T(8,128)(2,1)}, u32[]{:S(2)}) copy-start(bf16[128,2048]{1,0:T(8,128)(2,1)} %param.21) | copy-start | bytes 1572868
  7.2 8.5 %sort.19.cloned.1.call-start = ((), (), s32[]{:S(2)}) async-start(), calls=%async_computation.8 | async-start | bytes 393248 | tf_op jit(solution)/shard_map/jit(argsort)/sort | solution.py:111
  23.6 24.7 %all-to-all-start = ((bf16[128,2,1024]{2,1,0:T(2,128)(2,1)}), bf16[128,2,1024]{2,1,0:T(2,128)(2,1)S(1)}, u32[]{:S(2)}, u32[]{:S(2)}) async-start(bf16[128,2,1024]{2,1,0:T(2,128)(2,1)} %reshape.484), calls=%async_computation | async-start | bytes 1048576 | tf_op jit(solution)/shard_map/all_to_all | solution.py:77
  34.8 47.2 %all-gather.4.cloned.1.call-start = ((), (), s32[]{:S(2)}) async-start(), calls=%async_computation.4 | async-start | bytes 4718592 | tf_op jit(solution)/shard_map/all_gather | solution.py:128
  35.5 17.2 %copy-start.6 = (f32[2048]{0:T(1024)S(1)}, f32[2048]{0:T(1024)}, u32[]{:S(2)}) copy-start(f32[2048]{0:T(1024)} %param.29) | copy-start | bytes 24580
  50.0 4.7 copy-start.9
  52.5 29.5 %copy-start.13 = (bf16[2048,128]{1,0:T(8,128)(2,1)S(1)}, bf16[2048,128]{1,0:T(8,128)(2,1)}, u32[]{:S(2)}) copy-start(bf16[2048,128]{1,0:T(8,128)(2,1)} %param.32) | copy-start | bytes 1572868
  53.7 133.7 %reduce-scatter.3.cloned.1.call-start = ((), (), s32[]{:S(2)}) async-start(), calls=%async_computation.5 | async-start | bytes 9437184 | tf_op jit(solution)/shard_map/reduce_scatter | solution.py:171
  62.2 24.2 %copy-start.4 = (bf16[2048,128]{1,0:T(8,128)(2,1)S(1)}, bf16[2048,128]{1,0:T(8,128)(2,1)}, u32[]{:S(2)}) copy-start(bf16[2048,128]{1,0:T(8,128)(2,1)} %param.31) | copy-start | bytes 1572868
  82.0 4.4 copy-start.3
  85.6 2.3 copy-start.10
  85.6 3.7 copy-start.12
  89.3 4.8 copy-start.11
  94.2 2.5 copy-start.2
  101.3 15.9 %copy-start.5 = (bf16[1016,128]{1,0:T(8,128)(2,1)S(1)}, bf16[1016,128]{1,0:T(8,128)(2,1)}, u32[]{:S(2)}) copy-start(bf16[1016,128]{1,0:T(8,128)(2,1)} %slice.58) | copy-start | bytes 780292
  134.9 54.0 %copy-start.7 = (f32[2048]{0:T(1024)S(1)}, f32[2048]{0:T(1024)}, u32[]{:S(2)}) copy-start(f32[2048]{0:T(1024)} %param.36) | copy-start | bytes 24580
  134.9 125.8 %all-gather.6.cloned.1.call-start = ((), (), s32[]{:S(2)}) async-start(), calls=%async_computation.6 | async-start | bytes 8912896 | tf_op jit(solution)/shard_map/all_gather | solution.py:179
  189.9 206.8 %reduce-scatter.5.cloned.1.call-start = ((), (), s32[]{:S(2)}) async-start(), calls=%async_computation.7 | async-start | bytes 17825792 | tf_op jit(solution)/shard_map/reduce_scatter | solution.py:183
  286.3 115.7 %copy-start.8 = (f32[2048]{0:T(1024)S(1)}, f32[2048]{0:T(1024)}, u32[]{:S(2)}) copy-start(f32[2048]{0:T(1024)} %param.40) | copy-start | bytes 24580
  427.6 102.3 %all-to-all-start.1 = ((bf16[128,2,1024]{2,1,0:T(2,128)(2,1)}), bf16[128,2,1024]{2,1,0:T(2,128)(2,1)S(1)}, u32[]{:S(2)}, u32[]{:S(2)}) async-start(bf16[128,2,1024]{2,1,0:T(2,128)(2,1)} %reshape.486), calls=%async_computation.3 | async-start | bytes 1048576 | tf_op jit(solution)/shard_map/all_to_all | solution.py:77
Sparse Core Ops, SparseCore 0:
  10.8 4.6 sort.21.cloned.1.call-done
  53.9 28.0 all-gather.3
  135.0 52.3 reduce-scatter.2
  190.2 70.4 all-gather.5
  286.4 110.3 reduce-scatter.4
  (1 shorter events, 0.0 us)
where the time goes:
time: 545 us; the launch traced here: 540 us
  waiting for transfers between devices  266 us (49%)
  blocking collectives  116 us (21%)
  matrix products  74.9 us (14%)
  local copies, waits for them, and re-layouts  25.6 us (5%)
  other arithmetic  23.6 us (4%)
  starting transfers between devices  17.9 us (3%)
  between operations  15 us (3%)
    reduce_scatter x1, waiting for transfers between devices, shards(): lax.psum_scatter(jnp.dot(hidden_act, w_down, preferred_element_type=jnp.f...  110 us
    all_gather x1, waiting for transfers between devices, shards(): rows_piece = lax.all_gather(ffn_in, 'req', axis=0, tiled=True)  70.6 us
    pmax x1, blocking collectives, shards(): max_logit = lax.pmax(local_peaks, ('req', 'kv'))  64.6 us
    reduce_scatter x1, waiting for transfers between devices, shards(): lax.psum_scatter(jnp.dot(attended, o_proj, preferred_element_type=jnp.flo...  52.5 us
    all_gather x1, blocking collectives, shards(): lax.all_gather(tail_rows, 'req', axis=0, tiled=True)  26.2 us
    psum x1, blocking collectives, spread(): return lax.psum(jnp.where(mine, value, jnp.zeros_like(value)), axis)  25.6 us
    all_gather x1, waiting for transfers between devices, shards(): rows_piece = lax.all_gather(normed, 'kv', axis=0, tiled=True)  19.8 us
    all_to_all x2, starting transfers between devices, regroup(): lax.all_to_all(rows_in, ('req', 'kv'), split_axis=0, concat_axis=0, tiled...  17.3 us
  transfers between devices with their start and end apart: 6, of which 5 were waited for; matrix products, arithmetic and copies ran while one was open for 3% of the time, Pallas kernels for 0%

commit v1 on v0

--- a/solution.py
+++ b/solution.py
@@ -104,33 +104,35 @@
     kv_count = lax.axis_size("kv")
     devices = req_count * kv_count
     rows_dev = hidden_in.shape[0]
-    per_pair = rows_dev // devices
-    self_index = lax.axis_index("req") * kv_count + lax.axis_index("kv")
+    kv_index = lax.axis_index("kv")
+    self_index = lax.axis_index("req") * kv_count + kv_index
     slot_table = slot_tokens.reshape(devices, rows_dev)
     from_self = slot_table // rows_dev == self_index
-    picked = jnp.argsort(jnp.where(from_self, 0, 1).astype(jnp.int32), axis=1, stable=True)[
-        :, :per_pair
-    ]
-    send_rows = (jnp.take_along_axis(slot_table, picked, axis=1) - self_index * rows_dev).reshape(
-        -1
-    )
-    own_sources = lax.dynamic_index_in_dim(slot_table, self_index, 0, keepdims=False) // rows_dev
-    marks = (own_sources[:, None] == jnp.arange(devices, dtype=jnp.int32)[None, :]).astype(
-        jnp.int32
-    )
-    ranks = jnp.sum(marks * (jnp.cumsum(marks, axis=0) - 1), axis=1)
-    slot_place = own_sources * per_pair + ranks
+    send_rows = jnp.sum(jnp.where(from_self, slot_table - self_index * rows_dev, 0), axis=1)
+    slot_place = lax.dynamic_index_in_dim(slot_table, self_index, 0, keepdims=False) // rows_dev
     arrived = regroup(hidden_in[send_rows])
     owner_rows = arrived[slot_place]
-    normed = norm_rows(owner_rows, attn_gain).astype(jnp.bfloat16)
+    rows_all = lax.all_gather(owner_rows, "kv", axis=0, tiled=True)
+    normed = norm_rows(rows_all, attn_gain).astype(jnp.bfloat16)
+    o_full = lax.all_gather(o_proj, "kv", axis=0, tiled=True)
+    ff_dev = w_gate.shape[1]
+    ff_piece = ff_dev // kv_count
+    gate_w = lax.all_gather(
+        lax.dynamic_slice_in_dim(w_gate, kv_index * ff_piece, ff_piece, axis=1), "req", axis=1, tiled=True
+    )
+    up_w = lax.all_gather(
+        lax.dynamic_slice_in_dim(w_up, kv_index * ff_piece, ff_piece, axis=1), "req", axis=1, tiled=True
+    )
+    down_w = lax.all_gather(
+        lax.dynamic_slice_in_dim(w_down, kv_index * ff_piece, ff_piece, axis=0), "req", axis=0, tiled=True
+    )
     q_cols = q_proj.shape[1]
     kv_cols = k_proj.shape[1]
-    rows_piece = lax.all_gather(normed, "kv", axis=0, tiled=True)
     projected = jnp.concatenate(
         [
-            jnp.dot(rows_piece, q_proj, preferred_element_type=jnp.float32),
-            jnp.dot(rows_piece, k_proj, preferred_element_type=jnp.float32),
-            jnp.dot(rows_piece, v_proj, preferred_element_type=jnp.float32),
+            jnp.dot(normed, q_proj, preferred_element_type=jnp.float32),
+            jnp.dot(normed, k_proj, preferred_element_type=jnp.float32),
+            jnp.dot(normed, v_proj, preferred_element_type=jnp.float32),
         ],
         axis=1,
     )
@@ -167,31 +169,25 @@
         cache_len,
     )
     pieces = jnp.concatenate([pre_out, dec_out], axis=0)
-    attended = pieces.reshape(tok_req, q_cols)
-    attn_part = lax.psum_scatter(
-        jnp.dot(attended, o_proj, preferred_element_type=jnp.float32),
-        "kv",
-        scatter_dimension=0,
-        tiled=True,
-    )
-    resid = (owner_rows.astype(jnp.float32) + attn_part).astype(jnp.bfloat16)
+    pieces, gate_w, up_w, down_w = lax.optimization_barrier((pieces, gate_w, up_w, down_w))
+    attended = lax.all_gather(pieces.reshape(tok_req, q_cols), "kv", axis=1, tiled=True)
+    resid = (
+        rows_all.astype(jnp.float32) + jnp.dot(attended, o_full, preferred_element_type=jnp.float32)
+    ).astype(jnp.bfloat16)
     ffn_in = norm_rows(resid, ffn_gain).astype(jnp.bfloat16)
-    rows_piece = lax.all_gather(ffn_in, "req", axis=0, tiled=True)
-    gate_part = jnp.dot(rows_piece, w_gate, preferred_element_type=jnp.float32)
-    up_part = jnp.dot(rows_piece, w_up, preferred_element_type=jnp.float32)
+    gate_part = jnp.dot(ffn_in, gate_w, preferred_element_type=jnp.float32)
+    up_part = jnp.dot(ffn_in, up_w, preferred_element_type=jnp.float32)
     hidden_act = (jax.nn.silu(gate_part) * up_part).astype(jnp.bfloat16)
-    ffn_part = lax.psum_scatter(
-        jnp.dot(hidden_act, w_down, preferred_element_type=jnp.float32),
-        "req",
-        scatter_dimension=0,
-        tiled=True,
-    )
-    out_rows = (resid.astype(jnp.float32) + ffn_part).astype(jnp.bfloat16)
+    down_part = jnp.dot(hidden_act, down_w, preferred_element_type=jnp.float32)
+    ffn_part = lax.psum_scatter(down_part, "kv", scatter_dimension=0, tiled=True)
+    mine = lax.dynamic_slice_in_dim(resid, kv_index * rows_dev, rows_dev, axis=0)
+    out_rows = (mine.astype(jnp.float32) + ffn_part).astype(jnp.bfloat16)
     going_back = jnp.zeros_like(out_rows).at[slot_place].set(out_rows)
     returned = regroup(going_back)
     layer_out = jnp.zeros_like(hidden_in).at[send_rows].set(returned)
-    tail_rows = norm_rows(out_rows[rows_dev - dec_count - 1 :], final_gain).astype(jnp.bfloat16)
-    tail_rows = spread(tail_rows, "kv", kv_count - 1)
+    tail_sum = lax.psum(down_part[fresh_count - 1 :], "kv")
+    tail_out = (resid[fresh_count - 1 :].astype(jnp.float32) + tail_sum).astype(jnp.bfloat16)
+    tail_rows = norm_rows(tail_out, final_gain).astype(jnp.bfloat16)
     local_peaks = jnp.max(
         jnp.dot(
             lax.all_gather(tail_rows, "req", axis=0, tiled=True),

time: 545 us -> 578 us (1.061)
  waiting for transfers between devices: 266 us -> 321 us
  blocking collectives: 116 us -> 90.5 us
    reduce_scatter x2 -> x1, waiting for transfers between devices: 163 us -> 52 us  [shards(): lax.psum_scatter(down_part, 'kv', scatter_dimension=0, tiled=True)]
    all_gather x2 -> x6, waiting for transfers between devices: 90.4 us -> 196 us  [the longest x1 49 us: shards(): o_full = lax.all_gather(o_proj, 'kv', axis=0, tiled=True)]
    psum x0 -> x1, waiting for transfers between devices: none -> 58.5 us  [shards(): tail_sum = lax.psum(down_part[fresh_count - 1:], 'kv')]
    psum x1 -> x0, blocking collectives: 25.6 us -> none  [spread(): return lax.psum(jnp.where(mine, value, jnp.zeros_like(value)), axis)]
    dot_general x6, matrix products: 38.6 us -> 45 us  [the longest x1 14.2 us: shards(): jnp.dot(attended, o_full, preferred_element_type=jnp.float32)]
  transfers between devices with their start and end apart: 6 -> 10, of which waited for: 5 -> 8; matrix products, arithmetic and copies ran while one was open for 3% -> 12% of each run, Pallas kernels for 0% -> 0%
where the time goes in v1:
time: 578 us; the launch traced here: 573 us
  waiting for transfers between devices  321 us (56%)
  blocking collectives  90.5 us (16%)
  matrix products  79.3 us (14%)
  local copies, waits for them, and re-layouts  24.9 us (4%)
  other arithmetic  21.6 us (4%)
  starting transfers between devices  20.3 us (4%)
  between operations  15.5 us (3%)
    pmax x1, blocking collectives, shards(): max_logit = lax.pmax(local_peaks, ('req', 'kv'))  64.3 us
    psum x1, waiting for transfers between devices, shards(): tail_sum = lax.psum(down_part[fresh_count - 1:], 'kv')  58.5 us
    reduce_scatter x1, waiting for transfers between devices, shards(): lax.psum_scatter(down_part, 'kv', scatter_dimension=0, tiled=True)  52 us
    all_gather x1, waiting for transfers between devices, shards(): o_full = lax.all_gather(o_proj, 'kv', axis=0, tiled=True)  49 us
    all_gather x1, waiting for transfers between devices, shards(): lax.all_gather(lax.dynamic_slice_in_dim(w_up, kv_index * ff_piece, ff_pie...  49 us
    all_gather x1, waiting for transfers between devices, shards(): lax.all_gather(lax.dynamic_slice_in_dim(w_down, kv_index * ff_piece, ff_p...  48.9 us
    all_gather x1, waiting for transfers between devices, shards(): lax.all_gather(pieces.reshape(tok_req, q_cols), 'kv', axis=1, tiled=True)  34.5 us
    all_gather x1, blocking collectives, shards(): lax.all_gather(tail_rows, 'req', axis=0, tiled=True)  26.2 us
  transfers between devices with their start and end apart: 10, of which 8 were waited for; matrix products, arithmetic and copies ran while one was open for 12% of the time, Pallas kernels for 0%

profile of v1, /device:TPU:0, one launch (start us, length us, event | category | flops | bytes accessed | tf_op | source)
XLA Modules:
  0.0 572.9 jit_solution(5138658079195809557)
XLA Ops:
  8.3 2.6 gather_fusion
  13.5 11.1 %all-to-all-start = ((bf16[128,2,1024]{2,1,0:T(2,128)(2,1)}), bf16[128,2,1024]{2,1,0:T(2,128)(2,1)S(1)}, u32[]{:S(2)}, u32[]{:S(2)}) async-start(bf16[128,2,1024]{2,1,0:T(2,128)(2,1)} %reshape.450), calls=%async_computation | async-start | bytes 1048576 | tf_op jit(solution)/shard_map/all_to_all | solution.py:77
  25.4 12.8 %all-to-all-done = bf16[128,2,1024]{2,1,0:T(2,128)(2,1)S(1)} async-done(((bf16[128,2,1024]{2,1,0:T(2,128)(2,1)}), bf16[128,2,1024]{2,1,0:T(2,128)(2,1)S(1)}, u32[]{:S(2)}, u32[]{:S(2)}) %all-to-all-start) | async-done | bytes 524320 | tf_op jit(solution)/shard_map/all_to_all | solution.py:77
  39.0 1.7 gather_fusion.1
  44.3 1.6 constant_dynamic-slice_fusion
  47.9 1.9 multiply_cosine_fusion
  49.9 4.0 fusion.4
  53.9 15.0 %all-gather.19.cloned.1.call-done = bf16[1024,2048]{1,0:T(8,128)(2,1)} async-done(((bf16[128,2048]{1,0:T(8,128)(2,1)}), bf16[1024,2048]{1,0:T(8,128)(2,1)}) %all-gather.19.cloned.1.call-update) | async-done | bytes 4194320 | tf_op jit(solution)/shard_map/all_gather | solution.py:115
  69.0 3.2 fusion.10
  73.7 2.3 multiply_reduce_fusion
  76.0 1.6 copy.48
  77.6 3.7 multiply_reduce_fusion.1
  87.0 3.6 convolution_convert_fusion
  91.4 15.9 %fusion.78 = (f32[2,1016]{1,0:T(2,128)S(1)}, f32[2,1016,3064]{2,1,0:T(8,128)}) fusion(pred[1016,3064]{1,0:T(8,128)(4,1)} %fusion.4, bf16[1016,128]{1,0:T(8,128)(2,1)S(1)} %copy.47, bf16[2048,128]{1,0:T(8,128)(2,1)S(1)} %bitcast.93, bf16[1024,2,64]{2,0,1:T(8,128)(2,1)S(1)} %get-tuple-element.10, bf16[1024,2,64]{2,0,1:T(8,128)(2,1)S(1)} %get-tuple-element.11), kind=kOutput, calls=%fused_computation.144 | convolution fusion | flops 1621384704 | bytes 29334016 | tf_op jit(solution)/shard_map/sub | solution.py:48
  107.3 12.0 %fusion.18 = bf16[1016,2,128]{2,0,1:T(8,128)(2,1)S(1)} fusion(f32[2,1016,3064]{2,1,0:T(8,128)} %get-tuple-element.25, f32[2,1016]{1,0:T(2,128)S(1)} %get-tuple-element.24, bf16[1016,128]{1,0:T(8,128)(2,1)S(1)} %slice.54, bf16[2048,128]{1,0:T(8,128)(2,1)S(1)} %bitcast.94), kind=kOutput, calls=%fused_computation.32 | convolution fusion | flops 1608149248 | bytes 26216896 | tf_op jit(solution)/shard_map/gck,kd->cgd/dot_general | solution.py:50
  119.4 49.0 %all-gather.11.cloned.1.call-done = bf16[2048,768]{0,1:T(8,128)(2,1)} async-done(((bf16[2048,48]{0,1:T(8,128)(2,1)}), bf16[2048,768]{0,1:T(8,128)(2,1)}) %all-gather.11.cloned.1.call-update) | async-done | bytes 3145744 | tf_op jit(solution)/shard_map/all_gather | solution.py:123
  168.3 48.9 %all-gather.13.cloned.1.call-done = bf16[768,2048]{1,0:T(8,128)(2,1)} async-done(((bf16[48,2048]{1,0:T(8,128)(2,1)}), bf16[768,2048]{1,0:T(8,128)(2,1)}) %all-gather.13.cloned.1.call-update) | async-done | bytes 3145744 | tf_op jit(solution)/shard_map/all_gather | solution.py:126
  218.3 49.0 %all-gather.17.cloned.1.call-done = bf16[2048,2048]{1,0:T(8,128)(2,1)} async-done(((bf16[256,2048]{1,0:T(8,128)(2,1)}), bf16[2048,2048]{1,0:T(8,128)(2,1)}) %all-gather.17.cloned.1.call-update) | async-done | bytes 8388624 | tf_op jit(solution)/shard_map/all_gather | solution.py:117
  267.3 34.5 %all-gather.15.cloned.1.call-done = bf16[1024,2048]{0,1:T(8,128)(2,1)} async-done(((bf16[1024,256]{0,1:T(8,128)(2,1)}), bf16[1024,2048]{0,1:T(8,128)(2,1)}) %all-gather.15.cloned.1.call-update) | async-done | bytes 4194320 | tf_op jit(solution)/shard_map/all_gather | solution.py:173
  301.7 14.2 %fusion.7 = (f32[1024]{0:T(1024)S(1)}, bf16[1024,2048]{1,0:T(8,128)(2,1)S(1)}) fusion(bf16[1024,2048]{0,1:T(8,128)(2,1)} %all-gather.15.cloned.1.call-done, bf16[2048,2048]{1,0:T(8,128)(2,1)} %all-gather.17.cloned.1.call-done, bf16[1024,2048]{1,0:T(8,128)(2,1)} %all-gather.19.cloned.1.call-done), kind=kOutput, calls=%fused_computation.20 | convolution fusion | flops 8602516480 | bytes 20975616 | tf_op jit(solution)/shard_map/dot_general | solution.py:175
  315.9 1.9 copy-done.7
  317.9 7.1 %fusion.20 = f32[1024,768]{1,0:T(8,128)} fusion(bf16[2048,768]{0,1:T(8,128)(2,1)} %all-gather.9.cloned.1.call-done, bf16[1024,2048]{1,0:T(8,128)(2,1)S(1)} %get-tuple-element.27, f32[2048]{0:T(1024)S(1)} %copy-done.17, f32[1024]{0:T(1024)S(1)} %add_rsqrt_fusion.1), kind=kOutput, calls=%fused_computation.33 | convolution fusion | flops 3229614080 | bytes 10498048 | tf_op jit(solution)/shard_map/dot_general | solution.py:178
  325.0 14.1 %fusion.23 = f32[1024,2048]{1,0:T(8,128)} fusion(bf16[768,2048]{1,0:T(8,128)(2,1)} %all-gather.13.cloned.1.call-done, f32[1024,768]{1,0:T(8,128)} %fusion.20, bf16[2048,768]{0,1:T(8,128)(2,1)} %all-gather.11.cloned.1.call-done, bf16[1024,2048]{1,0:T(8,128)(2,1)} %copy-done.7, f32[2048]{0:T(1024)S(1)} %copy-done.17, f32[1024]{0:T(1024)S(1)} %add_rsqrt_fusion.1), kind=kOutput, calls=%fused_computation.34 | convolution fusion | flops 6455558144 | bytes 22032384 | tf_op jit(solution)/shard_map/dot_general | solution.py:181
  339.0 1.6 slice.65
  341.4 58.5 %all-reduce.2.cloned.1.call-done = f32[9,2048]{1,0:T(8,128)} async-done(((f32[9,2048]{1,0:T(8,128)}), f32[9,2048]{1,0:T(8,128)}) %all-reduce.2.cloned.1.call-update) | async-done | bytes 73744 | tf_op jit(solution)/shard_map/psum | solution.py:188
  402.0 52.0 %reduce-scatter.2.cloned.1.call-done = f32[128,2048]{1,0:T(8,128)} async-done(((f32[1024,2048]{1,0:T(8,128)}), f32[128,2048]{1,0:T(8,128)}) %reduce-scatter.2.cloned.1.call-update) | async-done | bytes 1048592 | tf_op jit(solution)/shard_map/reduce_scatter | solution.py:182
  453.9 2.6 scatter_custom_fusion
  458.7 8.3 %all-to-all-start.1 = ((bf16[128,2,1024]{2,1,0:T(2,128)(2,1)}), bf16[128,2,1024]{2,1,0:T(2,128)(2,1)S(1)}, u32[]{:S(2)}, u32[]{:S(2)}) async-start(bf16[128,2,1024]{2,1,0:T(2,128)(2,1)} %reshape.452), calls=%async_computation.2 | async-start | bytes 1048576 | tf_op jit(solution)/shard_map/all_to_all | solution.py:77
  467.0 26.2 %all-gather.1 = bf16[16,9,2048]{2,1,0:T(8,128)(2,1)S(1)} all-gather(bf16[1,9,2048]{2,1,0:T(8,128)(2,1)S(1)} %fusion.51), channel_id=1, replica_groups=mesh['req'=16,'kv'=8] {'req'}, dimensions={0}, use_global_device_ids=true | all-gather | bytes 626688 | tf_op jit(solution)/shard_map/all_gather | solution.py:193
  494.2 4.4 convolution_reduce_fusion
  498.6 64.3 %pmax.7 = f32[144]{0:T(256)} all-reduce(f32[144]{0:T(256)S(1)} %convolution_reduce_fusion), channel_id=1, replica_groups=mesh['req'=16,'kv'=8] {'req','kv'}, use_global_device_ids=true, to_apply=%region_15.16 | all-reduce | flops 144 | bytes 1152 | tf_op jit(solution)/shard_map/pmax | solution.py:199
  563.4 2.4 scatter_custom_fusion.1
  (106 shorter events, 25.8 us)
Async XLA Ops:
  7.2 33.6 %copy-start = (bf16[2048,384]{1,0:T(8,128)(2,1)S(1)}, bf16[2048,384]{1,0:T(8,128)(2,1)}, u32[]{:S(2)}) copy-start(bf16[2048,384]{1,0:T(8,128)(2,1)} %param.37) | copy-start | bytes 4718596
  13.5 24.7 %all-to-all-start = ((bf16[128,2,1024]{2,1,0:T(2,128)(2,1)}), bf16[128,2,1024]{2,1,0:T(2,128)(2,1)S(1)}, u32[]{:S(2)}, u32[]{:S(2)}) async-start(bf16[128,2,1024]{2,1,0:T(2,128)(2,1)} %reshape.450), calls=%async_computation | async-start | bytes 1048576 | tf_op jit(solution)/shard_map/all_to_all | solution.py:77
  24.7 44.3 %all-gather.19.cloned.1.call-start = ((), (), s32[]{:S(2)}) async-start(), calls=%async_computation.10 | async-start | bytes 4718592 | tf_op jit(solution)/shard_map/all_gather | solution.py:115
  40.7 7.1 %copy-start.10 = (s32[8]{0:T(128)S(1)}, s32[8]{0:T(128)}, u32[]{:S(2)}) copy-start(s32[8]{0:T(128)} %param.23) | copy-start | bytes 100
  40.7 78.6 %all-gather.9.cloned.1.call-start = ((), (), s32[]{:S(2)}) async-start(), calls=%async_computation.3 | async-start | bytes 3342336 | tf_op jit(solution)/shard_map/all_gather | solution.py:120
  41.9 126.4 %all-gather.11.cloned.1.call-start = ((), (), s32[]{:S(2)}) async-start(), calls=%async_computation.4 | async-start | bytes 3342336 | tf_op jit(solution)/shard_map/all_gather | solution.py:123
  44.3 172.9 %all-gather.13.cloned.1.call-start = ((), (), s32[]{:S(2)}) async-start(), calls=%async_computation.5 | async-start | bytes 3342336 | tf_op jit(solution)/shard_map/all_gather | solution.py:126
  46.0 221.3 %all-gather.17.cloned.1.call-start = ((), (), s32[]{:S(2)}) async-start(), calls=%async_computation.7 | async-start | bytes 9437184 | tf_op jit(solution)/shard_map/all_gather | solution.py:117
  46.6 255.2 %all-gather.15.cloned.1.call-start = ((), (), s32[]{:S(2)}) async-start(), calls=%async_computation.6 | async-start | bytes 4718592 | tf_op jit(solution)/shard_map/all_gather | solution.py:173
  47.9 24.3 %copy-start.8 = (f32[2048]{0:T(1024)S(1)}, f32[2048]{0:T(1024)}, u32[]{:S(2)}) copy-start(f32[2048]{0:T(1024)} %param.29) | copy-start | bytes 24580
  69.0 3.4 copy-start.2
  72.4 1.2 copy-start.13
  73.7 2.3 copy-start.3
  73.7 3.9 copy-start.6
  76.0 5.3 copy-start.11
  77.5 5.4 copy-start.12
  82.9 2.2 copy-start.4
  83.8 3.2 copy-start.14
  87.0 3.7 copy-start.5
  87.0 4.4 copy-start.15
  91.4 15.9 %copy-start.16 = (bf16[1,2048,128]{2,1,0:T(8,128)(2,1)S(1)}, bf16[1,2048,128]{2,1,0:T(8,128)(2,1)}, u32[]{:S(2)}) copy-start(bf16[1,2048,128]{2,1,0:T(8,128)(2,1)} %param.28) | copy-start | bytes 1572868
  218.3 99.6 %copy-start.17 = (f32[2048]{0:T(1024)S(1)}, f32[2048]{0:T(1024)}, u32[]{:S(2)}) copy-start(f32[2048]{0:T(1024)} %param.36) | copy-start | bytes 24580
  218.3 181.6 %all-reduce.2.cloned.1.call-start = ((), (), s32[]{:S(2)}) async-start(), calls=%async_computation.9 | async-start | bytes 262144 | tf_op jit(solution)/shard_map/psum | solution.py:188
  315.9 1.9 copy-start.7
  340.6 60.3 %copy-start.9 = (f32[2048]{0:T(1024)S(1)}, f32[2048]{0:T(1024)}, u32[]{:S(2)}) copy-start(f32[2048]{0:T(1024)} %param.40) | copy-start | bytes 24580
  340.6 113.3 %reduce-scatter.2.cloned.1.call-start = ((), (), s32[]{:S(2)}) async-start(), calls=%async_computation.8 | async-start | bytes 9437184 | tf_op jit(solution)/shard_map/reduce_scatter | solution.py:182
  458.7 104.3 %all-to-all-start.1 = ((bf16[128,2,1024]{2,1,0:T(2,128)(2,1)}), bf16[128,2,1024]{2,1,0:T(2,128)(2,1)S(1)}, u32[]{:S(2)}, u32[]{:S(2)}) async-start(bf16[128,2,1024]{2,1,0:T(2,128)(2,1)} %reshape.452), calls=%async_computation.2 | async-start | bytes 1048576 | tf_op jit(solution)/shard_map/all_to_all | solution.py:77
  493.1 72.7 %copy-start.1 = (bf16[2048,384]{1,0:T(8,128)(2,1)S(1)}, bf16[2048,384]{1,0:T(8,128)(2,1)}, u32[]{:S(2)}) copy-start(bf16[2048,384]{1,0:T(8,128)(2,1)} %param.37) | copy-start | bytes 4718596
Sparse Core Ops, SparseCore 0:
  40.8 28.0 all-gather.18
  71.1 48.0 all-gather.8
  121.4 46.8 all-gather.10
  170.3 46.8 all-gather.12
  218.8 48.4 all-gather.16
  269.4 32.2 all-gather.14
  340.8 59.1 all-reduce.1
  402.4 51.4 reduce-scatter.1

commit v2 on v1

--- a/solution.py
+++ b/solution.py
@@ -117,15 +117,27 @@
     o_full = lax.all_gather(o_proj, "kv", axis=0, tiled=True)
     ff_dev = w_gate.shape[1]
     ff_piece = ff_dev // kv_count
-    gate_w = lax.all_gather(
-        lax.dynamic_slice_in_dim(w_gate, kv_index * ff_piece, ff_piece, axis=1), "req", axis=1, tiled=True
-    )
-    up_w = lax.all_gather(
-        lax.dynamic_slice_in_dim(w_up, kv_index * ff_piece, ff_piece, axis=1), "req", axis=1, tiled=True
-    )
-    down_w = lax.all_gather(
-        lax.dynamic_slice_in_dim(w_down, kv_index * ff_piece, ff_piece, axis=0), "req", axis=0, tiled=True
-    )
+    weight_piece = jnp.concatenate(
+        [
+            lax.dynamic_slice_in_dim(w_gate, kv_index * ff_piece, ff_piece, axis=1),
+            lax.dynamic_slice_in_dim(w_up, kv_index * ff_piece, ff_piece, axis=1),
+            lax.dynamic_slice_in_dim(w_down, kv_index * ff_piece, ff_piece, axis=0).T,
+        ],
+        axis=1,
+    )
+    weight_all = lax.all_to_all(
+        jnp.broadcast_to(weight_piece[None], (req_count,) + weight_piece.shape),
+        "req",
+        split_axis=0,
+        concat_axis=0,
+        tiled=True,
+    )
+    model_dim = w_gate.shape[0]
+    gate_w = weight_all[:, :, :ff_piece].transpose(1, 0, 2).reshape(model_dim, req_count * ff_piece)
+    up_w = weight_all[:, :, ff_piece : 2 * ff_piece].transpose(1, 0, 2).reshape(
+        model_dim, req_count * ff_piece
+    )
+    down_w = weight_all[:, :, 2 * ff_piece :].transpose(0, 2, 1).reshape(req_count * ff_piece, model_dim)
     q_cols = q_proj.shape[1]
     kv_cols = k_proj.shape[1]
     projected = jnp.concatenate(
@@ -179,13 +191,23 @@
     up_part = jnp.dot(ffn_in, up_w, preferred_element_type=jnp.float32)
     hidden_act = (jax.nn.silu(gate_part) * up_part).astype(jnp.bfloat16)
     down_part = jnp.dot(hidden_act, down_w, preferred_element_type=jnp.float32)
-    ffn_part = lax.psum_scatter(down_part, "kv", scatter_dimension=0, tiled=True)
+    tail_count = tok_req - fresh_count + 1
+    tail_pad = -(-tail_count // 8) * 8
+    scatter_in = jnp.concatenate(
+        [
+            down_part.reshape(kv_count, rows_dev, model_dim),
+            jnp.broadcast_to(down_part[None, tok_req - tail_pad :], (kv_count, tail_pad, model_dim)),
+        ],
+        axis=1,
+    ).reshape(kv_count * (rows_dev + tail_pad), model_dim)
+    scattered = lax.psum_scatter(scatter_in, "kv", scatter_dimension=0, tiled=True)
+    ffn_part = scattered[:rows_dev]
+    tail_sum = scattered[rows_dev + tail_pad - tail_count :]
     mine = lax.dynamic_slice_in_dim(resid, kv_index * rows_dev, rows_dev, axis=0)
     out_rows = (mine.astype(jnp.float32) + ffn_part).astype(jnp.bfloat16)
     going_back = jnp.zeros_like(out_rows).at[slot_place].set(out_rows)
     returned = regroup(going_back)
     layer_out = jnp.zeros_like(hidden_in).at[send_rows].set(returned)
-    tail_sum = lax.psum(down_part[fresh_count - 1 :], "kv")
     tail_out = (resid[fresh_count - 1 :].astype(jnp.float32) + tail_sum).astype(jnp.bfloat16)
     tail_rows = norm_rows(tail_out, final_gain).astype(jnp.bfloat16)
     local_peaks = jnp.max(
@@ -196,7 +218,7 @@
         ),
         axis=1,
     )
-    max_logit = lax.pmax(local_peaks, ("req", "kv"))
+    max_logit = jnp.max(lax.all_gather(local_peaks, ("req", "kv"), axis=0), axis=0)
     return (layer_out, max_logit)
 
 

time: 578 us -> 537 us (0.929)
  blocking collectives: 90.5 us -> 26.1 us
  other arithmetic: 21.6 us -> 33 us
  local copies, waits for them, and re-layouts: 24.9 us -> 33.7 us
    unnamed x8 -> x6, waiting for transfers between devices: 1.33 us -> 135 us
    all_gather x3 -> x0, waiting for transfers between devices: 97.9 us -> none  [the longest x1 49 us: shards(): lax.all_gather(lax.dynamic_slice_in_dim(w_up, kv_index * ff_piece, ff_pie...]
    all_to_all x0 -> x1, waiting for transfers between devices: none -> 77.8 us  [shards(): lax.all_to_all(jnp.broadcast_to(weight_piece[None], (req_count,) + weight...]
    pmax x1 -> x0, blocking collectives: 64.3 us -> none  [shards(): max_logit = lax.pmax(local_peaks, ('req', 'kv'))]
    psum x1 -> x0, waiting for transfers between devices: 58.5 us -> none  [shards(): tail_sum = lax.psum(down_part[fresh_count - 1:], 'kv')]
    all_gather x1, waiting for transfers between devices: 49 us -> 0.02 us  [shards(): o_full = lax.all_gather(o_proj, 'kv', axis=0, tiled=True)]
    concatenate x0 -> x2, other arithmetic: none -> 8.43 us  [the longest x1 8.39 us: shards(): jnp.concatenate([down_part.reshape(kv_count, rows_dev, model_dim), jnp.br...]
    all_gather x1, waiting for transfers between devices: 15 us -> 6.69 us  [shards(): rows_all = lax.all_gather(owner_rows, 'kv', axis=0, tiled=True)]
  transfers between devices with their start and end apart: 10 -> 8, of which waited for: 8 -> 6; matrix products, arithmetic and copies ran while one was open for 12% -> 15% of each run, Pallas kernels for 0% -> 0%
where the time goes in v2:
time: 537 us; the launch traced here: 529 us
  waiting for transfers between devices  319 us (59%)
  matrix products  76.6 us (14%)
  local copies, waits for them, and re-layouts  33.7 us (6%)
  other arithmetic  33 us (6%)
  blocking collectives  26.1 us (5%)
  starting transfers between devices  25.1 us (5%)
  between operations  15.1 us (3%)
    unnamed x6, waiting for transfers between devices  135 us
    all_to_all x1, waiting for transfers between devices, shards(): lax.all_to_all(jnp.broadcast_to(weight_piece[None], (req_count,) + weight...  77.8 us
    reduce_scatter x1, waiting for transfers between devices, shards(): lax.psum_scatter(scatter_in, 'kv', scatter_dimension=0, tiled=True)  57.5 us
    all_gather x1, waiting for transfers between devices, shards(): lax.all_gather(pieces.reshape(tok_req, q_cols), 'kv', axis=1, tiled=True)  29.6 us
    all_gather x1, blocking collectives, shards(): lax.all_gather(tail_rows, 'req', axis=0, tiled=True)  26.1 us
    all_to_all x2, starting transfers between devices, regroup(): lax.all_to_all(rows_in, ('req', 'kv'), split_axis=0, concat_axis=0, tiled...  19.4 us
    sub x1, matrix products, prefill_full(): expd = jnp.exp(scores - row_peak)  16.1 us
    dot_general x1, matrix products, shards(): jnp.dot(attended, o_full, preferred_element_type=jnp.float32)  14.2 us
  transfers between devices with their start and end apart: 8, of which 6 were waited for; matrix products, arithmetic and copies ran while one was open for 15% of the time, Pallas kernels for 0%

profile of v2, /device:TPU:0, one launch (start us, length us, event | category | flops | bytes accessed | tf_op | source)
XLA Modules:
  0.0 528.5 jit_solution(11033969276229431187)
XLA Ops:
  8.3 2.6 gather_fusion
  13.5 11.1 %all-to-all-start = ((bf16[128,2,1024]{2,1,0:T(2,128)(2,1)}), bf16[128,2,1024]{2,1,0:T(2,128)(2,1)S(1)}, u32[]{:S(2)}, u32[]{:S(2)}) async-start(bf16[128,2,1024]{2,1,0:T(2,128)(2,1)} %reshape.475), calls=%async_computation | async-start | bytes 1048576 | tf_op jit(solution)/shard_map/all_to_all | solution.py:77
  25.4 12.8 %all-to-all-done = bf16[128,2,1024]{2,1,0:T(2,128)(2,1)S(1)} async-done(((bf16[128,2,1024]{2,1,0:T(2,128)(2,1)}), bf16[128,2,1024]{2,1,0:T(2,128)(2,1)S(1)}, u32[]{:S(2)}, u32[]{:S(2)}) %all-to-all-start) | async-done | bytes 524320 | tf_op jit(solution)/shard_map/all_to_all | solution.py:77
  39.0 1.7 gather_fusion.1
  41.5 1.9 constant_dynamic-slice_fusion
  43.9 4.9 broadcast_in_dim.48
  48.8 5.0 all-to-all-start.1
  55.2 2.9 multiply_cosine_fusion
  58.2 4.1 fusion.4
  62.3 6.7 %all-gather.11.cloned.1.call-done = bf16[1024,2048]{1,0:T(8,128)(2,1)} async-done(((bf16[128,2048]{1,0:T(8,128)(2,1)}), bf16[1024,2048]{1,0:T(8,128)(2,1)}) %all-gather.11.cloned.1.call-update) | async-done | bytes 4194320 | tf_op jit(solution)/shard_map/all_gather | solution.py:115
  69.0 3.2 fusion.10
  73.7 1.3 multiply_reduce_fusion
  75.6 1.5 multiply_reduce_fusion.1
  79.3 1.9 subtract_convert_fusion
  83.7 3.6 convolution_convert_fusion
  88.1 16.1 %fusion.82 = (f32[2,1016]{1,0:T(2,128)S(1)}, f32[2,1016,3064]{2,1,0:T(8,128)}) fusion(pred[1016,3064]{1,0:T(8,128)(4,1)} %fusion.4, bf16[1016,128]{1,0:T(8,128)(2,1)S(1)} %copy.52, bf16[2048,128]{1,0:T(8,128)(2,1)S(1)} %bitcast.111, bf16[1024,2,64]{2,0,1:T(8,128)(2,1)S(1)} %get-tuple-element.13, bf16[1024,2,64]{2,0,1:T(8,128)(2,1)S(1)} %get-tuple-element.14), kind=kOutput, calls=%fused_computation.149 | convolution fusion | flops 1621384704 | bytes 29334016 | tf_op jit(solution)/shard_map/sub | solution.py:48
  104.2 12.2 %fusion.18 = bf16[1016,2,128]{2,0,1:T(8,128)(2,1)S(1)} fusion(f32[2,1016,3064]{2,1,0:T(8,128)} %get-tuple-element.28, f32[2,1016]{1,0:T(2,128)S(1)} %get-tuple-element.27, bf16[1016,128]{1,0:T(8,128)(2,1)S(1)} %slice.74, bf16[2048,128]{1,0:T(8,128)(2,1)} %bitcast.112), kind=kOutput, calls=%fused_computation.33 | convolution fusion | flops 1608149248 | bytes 26216896 | tf_op jit(solution)/shard_map/gck,kd->cgd/dot_general | solution.py:50
  116.4 77.8 %all-to-all-done.1 = bf16[16,2048,144]{1,2,0:T(8,128)(2,1)} async-done(((bf16[16,2048,144]{1,2,0:T(8,128)(2,1)}), bf16[16,2048,144]{1,2,0:T(8,128)(2,1)}, u32[]{:S(2)}, u32[]{:S(2)}) %all-to-all-start.1) | async-done | bytes 9437216 | tf_op jit(solution)/shard_map/all_to_all | solution.py:128
  194.1 6.6 %fusion.80 = (bf16[16,2048,48]{1,2,0:T(8,128)(2,1)}, bf16[16,2048,48]{1,2,0:T(8,128)(2,1)}, bf16[16,2048,48]{1,2,0:T(8,128)(2,1)}) fusion(bf16[16,2048,144]{1,2,0:T(8,128)(2,1)} %all-to-all-done.1), kind=kLoop, calls=%fused_computation.147 | loop fusion | bytes 18874368 | tf_op jit(solution)/shard_map/slice | solution.py:140
  201.9 29.6 %all-gather.7.cloned.1.call-done = bf16[1024,2048]{0,1:T(8,128)(2,1)} async-done(((bf16[1024,256]{0,1:T(8,128)(2,1)}), bf16[1024,2048]{0,1:T(8,128)(2,1)}) %all-gather.7.cloned.1.call-update) | async-done | bytes 4194320 | tf_op jit(solution)/shard_map/all_gather | solution.py:185
  231.5 14.2 %fusion.7 = (f32[1024]{0:T(1024)S(1)}, bf16[1024,2048]{1,0:T(8,128)(2,1)S(1)}) fusion(bf16[1024,2048]{0,1:T(8,128)(2,1)} %all-gather.7.cloned.1.call-done, bf16[2048,2048]{1,0:T(8,128)(2,1)} %all-gather.9.cloned.1.call-done, bf16[1024,2048]{1,0:T(8,128)(2,1)} %all-gather.11.cloned.1.call-done), kind=kOutput, calls=%fused_computation.21 | convolution fusion | flops 8602516480 | bytes 20975616 | tf_op jit(solution)/shard_map/dot_general | solution.py:187
  245.7 2.0 copy-done.8
  247.7 7.2 %fusion.20 = f32[1024,768]{1,0:T(8,128)} fusion(bf16[2048,768]{0,1:T(8,128)(2,1)} %bitcast.103, bf16[1024,2048]{1,0:T(8,128)(2,1)S(1)} %get-tuple-element.30, f32[2048]{0:T(1024)S(1)} %copy-done.17, f32[1024]{0:T(1024)S(1)} %add_rsqrt_fusion.1), kind=kOutput, calls=%fused_computation.34 | convolution fusion | flops 3229614080 | bytes 10498048 | tf_op jit(solution)/shard_map/dot_general | solution.py:190
  254.8 14.0 %fusion.23 = f32[1024,2048]{1,0:T(8,128)} fusion(bf16[768,2048]{1,0:T(8,128)(2,1)} %bitcast.101, f32[1024,768]{1,0:T(8,128)} %fusion.20, bf16[2048,768]{0,1:T(8,128)(2,1)} %bitcast.102, bf16[1024,2048]{1,0:T(8,128)(2,1)} %copy-done.8, f32[2048]{0:T(1024)S(1)} %copy-done.17, f32[1024]{0:T(1024)S(1)} %add_rsqrt_fusion.1), kind=kOutput, calls=%fused_computation.35 | convolution fusion | flops 6455558144 | bytes 22032384 | tf_op jit(solution)/shard_map/dot_general | solution.py:193
  269.9 8.4 %pad_maximum_fusion = f32[8,144,2048]{2,1,0:T(8,128)} fusion(f32[8,16,2048]{2,1,0:T(8,128)S(1)} %broadcast_in_dim.49, f32[8,128,2048]{2,1,0:T(8,128)} %bitcast.100), kind=kLoop, calls=%fused_computation.20 | loop fusion | flops 2359296 | bytes 18874368 | tf_op jit(solution)/shard_map/concatenate | solution.py:196
  278.3 57.5 %reduce-scatter.2.cloned.1.call-done = f32[144,2048]{1,0:T(8,128)} async-done(((f32[1152,2048]{1,0:T(8,128)}), f32[144,2048]{1,0:T(8,128)}) %reduce-scatter.2.cloned.1.call-update) | async-done | bytes 1179664 | tf_op jit(solution)/shard_map/reduce_scatter | solution.py:203
  335.8 2.6 scatter_custom_fusion
  340.6 8.2 %all-to-all-start.2 = ((bf16[128,2,1024]{2,1,0:T(2,128)(2,1)}), bf16[128,2,1024]{2,1,0:T(2,128)(2,1)S(1)}, u32[]{:S(2)}, u32[]{:S(2)}) async-start(bf16[128,2,1024]{2,1,0:T(2,128)(2,1)} %reshape.477), calls=%async_computation.3 | async-start | bytes 1048576 | tf_op jit(solution)/shard_map/all_to_all | solution.py:77
  350.9 26.1 %all-gather.2 = bf16[16,9,2048]{2,1,0:T(8,128)(2,1)S(1)} all-gather(bf16[1,9,2048]{2,1,0:T(8,128)(2,1)S(1)} %fusion.54), channel_id=1, replica_groups=mesh['req'=16,'kv'=8] {'req'}, dimensions={0}, use_global_device_ids=true | all-gather | bytes 626688 | tf_op jit(solution)/shard_map/all_gather | solution.py:215
  378.1 4.4 convolution_reduce_fusion
  383.5 133.8 %all-reduce.3.cloned.1.call-done = f32[18432]{0:T(1024)} async-done(((f32[18432]{0:T(1024)}), f32[18432]{0:T(1024)}) %all-reduce.3.cloned.1.call-update) | async-done | bytes 73744
  519.3 2.4 scatter_custom_fusion.1
  (106 shorter events, 25.1 us)
Async XLA Ops:
  7.2 36.6 %copy-start = (bf16[384,2048]{1,0:T(8,128)(2,1)S(1)}, bf16[384,2048]{1,0:T(8,128)(2,1)}, u32[]{:S(2)}) copy-start(bf16[384,2048]{1,0:T(8,128)(2,1)} %param.39) | copy-start | bytes 4718596
  13.5 24.7 %all-to-all-start = ((bf16[128,2,1024]{2,1,0:T(2,128)(2,1)}), bf16[128,2,1024]{2,1,0:T(2,128)(2,1)S(1)}, u32[]{:S(2)}, u32[]{:S(2)}) async-start(bf16[128,2,1024]{2,1,0:T(2,128)(2,1)} %reshape.475), calls=%async_computation | async-start | bytes 1048576 | tf_op jit(solution)/shard_map/all_to_all | solution.py:77
  24.7 44.3 %all-gather.11.cloned.1.call-start = ((), (), s32[]{:S(2)}) async-start(), calls=%async_computation.7 | async-start | bytes 4718592 | tf_op jit(solution)/shard_map/all_gather | solution.py:115
  40.7 161.1 %all-gather.9.cloned.1.call-start = ((), (), s32[]{:S(2)}) async-start(), calls=%async_computation.5 | async-start | bytes 9437184 | tf_op jit(solution)/shard_map/all_gather | solution.py:117
  48.8 6.2 %copy-start.11 = (s32[8]{0:T(128)S(1)}, s32[8]{0:T(128)}, u32[]{:S(2)}) copy-start(s32[8]{0:T(128)} %param.23) | copy-start | bytes 100
  48.8 145.3 %all-to-all-start.1 = ((bf16[16,2048,144]{1,2,0:T(8,128)(2,1)}), bf16[16,2048,144]{1,2,0:T(8,128)(2,1)}, u32[]{:S(2)}, u32[]{:S(2)}) async-start(bf16[16,2048,144]{1,2,0:T(8,128)(2,1)} %broadcast_in_dim.48), calls=%async_computation.1 | async-start | bytes 18874368 | tf_op jit(solution)/shard_map/all_to_all | solution.py:128
  53.8 177.7 %all-gather.7.cloned.1.call-start = ((), (), s32[]{:S(2)}) async-start(), calls=%async_computation.4 | async-start | bytes 4718592 | tf_op jit(solution)/shard_map/all_gather | solution.py:185
  55.2 17.0 %copy-start.9 = (f32[2048]{0:T(1024)S(1)}, f32[2048]{0:T(1024)}, u32[]{:S(2)}) copy-start(f32[2048]{0:T(1024)} %param.29) | copy-start | bytes 24580
  69.0 3.4 copy-start.2
  72.4 1.2 copy-start.14
  73.6 1.9 copy-start.3
  73.7 1.9 copy-start.6
  75.6 1.9 copy-start.12
  75.6 3.4 copy-start.13
  78.9 2.9 copy-start.4
  81.2 2.4 copy-start.15
  83.6 3.7 copy-start.5
  83.6 4.4 copy-start.16
  201.8 45.9 %copy-start.17 = (f32[2048]{0:T(1024)S(1)}, f32[2048]{0:T(1024)}, u32[]{:S(2)}) copy-start(f32[2048]{0:T(1024)} %param.36) | copy-start | bytes 24580
  201.8 134.0 %reduce-scatter.2.cloned.1.call-start = ((), (), s32[]{:S(2)}) async-start(), calls=%async_computation.6 | async-start | bytes 10616832 | tf_op jit(solution)/shard_map/reduce_scatter | solution.py:203
  245.7 2.0 copy-start.8
  278.3 71.6 %copy-start.10 = (f32[2048]{0:T(1024)S(1)}, f32[2048]{0:T(1024)}, u32[]{:S(2)}) copy-start(f32[2048]{0:T(1024)} %param.40) | copy-start | bytes 24580
  340.6 178.3 %all-to-all-start.2 = ((bf16[128,2,1024]{2,1,0:T(2,128)(2,1)}), bf16[128,2,1024]{2,1,0:T(2,128)(2,1)S(1)}, u32[]{:S(2)}, u32[]{:S(2)}) async-start(bf16[128,2,1024]{2,1,0:T(2,128)(2,1)} %reshape.477), calls=%async_computation.3 | async-start | bytes 1048576 | tf_op jit(solution)/shard_map/all_to_all | solution.py:77
  348.8 168.5 %all-reduce.3.cloned.1.call-start = ((), (), s32[]{:S(2)}) async-start(), calls=%async_computation.8 | async-start | bytes 147456
  377.1 144.7 %copy-start.1 = (bf16[384,2048]{1,0:T(8,128)(2,1)S(1)}, bf16[384,2048]{1,0:T(8,128)(2,1)}, u32[]{:S(2)}) copy-start(bf16[384,2048]{1,0:T(8,128)(2,1)} %param.39) | copy-start | bytes 4718596
  382.8 0.6 copy-start.7
Sparse Core Ops, SparseCore 0:
  40.8 28.0 all-gather.10
  70.7 49.6 all-gather.8
  201.9 29.5 all-gather.6
  278.4 57.3 reduce-scatter.1
  383.6 133.6 all-reduce.2

commit v3 on v2

--- a/solution.py
+++ b/solution.py
@@ -114,7 +114,9 @@
     owner_rows = arrived[slot_place]
     rows_all = lax.all_gather(owner_rows, "kv", axis=0, tiled=True)
     normed = norm_rows(rows_all, attn_gain).astype(jnp.bfloat16)
-    o_full = lax.all_gather(o_proj, "kv", axis=0, tiled=True)
+    o_full = lax.all_to_all(
+        jnp.broadcast_to(o_proj[None], (kv_count,) + o_proj.shape), "kv", split_axis=0, concat_axis=0, tiled=True
+    ).reshape(kv_count * o_proj.shape[0], o_proj.shape[1])
     ff_dev = w_gate.shape[1]
     ff_piece = ff_dev // kv_count
     weight_piece = jnp.concatenate(
@@ -125,13 +127,7 @@
         ],
         axis=1,
     )
-    weight_all = lax.all_to_all(
-        jnp.broadcast_to(weight_piece[None], (req_count,) + weight_piece.shape),
-        "req",
-        split_axis=0,
-        concat_axis=0,
-        tiled=True,
-    )
+    weight_all = lax.all_gather(weight_piece, "req", axis=0)
     model_dim = w_gate.shape[0]
     gate_w = weight_all[:, :, :ff_piece].transpose(1, 0, 2).reshape(model_dim, req_count * ff_piece)
     up_w = weight_all[:, :, ff_piece : 2 * ff_piece].transpose(1, 0, 2).reshape(
@@ -181,7 +177,7 @@
         cache_len,
     )
     pieces = jnp.concatenate([pre_out, dec_out], axis=0)
-    pieces, gate_w, up_w, down_w = lax.optimization_barrier((pieces, gate_w, up_w, down_w))
+    pieces, gate_w, up_w, down_w, o_full = lax.optimization_barrier((pieces, gate_w, up_w, down_w, o_full))
     attended = lax.all_gather(pieces.reshape(tok_req, q_cols), "kv", axis=1, tiled=True)
     resid = (
         rows_all.astype(jnp.float32) + jnp.dot(attended, o_full, preferred_element_type=jnp.float32)
@@ -218,7 +214,7 @@
         ),
         axis=1,
     )
-    max_logit = jnp.max(lax.all_gather(local_peaks, ("req", "kv"), axis=0), axis=0)
+    max_logit = lax.pmax(local_peaks, ("req", "kv"))
     return (layer_out, max_logit)
 
 

time: 537 us -> 461 us (0.86)
  waiting for transfers between devices: 319 us -> 160 us
  blocking collectives: 26.1 us -> 89 us
  local copies, waits for them, and re-layouts: 33.7 us -> 55 us
    unnamed x6 -> x4, waiting for transfers between devices: 135 us -> 0.07 us
    all_to_all x1, waiting for transfers between devices: 77.8 us -> 0.01 us  [shards(): lax.all_to_all(jnp.broadcast_to(o_proj[None], (kv_count,) + o_proj.shape)...]
    pmax x0 -> x1, blocking collectives: none -> 62.8 us  [shards(): max_logit = lax.pmax(local_peaks, ('req', 'kv'))]
    all_gather x1, waiting for transfers between devices: 0.02 us -> 34.8 us  [shards(): weight_all = lax.all_gather(weight_piece, 'req', axis=0)]
    all_gather x1, waiting for transfers between devices: 6.69 us -> 22.8 us  [shards(): rows_all = lax.all_gather(owner_rows, 'kv', axis=0, tiled=True)]
    transpose x0 -> x4, local copies, waits for them, and re-layouts: none -> 14.7 us  [the longest x2 7.89 us: shards(): weight_all[:, :, 2 * ff_piece:].transpose(0, 2, 1)]
    unnamed x46 -> x43, local copies, waits for them, and re-layouts: 9.28 us -> 22.9 us
    slice x1 -> x0, local copies, waits for them, and re-layouts: 6.6 us -> none  [shards(): weight_all[:, :, 2 * ff_piece:].transpose(0, 2, 1)]
  transfers between devices with their start and end apart: 8 -> 7, of which waited for: 6 -> 5; matrix products, arithmetic and copies ran while one was open for 15% -> 22% of each run, Pallas kernels for 0% -> 0%
where the time goes in v3:
time: 461 us; the launch traced here: 456 us
  waiting for transfers between devices  160 us (35%)
  blocking collectives  89 us (19%)
  matrix products  79.2 us (17%)
  local copies, waits for them, and re-layouts  55 us (12%)
  other arithmetic  32.9 us (7%)
  starting transfers between devices  24.8 us (5%)
  between operations  15.1 us (3%)
    pmax x1, blocking collectives, shards(): max_logit = lax.pmax(local_peaks, ('req', 'kv'))  62.8 us
    reduce_scatter x1, waiting for transfers between devices, shards(): lax.psum_scatter(scatter_in, 'kv', scatter_dimension=0, tiled=True)  57.5 us
    all_gather x1, waiting for transfers between devices, shards(): weight_all = lax.all_gather(weight_piece, 'req', axis=0)  34.8 us
    all_gather x1, waiting for transfers between devices, shards(): lax.all_gather(pieces.reshape(tok_req, q_cols), 'kv', axis=1, tiled=True)  31.7 us
    all_gather x1, blocking collectives, shards(): lax.all_gather(tail_rows, 'req', axis=0, tiled=True)  26.2 us
    unnamed x43, local copies, waits for them, and re-layouts  22.9 us
    all_gather x1, waiting for transfers between devices, shards(): rows_all = lax.all_gather(owner_rows, 'kv', axis=0, tiled=True)  22.8 us
    all_to_all x2, starting transfers between devices, regroup(): lax.all_to_all(rows_in, ('req', 'kv'), split_axis=0, concat_axis=0, tiled...  19.4 us
  transfers between devices with their start and end apart: 7, of which 5 were waited for; matrix products, arithmetic and copies ran while one was open for 22% of the time, Pallas kernels for 0%

profile of v3, /device:TPU:0, one launch (start us, length us, event | category | flops | bytes accessed | tf_op | source)
XLA Modules:
  0.0 455.7 jit_solution(14485776248099919321)
XLA Ops:
  8.3 2.6 gather_fusion
  13.5 11.1 %all-to-all-start = ((bf16[128,2,1024]{2,1,0:T(2,128)(2,1)}), bf16[128,2,1024]{2,1,0:T(2,128)(2,1)S(1)}, u32[]{:S(2)}, u32[]{:S(2)}) async-start(bf16[128,2,1024]{2,1,0:T(2,128)(2,1)} %reshape.477), calls=%async_computation | async-start | bytes 1048576 | tf_op jit(solution)/shard_map/all_to_all | solution.py:77
  25.4 12.8 %all-to-all-done = bf16[128,2,1024]{2,1,0:T(2,128)(2,1)S(1)} async-done(((bf16[128,2,1024]{2,1,0:T(2,128)(2,1)}), bf16[128,2,1024]{2,1,0:T(2,128)(2,1)S(1)}, u32[]{:S(2)}, u32[]{:S(2)}) %all-to-all-start) | async-done | bytes 524320 | tf_op jit(solution)/shard_map/all_to_all | solution.py:77
  44.1 5.6 %broadcast_in_dim.48 = bf16[8,256,2048]{2,1,0:T(8,128)(2,1)} broadcast(bf16[256,2048]{1,0:T(8,128)(2,1)} %param.35), dimensions={1,2} | broadcast | bytes 9437184 | tf_op jit(solution)/shard_map/broadcast_in_dim | solution.py:118
  49.6 5.1 %all-to-all-start.1 = ((bf16[8,256,2048]{2,1,0:T(8,128)(2,1)}), bf16[8,256,2048]{2,1,0:T(8,128)(2,1)}, u32[]{:S(2)}, u32[]{:S(2)}) async-start(bf16[8,256,2048]{2,1,0:T(8,128)(2,1)} %broadcast_in_dim.48), calls=%async_computation.1 | async-start | bytes 16777216 | tf_op jit(solution)/shard_map/all_to_all | solution.py:117
  55.7 2.9 multiply_cosine_fusion
  58.8 4.0 fusion.4
  62.8 22.8 %all-gather.9.cloned.1.call-done = bf16[1024,2048]{1,0:T(8,128)(2,1)} async-done(((bf16[128,2048]{1,0:T(8,128)(2,1)}), bf16[1024,2048]{1,0:T(8,128)(2,1)}) %all-gather.9.cloned.1.call-update) | async-done | bytes 4194320 | tf_op jit(solution)/shard_map/all_gather | solution.py:115
  85.6 3.2 fusion.10
  92.5 3.7 multiply_reduce_fusion.1
  102.1 3.8 convolution_convert_fusion
  106.7 16.2 %fusion.81 = (f32[2,1016]{1,0:T(2,128)S(1)}, f32[2,1016,3064]{2,1,0:T(8,128)}) fusion(pred[1016,3064]{1,0:T(8,128)(4,1)} %fusion.4, bf16[1016,128]{1,0:T(8,128)(2,1)S(1)} %copy.66, bf16[2048,128]{1,0:T(8,128)(2,1)S(1)} %bitcast.118, bf16[1024,2,64]{2,0,1:T(8,128)(2,1)S(1)} %get-tuple-element.15, bf16[1024,2,64]{2,0,1:T(8,128)(2,1)S(1)} %get-tuple-element.16), kind=kOutput, calls=%fused_computation.151 | convolution fusion | flops 1621384704 | bytes 29334016 | tf_op jit(solution)/shard_map/sub | solution.py:48
  122.9 12.5 %fusion.18 = bf16[1016,2,128]{2,0,1:T(8,128)(2,1)S(1)} fusion(f32[2,1016,3064]{2,1,0:T(8,128)} %get-tuple-element.30, f32[2,1016]{1,0:T(2,128)S(1)} %get-tuple-element.29, bf16[1016,128]{1,0:T(8,128)(2,1)S(1)} %slice.74, bf16[2048,128]{1,0:T(8,128)(2,1)} %bitcast.119), kind=kOutput, calls=%fused_computation.36 | convolution fusion | flops 1608149248 | bytes 26216896 | tf_op jit(solution)/shard_map/gck,kd->cgd/dot_general | solution.py:50
  135.5 34.8 %all-gather.11.cloned.1.call-done = bf16[32768,144]{0,1:T(8,128)(2,1)} async-done(((bf16[2048,144]{0,1:T(8,128)(2,1)}), bf16[32768,144]{0,1:T(8,128)(2,1)}) %all-gather.11.cloned.1.call-update) | async-done | bytes 9437200 | tf_op jit(solution)/shard_map/all_gather | solution.py:130
  170.3 14.6 %copy.84 = bf16[18,8,16,2048]{3,2,1,0:T(8,128)(2,1)} copy(bf16[18,8,16,2048]{3,1,2,0:T(8,128)(2,1)} %bitcast.106) | data formatting | bytes 18874368
  184.9 4.5 slice_bitcast_fusion
  189.4 3.4 copy.73
  192.8 3.4 copy.74
  196.3 3.4 copy.75
  200.7 31.7 %all-gather.7.cloned.1.call-done = bf16[1024,2048]{0,1:T(8,128)(2,1)} async-done(((bf16[1024,256]{0,1:T(8,128)(2,1)}), bf16[1024,2048]{0,1:T(8,128)(2,1)}) %all-gather.7.cloned.1.call-update) | async-done | bytes 4194320 | tf_op jit(solution)/shard_map/all_gather | solution.py:181
  232.5 14.0 %fusion.7 = (f32[1024]{0:T(1024)S(1)}, bf16[1024,2048]{1,0:T(8,128)(2,1)S(1)}) fusion(bf16[1024,2048]{0,1:T(8,128)(2,1)} %all-gather.7.cloned.1.call-done, bf16[2048,2048]{1,0:T(8,128)(2,1)} %bitcast.27, bf16[1024,2048]{1,0:T(8,128)(2,1)} %all-gather.9.cloned.1.call-done), kind=kOutput, calls=%fused_computation.21 | convolution fusion | flops 8602516480 | bytes 20975616 | tf_op jit(solution)/shard_map/dot_general | solution.py:183
  246.5 2.0 copy-done.7
  248.5 7.1 %fusion.20 = f32[1024,768]{1,0:T(8,128)} fusion(bf16[2048,768]{0,1:T(8,128)(2,1)} %bitcast.108, bf16[1024,2048]{1,0:T(8,128)(2,1)S(1)} %get-tuple-element.32, f32[2048]{0:T(1024)S(1)} %copy-done.16, f32[1024]{0:T(1024)S(1)} %add_rsqrt_fusion.1), kind=kOutput, calls=%fused_computation.37 | convolution fusion | flops 3229614080 | bytes 10498048 | tf_op jit(solution)/shard_map/dot_general | solution.py:186
  255.6 14.0 %fusion.23 = f32[1024,2048]{1,0:T(8,128)} fusion(bf16[768,2048]{1,0:T(8,128)(2,1)} %bitcast.110, f32[1024,768]{1,0:T(8,128)} %fusion.20, bf16[2048,768]{0,1:T(8,128)(2,1)} %bitcast.109, bf16[1024,2048]{1,0:T(8,128)(2,1)} %copy-done.7, f32[2048]{0:T(1024)S(1)} %copy-done.16, f32[1024]{0:T(1024)S(1)} %add_rsqrt_fusion.1), kind=kOutput, calls=%fused_computation.38 | convolution fusion | flops 6455558144 | bytes 22032384 | tf_op jit(solution)/shard_map/dot_general | solution.py:189
  270.7 8.4 %pad_maximum_fusion = f32[8,144,2048]{2,1,0:T(8,128)} fusion(f32[8,16,2048]{2,1,0:T(8,128)S(1)} %broadcast_in_dim.49, f32[8,128,2048]{2,1,0:T(8,128)} %bitcast.107), kind=kLoop, calls=%fused_computation.20 | loop fusion | flops 2359296 | bytes 18874368 | tf_op jit(solution)/shard_map/concatenate | solution.py:192
  279.1 57.5 %reduce-scatter.2.cloned.1.call-done = f32[144,2048]{1,0:T(8,128)} async-done(((f32[1152,2048]{1,0:T(8,128)}), f32[144,2048]{1,0:T(8,128)}) %reduce-scatter.2.cloned.1.call-update) | async-done | bytes 1179664 | tf_op jit(solution)/shard_map/reduce_scatter | solution.py:199
  336.6 2.5 scatter_custom_fusion
  341.3 8.3 %all-to-all-start.2 = ((bf16[128,2,1024]{2,1,0:T(2,128)(2,1)}), bf16[128,2,1024]{2,1,0:T(2,128)(2,1)S(1)}, u32[]{:S(2)}, u32[]{:S(2)}) async-start(bf16[128,2,1024]{2,1,0:T(2,128)(2,1)} %reshape.479), calls=%async_computation.3 | async-start | bytes 1048576 | tf_op jit(solution)/shard_map/all_to_all | solution.py:77
  351.6 26.2 %all-gather.2 = bf16[16,9,2048]{2,1,0:T(8,128)(2,1)S(1)} all-gather(bf16[1,9,2048]{2,1,0:T(8,128)(2,1)S(1)} %fusion.54), channel_id=1, replica_groups=mesh['req'=16,'kv'=8] {'req'}, dimensions={0}, use_global_device_ids=true | all-gather | bytes 626688 | tf_op jit(solution)/shard_map/all_gather | solution.py:211
  378.9 4.4 convolution_reduce_fusion
  383.3 62.8 %pmax.7 = f32[144]{0:T(256)} all-reduce(f32[144]{0:T(256)S(1)} %convolution_reduce_fusion), channel_id=1, replica_groups=mesh['req'=16,'kv'=8] {'req','kv'}, use_global_device_ids=true, to_apply=%region_14.15 | all-reduce | flops 144 | bytes 1152 | tf_op jit(solution)/shard_map/pmax | solution.py:217
  446.5 2.4 scatter_custom_fusion.1
  (102 shorter events, 28.9 us)
Async XLA Ops:
  7.2 35.9 %copy-start = (bf16[384,2048]{1,0:T(8,128)(2,1)S(1)}, bf16[384,2048]{1,0:T(8,128)(2,1)}, u32[]{:S(2)}) copy-start(bf16[384,2048]{1,0:T(8,128)(2,1)} %param.39) | copy-start | bytes 4718596
  13.5 24.7 %all-to-all-start = ((bf16[128,2,1024]{2,1,0:T(2,128)(2,1)}), bf16[128,2,1024]{2,1,0:T(2,128)(2,1)S(1)}, u32[]{:S(2)}, u32[]{:S(2)}) async-start(bf16[128,2,1024]{2,1,0:T(2,128)(2,1)} %reshape.477), calls=%async_computation | async-start | bytes 1048576 | tf_op jit(solution)/shard_map/all_to_all | solution.py:77
  24.7 60.9 %all-gather.9.cloned.1.call-start = ((), (), s32[]{:S(2)}) async-start(), calls=%async_computation.6 | async-start | bytes 4718592 | tf_op jit(solution)/shard_map/all_gather | solution.py:115
  40.7 129.6 %all-gather.11.cloned.1.call-start = ((), (), s32[]{:S(2)}) async-start(), calls=%async_computation.7 | async-start | bytes 10027008 | tf_op jit(solution)/shard_map/all_gather | solution.py:130
  49.6 6.0 %copy-start.10 = (s32[8]{0:T(128)S(1)}, s32[8]{0:T(128)}, u32[]{:S(2)}) copy-start(s32[8]{0:T(128)} %param.23) | copy-start | bytes 100
  49.6 150.0 %all-to-all-start.1 = ((bf16[8,256,2048]{2,1,0:T(8,128)(2,1)}), bf16[8,256,2048]{2,1,0:T(8,128)(2,1)}, u32[]{:S(2)}, u32[]{:S(2)}) async-start(bf16[8,256,2048]{2,1,0:T(8,128)(2,1)} %broadcast_in_dim.48), calls=%async_computation.1 | async-start | bytes 16777216 | tf_op jit(solution)/shard_map/all_to_all | solution.py:117
  54.7 177.8 %all-gather.7.cloned.1.call-start = ((), (), s32[]{:S(2)}) async-start(), calls=%async_computation.4 | async-start | bytes 4718592 | tf_op jit(solution)/shard_map/all_gather | solution.py:181
  55.7 33.1 %copy-start.8 = (f32[2048]{0:T(1024)S(1)}, f32[2048]{0:T(1024)}, u32[]{:S(2)}) copy-start(f32[2048]{0:T(1024)} %param.29) | copy-start | bytes 24580
  85.6 3.4 copy-start.2
  89.0 1.2 copy-start.13
  90.2 1.9 copy-start.3
  90.2 2.3 copy-start.6
  92.2 4.1 copy-start.11
  92.5 5.2 %copy-start.12 = (f32[128]{0:T(128)S(1)}, f32[128]{0:T(128)}, u32[]{:S(2)}) copy-start(f32[128]{0:T(128)} %param.33) | copy-start | bytes 1540
  97.7 2.4 copy-start.4
  99.7 2.3 copy-start.14
  102.1 3.9 copy-start.5
  102.1 4.7 %copy-start.15 = (bf16[1,2048,128]{2,1,0:T(8,128)(2,1)S(1)}, bf16[1,2048,128]{2,1,0:T(8,128)(2,1)}, u32[]{:S(2)}) copy-start(bf16[1,2048,128]{2,1,0:T(8,128)(2,1)} %param.27) | copy-start | bytes 1572868
  200.7 47.8 %copy-start.16 = (f32[2048]{0:T(1024)S(1)}, f32[2048]{0:T(1024)}, u32[]{:S(2)}) copy-start(f32[2048]{0:T(1024)} %param.36) | copy-start | bytes 24580
  200.7 135.9 %reduce-scatter.2.cloned.1.call-start = ((), (), s32[]{:S(2)}) async-start(), calls=%async_computation.5 | async-start | bytes 10616832 | tf_op jit(solution)/shard_map/reduce_scatter | solution.py:199
  246.5 2.0 copy-start.7
  279.1 71.6 %copy-start.9 = (f32[2048]{0:T(1024)S(1)}, f32[2048]{0:T(1024)}, u32[]{:S(2)}) copy-start(f32[2048]{0:T(1024)} %param.40) | copy-start | bytes 24580
  341.3 104.8 %all-to-all-start.2 = ((bf16[128,2,1024]{2,1,0:T(2,128)(2,1)}), bf16[128,2,1024]{2,1,0:T(2,128)(2,1)S(1)}, u32[]{:S(2)}, u32[]{:S(2)}) async-start(bf16[128,2,1024]{2,1,0:T(2,128)(2,1)} %reshape.479), calls=%async_computation.3 | async-start | bytes 1048576 | tf_op jit(solution)/shard_map/all_to_all | solution.py:77
  377.8 71.1 %copy-start.1 = (bf16[384,2048]{1,0:T(8,128)(2,1)S(1)}, bf16[384,2048]{1,0:T(8,128)(2,1)}, u32[]{:S(2)}) copy-start(bf16[384,2048]{1,0:T(8,128)(2,1)} %param.39) | copy-start | bytes 4718596
Sparse Core Ops, SparseCore 0:
  40.8 44.6 all-gather.8
  87.7 82.5 all-gather.10
  200.8 31.6 all-gather.6
  279.2 57.3 reduce-scatter.1

commit v4 on v3

--- a/solution.py
+++ b/solution.py
@@ -119,21 +119,18 @@
     ).reshape(kv_count * o_proj.shape[0], o_proj.shape[1])
     ff_dev = w_gate.shape[1]
     ff_piece = ff_dev // kv_count
-    weight_piece = jnp.concatenate(
+    weight_piece = jnp.stack(
         [
-            lax.dynamic_slice_in_dim(w_gate, kv_index * ff_piece, ff_piece, axis=1),
-            lax.dynamic_slice_in_dim(w_up, kv_index * ff_piece, ff_piece, axis=1),
-            lax.dynamic_slice_in_dim(w_down, kv_index * ff_piece, ff_piece, axis=0).T,
-        ],
-        axis=1,
-    )
-    weight_all = lax.all_gather(weight_piece, "req", axis=0)
+            lax.dynamic_slice_in_dim(w_gate, kv_index * ff_piece, ff_piece, axis=1).T,
+            lax.dynamic_slice_in_dim(w_up, kv_index * ff_piece, ff_piece, axis=1).T,
+            lax.dynamic_slice_in_dim(w_down, kv_index * ff_piece, ff_piece, axis=0),
+        ]
+    )
+    weight_all = lax.all_gather(weight_piece, "req", axis=1, tiled=True)
     model_dim = w_gate.shape[0]
-    gate_w = weight_all[:, :, :ff_piece].transpose(1, 0, 2).reshape(model_dim, req_count * ff_piece)
-    up_w = weight_all[:, :, ff_piece : 2 * ff_piece].transpose(1, 0, 2).reshape(
-        model_dim, req_count * ff_piece
-    )
-    down_w = weight_all[:, :, 2 * ff_piece :].transpose(0, 2, 1).reshape(req_count * ff_piece, model_dim)
+    gate_w = weight_all[0]
+    up_w = weight_all[1]
+    down_w = weight_all[2]
     q_cols = q_proj.shape[1]
     kv_cols = k_proj.shape[1]
     projected = jnp.concatenate(
@@ -183,19 +180,21 @@
         rows_all.astype(jnp.float32) + jnp.dot(attended, o_full, preferred_element_type=jnp.float32)
     ).astype(jnp.bfloat16)
     ffn_in = norm_rows(resid, ffn_gain).astype(jnp.bfloat16)
-    gate_part = jnp.dot(ffn_in, gate_w, preferred_element_type=jnp.float32)
-    up_part = jnp.dot(ffn_in, up_w, preferred_element_type=jnp.float32)
+    contract_last = (((1,), (1,)), ((), ()))
+    gate_part = lax.dot_general(ffn_in, gate_w, contract_last, preferred_element_type=jnp.float32)
+    up_part = lax.dot_general(ffn_in, up_w, contract_last, preferred_element_type=jnp.float32)
     hidden_act = (jax.nn.silu(gate_part) * up_part).astype(jnp.bfloat16)
-    down_part = jnp.dot(hidden_act, down_w, preferred_element_type=jnp.float32)
     tail_count = tok_req - fresh_count + 1
     tail_pad = -(-tail_count // 8) * 8
-    scatter_in = jnp.concatenate(
+    hidden_width = hidden_act.shape[1]
+    scatter_rows = jnp.concatenate(
         [
-            down_part.reshape(kv_count, rows_dev, model_dim),
-            jnp.broadcast_to(down_part[None, tok_req - tail_pad :], (kv_count, tail_pad, model_dim)),
+            hidden_act.reshape(kv_count, rows_dev, hidden_width),
+            jnp.broadcast_to(hidden_act[None, tok_req - tail_pad :], (kv_count, tail_pad, hidden_width)),
         ],
         axis=1,
-    ).reshape(kv_count * (rows_dev + tail_pad), model_dim)
+    ).reshape(kv_count * (rows_dev + tail_pad), hidden_width)
+    scatter_in = jnp.dot(scatter_rows, down_w, preferred_element_type=jnp.float32)
     scattered = lax.psum_scatter(scatter_in, "kv", scatter_dimension=0, tiled=True)
     ffn_part = scattered[:rows_dev]
     tail_sum = scattered[rows_dev + tail_pad - tail_count :]
@@ -214,7 +213,7 @@
         ),
         axis=1,
     )
-    max_logit = lax.pmax(local_peaks, ("req", "kv"))
+    max_logit = lax.pmax(lax.pmax(local_peaks, "kv"), "req")
     return (layer_out, max_logit)
 
 

time: 461 us -> 411 us (0.89)
  local copies, waits for them, and re-layouts: 55 us -> 29.5 us
  blocking collectives: 89 us -> 77.3 us
  other arithmetic: 32.9 us -> 24.5 us
    unnamed x43 -> x46, local copies, waits for them, and re-layouts: 22.9 us -> 6.29 us
    transpose x5 -> x0, local copies, waits for them, and re-layouts: 14.8 us -> none  [the longest x2 7.89 us: shards(): weight_all[:, :, 2 * ff_piece:].transpose(0, 2, 1)]
    pmax x1 -> x2, blocking collectives: 62.8 us -> 51.1 us  [shards(): max_logit = lax.pmax(lax.pmax(local_peaks, 'kv'), 'req')]
    concatenate x2 -> x1, other arithmetic: 9.29 us -> 0.12 us  [shards(): jnp.concatenate([hidden_act.reshape(kv_count, rows_dev, hidden_width), jn...]
    squeeze x0 -> x1, local copies, waits for them, and re-layouts: none -> 6.73 us  [shards(): down_w = weight_all[2]]
    dot_general x2 -> x3, matrix products: 21.2 us -> 17.3 us  [the longest x1 7 us: shards(): lax.dot_general(ffn_in, gate_w, contract_last, preferred_element_type=jnp...]
  transfers between devices with their start and end apart: 7 -> 7, of which waited for: 5 -> 5; matrix products, arithmetic and copies ran while one was open for 22% -> 19% of each run, Pallas kernels for 0% -> 0%
where the time goes in v4:
time: 411 us; the launch traced here: 406 us
  waiting for transfers between devices  159 us (39%)
  blocking collectives  77.3 us (19%)
  matrix products  75.3 us (18%)
  local copies, waits for them, and re-layouts  29.5 us (7%)
  starting transfers between devices  25.2 us (6%)
  other arithmetic  24.5 us (6%)
  between operations  15.2 us (4%)
    reduce_scatter x1, waiting for transfers between devices, shards(): lax.psum_scatter(scatter_in, 'kv', scatter_dimension=0, tiled=True)  57.5 us
    pmax x2, blocking collectives, shards(): max_logit = lax.pmax(lax.pmax(local_peaks, 'kv'), 'req')  51.1 us
    all_gather x1, waiting for transfers between devices, shards(): weight_all = lax.all_gather(weight_piece, 'req', axis=1, tiled=True)  34.8 us
    all_gather x1, waiting for transfers between devices, shards(): lax.all_gather(pieces.reshape(tok_req, q_cols), 'kv', axis=1, tiled=True)  31.7 us
    all_gather x1, blocking collectives, shards(): lax.all_gather(tail_rows, 'req', axis=0, tiled=True)  26.2 us
    all_gather x1, waiting for transfers between devices, shards(): rows_all = lax.all_gather(owner_rows, 'kv', axis=0, tiled=True)  22.4 us
    all_to_all x2, starting transfers between devices, regroup(): lax.all_to_all(rows_in, ('req', 'kv'), split_axis=0, concat_axis=0, tiled...  19.4 us
    sub x1, matrix products, prefill_full(): expd = jnp.exp(scores - row_peak)  16 us
  transfers between devices with their start and end apart: 7, of which 5 were waited for; matrix products, arithmetic and copies ran while one was open for 19% of the time, Pallas kernels for 0%

profile of v4, /device:TPU:0, one launch (start us, length us, event | category | flops | bytes accessed | tf_op | source)
XLA Modules:
  0.0 406.2 jit_solution(8154085144703892123)
XLA Ops:
  8.3 2.6 gather_fusion
  13.5 11.1 %all-to-all-start = ((bf16[128,2,1024]{2,1,0:T(2,128)(2,1)}), bf16[128,2,1024]{2,1,0:T(2,128)(2,1)S(1)}, u32[]{:S(2)}, u32[]{:S(2)}) async-start(bf16[128,2,1024]{2,1,0:T(2,128)(2,1)} %reshape.464), calls=%async_computation | async-start | bytes 1048576 | tf_op jit(solution)/shard_map/all_to_all | solution.py:77
  25.4 12.8 %all-to-all-done = bf16[128,2,1024]{2,1,0:T(2,128)(2,1)S(1)} async-done(((bf16[128,2,1024]{2,1,0:T(2,128)(2,1)}), bf16[128,2,1024]{2,1,0:T(2,128)(2,1)S(1)}, u32[]{:S(2)}, u32[]{:S(2)}) %all-to-all-start) | async-done | bytes 524320 | tf_op jit(solution)/shard_map/all_to_all | solution.py:77
  39.0 1.7 gather_fusion.1
  40.8 1.9 constant_dynamic-slice_fusion
  44.1 5.6 %broadcast_in_dim.48 = bf16[8,256,2048]{2,1,0:T(8,128)(2,1)} broadcast(bf16[256,2048]{1,0:T(8,128)(2,1)} %param.35), dimensions={1,2} | broadcast | bytes 9437184 | tf_op jit(solution)/shard_map/broadcast_in_dim | solution.py:118
  49.6 5.1 %all-to-all-start.1 = ((bf16[8,256,2048]{2,1,0:T(8,128)(2,1)}), bf16[8,256,2048]{2,1,0:T(8,128)(2,1)}, u32[]{:S(2)}, u32[]{:S(2)}) async-start(bf16[8,256,2048]{2,1,0:T(8,128)(2,1)} %broadcast_in_dim.48), calls=%async_computation.1 | async-start | bytes 16777216 | tf_op jit(solution)/shard_map/all_to_all | solution.py:117
  56.1 2.9 multiply_cosine_fusion
  59.1 4.0 fusion.4
  63.1 22.4 %all-gather.10.cloned.1.call-done = bf16[1024,2048]{1,0:T(8,128)(2,1)} async-done(((bf16[128,2048]{1,0:T(8,128)(2,1)}), bf16[1024,2048]{1,0:T(8,128)(2,1)}) %all-gather.10.cloned.1.call-update) | async-done | bytes 4194320 | tf_op jit(solution)/shard_map/all_gather | solution.py:115
  85.5 3.2 fusion.10
  90.2 1.3 multiply_reduce_fusion
  92.5 3.7 multiply_reduce_fusion.1
  98.0 1.7 subtract_convert_fusion
  102.0 3.8 convolution_convert_fusion
  106.7 16.0 %fusion.77 = (f32[2,1016]{1,0:T(2,128)S(1)}, f32[2,1016,3064]{2,1,0:T(8,128)}) fusion(pred[1016,3064]{1,0:T(8,128)(4,1)} %fusion.4, bf16[1016,128]{1,0:T(8,128)(2,1)S(1)} %copy.49, bf16[2048,128]{1,0:T(8,128)(2,1)S(1)} %bitcast.115, bf16[1024,2,64]{2,0,1:T(8,128)(2,1)S(1)} %get-tuple-element.15, bf16[1024,2,64]{2,0,1:T(8,128)(2,1)S(1)} %get-tuple-element.16), kind=kOutput, calls=%fused_computation.149 | convolution fusion | flops 1621384704 | bytes 29334016 | tf_op jit(solution)/shard_map/sub | solution.py:48
  122.7 12.5 %fusion.18 = bf16[1016,2,128]{2,0,1:T(8,128)(2,1)S(1)} fusion(f32[2,1016,3064]{2,1,0:T(8,128)} %get-tuple-element.30, f32[2,1016]{1,0:T(2,128)S(1)} %get-tuple-element.29, bf16[1016,128]{1,0:T(8,128)(2,1)S(1)} %slice.74, bf16[2048,128]{1,0:T(8,128)(2,1)} %bitcast.116), kind=kOutput, calls=%fused_computation.36 | convolution fusion | flops 1608149248 | bytes 26216896 | tf_op jit(solution)/shard_map/gck,kd->cgd/dot_general | solution.py:50
  135.2 34.8 %all-gather.6.cloned.1.call-done = bf16[3,768,2048]{2,1,0:T(8,128)(2,1)} async-done(((bf16[3,48,2048]{2,1,0:T(8,128)(2,1)}), bf16[3,768,2048]{2,1,0:T(8,128)(2,1)}) %all-gather.6.cloned.1.call-update) | async-done | bytes 9437200 | tf_op jit(solution)/shard_map/all_gather | solution.py:129
  170.1 6.7 %slice_bitcast_fusion = (bf16[768,2048]{1,0:T(8,128)(2,1)}, bf16[768,2048]{1,0:T(8,128)(2,1)}, bf16[768,2048]{1,0:T(8,128)(2,1)}) fusion(bf16[3,768,2048]{2,1,0:T(8,128)(2,1)} %all-gather.6.cloned.1.call-done), kind=kLoop, calls=%fused_computation.27 | loop fusion | bytes 18874368 | tf_op jit(solution)/shard_map/squeeze | solution.py:133
  177.9 31.7 %all-gather.8.cloned.1.call-done = bf16[1024,2048]{0,1:T(8,128)(2,1)} async-done(((bf16[1024,256]{0,1:T(8,128)(2,1)}), bf16[1024,2048]{0,1:T(8,128)(2,1)}) %all-gather.8.cloned.1.call-update) | async-done | bytes 4194320 | tf_op jit(solution)/shard_map/all_gather | solution.py:178
  209.7 14.2 %fusion.7 = (f32[1024]{0:T(1024)S(1)}, bf16[1024,2048]{1,0:T(8,128)(2,1)S(1)}) fusion(bf16[1024,2048]{0,1:T(8,128)(2,1)} %all-gather.8.cloned.1.call-done, bf16[2048,2048]{1,0:T(8,128)(2,1)} %bitcast.28, bf16[1024,2048]{1,0:T(8,128)(2,1)} %all-gather.10.cloned.1.call-done), kind=kOutput, calls=%fused_computation.20 | convolution fusion | flops 8602516480 | bytes 20975616 | tf_op jit(solution)/shard_map/dot_general | solution.py:180
  223.9 7.0 %fusion.20 = f32[1024,768]{1,0:T(8,128)S(1)} fusion(bf16[768,2048]{1,0:T(8,128)(2,1)} %get-tuple-element.9, bf16[1024,2048]{1,0:T(8,128)(2,1)S(1)} %get-tuple-element.32, f32[2048]{0:T(1024)S(1)} %copy-done.18, f32[1024]{0:T(1024)S(1)} %add_rsqrt_fusion.1), kind=kOutput, calls=%fused_computation.37 | convolution fusion | flops 3229614080 | bytes 10498048 | tf_op jit(solution)/shard_map/dot_general | solution.py:184
  230.9 3.9 multiply_convert_fusion
  235.0 6.5 %fusion.82 = f32[1152,2048]{1,0:T(8,128)} fusion(bf16[1152,768]{1,0:T(8,128)(2,1)S(1)} %bitcast.107, bf16[768,2048]{1,0:T(8,128)(2,1)S(1)} %copy-done.6), kind=kOutput, calls=%fused_computation.150 | convolution fusion | flops 3623878656 | bytes 14352384 | tf_op jit(solution)/shard_map/dot_general | solution.py:197
  241.5 57.5 %reduce-scatter.2.cloned.1.call-done = f32[144,2048]{1,0:T(8,128)} async-done(((f32[1152,2048]{1,0:T(8,128)}), f32[144,2048]{1,0:T(8,128)}) %reduce-scatter.2.cloned.1.call-update) | async-done | bytes 1179664 | tf_op jit(solution)/shard_map/reduce_scatter | solution.py:198
  299.0 2.3 scatter_custom_fusion
  303.5 8.3 %all-to-all-start.2 = ((bf16[128,2,1024]{2,1,0:T(2,128)(2,1)}), bf16[128,2,1024]{2,1,0:T(2,128)(2,1)S(1)}, u32[]{:S(2)}, u32[]{:S(2)}) async-start(bf16[128,2,1024]{2,1,0:T(2,128)(2,1)} %reshape.466), calls=%async_computation.3 | async-start | bytes 1048576 | tf_op jit(solution)/shard_map/all_to_all | solution.py:77
  313.8 26.2 %all-gather.1 = bf16[16,9,2048]{2,1,0:T(8,128)(2,1)S(1)} all-gather(bf16[1,9,2048]{2,1,0:T(8,128)(2,1)S(1)} %fusion.51), channel_id=1, replica_groups=mesh['req'=16,'kv'=8] {'req'}, dimensions={0}, use_global_device_ids=true | all-gather | bytes 626688 | tf_op jit(solution)/shard_map/all_gather | solution.py:210
  341.1 4.4 %convolution_reduce_fusion = f32[144]{0:T(256)S(1)} fusion(bf16[144,2048]{1,0:T(8,128)(2,1)} %reshape.455, bf16[2048,1187]{0,1:T(8,128)(2,1)} %param.41), kind=kOutput, calls=%fused_computation.39 | convolution fusion | flops 700291840 | bytes 5452352 | tf_op jit(solution)/shard_map/dot_general | solution.py:209
  345.4 12.4 %pmax.14 = f32[144]{0:T(256)S(1)} all-reduce(f32[144]{0:T(256)S(1)} %convolution_reduce_fusion), channel_id=1, replica_groups=mesh['req'=16,'kv'=8] {'kv'}, use_global_device_ids=true, to_apply=%region_14.15 | all-reduce | flops 144 | bytes 1152 | tf_op jit(solution)/shard_map/pmax | solution.py:216
  357.9 38.7 %pmax.15 = f32[144]{0:T(256)} all-reduce(f32[144]{0:T(256)S(1)} %pmax.14), channel_id=1, replica_groups=mesh['req'=16,'kv'=8] {'req'}, use_global_device_ids=true, to_apply=%region_15.16 | all-reduce | flops 144 | bytes 1152 | tf_op jit(solution)/shard_map/pmax | solution.py:216
  397.0 2.4 scatter_custom_fusion.1
  (104 shorter events, 21.7 us)
Async XLA Ops:
  7.2 35.9 %copy-start = (bf16[384,2048]{1,0:T(8,128)(2,1)S(1)}, bf16[384,2048]{1,0:T(8,128)(2,1)}, u32[]{:S(2)}) copy-start(bf16[384,2048]{1,0:T(8,128)(2,1)} %param.39) | copy-start | bytes 4718596
  13.5 24.7 %all-to-all-start = ((bf16[128,2,1024]{2,1,0:T(2,128)(2,1)}), bf16[128,2,1024]{2,1,0:T(2,128)(2,1)S(1)}, u32[]{:S(2)}, u32[]{:S(2)}) async-start(bf16[128,2,1024]{2,1,0:T(2,128)(2,1)} %reshape.464), calls=%async_computation | async-start | bytes 1048576 | tf_op jit(solution)/shard_map/all_to_all | solution.py:77
  24.7 60.8 %all-gather.10.cloned.1.call-start = ((), (), s32[]{:S(2)}) async-start(), calls=%async_computation.7 | async-start | bytes 4718592 | tf_op jit(solution)/shard_map/all_gather | solution.py:115
  40.7 129.4 %all-gather.6.cloned.1.call-start = ((), (), s32[]{:S(2)}) async-start(), calls=%async_computation.4 | async-start | bytes 10027008 | tf_op jit(solution)/shard_map/all_gather | solution.py:129
  49.6 6.3 %copy-start.12 = (s32[8]{0:T(128)S(1)}, s32[8]{0:T(128)}, u32[]{:S(2)}) copy-start(s32[8]{0:T(128)} %param.23) | copy-start | bytes 100
  49.6 127.2 %all-to-all-start.1 = ((bf16[8,256,2048]{2,1,0:T(8,128)(2,1)}), bf16[8,256,2048]{2,1,0:T(8,128)(2,1)}, u32[]{:S(2)}, u32[]{:S(2)}) async-start(bf16[8,256,2048]{2,1,0:T(8,128)(2,1)} %broadcast_in_dim.48), calls=%async_computation.1 | async-start | bytes 16777216 | tf_op jit(solution)/shard_map/all_to_all | solution.py:117
  54.7 154.9 %all-gather.8.cloned.1.call-start = ((), (), s32[]{:S(2)}) async-start(), calls=%async_computation.5 | async-start | bytes 4718592 | tf_op jit(solution)/shard_map/all_gather | solution.py:178
  56.1 32.7 %copy-start.10 = (f32[2048]{0:T(1024)S(1)}, f32[2048]{0:T(1024)}, u32[]{:S(2)}) copy-start(f32[2048]{0:T(1024)} %param.29) | copy-start | bytes 24580
  85.5 3.4 copy-start.2
  89.0 1.2 copy-start.15
  90.2 1.9 copy-start.3
  90.2 2.3 copy-start.8
  92.1 4.1 %copy-start.13 = (f32[128]{0:T(128)S(1)}, f32[128]{0:T(128)}, u32[]{:S(2)}) copy-start(f32[128]{0:T(128)} %param.34) | copy-start | bytes 1540
  92.5 5.2 %copy-start.14 = (f32[128]{0:T(128)S(1)}, f32[128]{0:T(128)}, u32[]{:S(2)}) copy-start(f32[128]{0:T(128)} %param.33) | copy-start | bytes 1540
  97.7 2.4 copy-start.4
  99.7 2.3 copy-start.16
  102.0 3.9 copy-start.5
  102.0 4.7 %copy-start.17 = (bf16[1,2048,128]{2,1,0:T(8,128)(2,1)S(1)}, bf16[1,2048,128]{2,1,0:T(8,128)(2,1)}, u32[]{:S(2)}) copy-start(bf16[1,2048,128]{2,1,0:T(8,128)(2,1)} %param.27) | copy-start | bytes 1572868
  177.9 46.0 %copy-start.18 = (f32[2048]{0:T(1024)S(1)}, f32[2048]{0:T(1024)}, u32[]{:S(2)}) copy-start(f32[2048]{0:T(1024)} %param.36) | copy-start | bytes 24580
  177.9 121.1 %reduce-scatter.2.cloned.1.call-start = ((), (), s32[]{:S(2)}) async-start(), calls=%async_computation.6 | async-start | bytes 10616832 | tf_op jit(solution)/shard_map/reduce_scatter | solution.py:198
  223.8 7.1 %copy-start.9 = (bf16[1024,2048]{1,0:T(8,128)(2,1)}, bf16[1024,2048]{1,0:T(8,128)(2,1)S(1)}, u32[]{:S(2)}) copy-start(bf16[1024,2048]{1,0:T(8,128)(2,1)S(1)} %get-tuple-element.32) | copy-start | bytes 12582916
  223.9 7.0 %copy-start.7 = (bf16[768,2048]{1,0:T(8,128)(2,1)S(1)}, bf16[768,2048]{1,0:T(8,128)(2,1)}, u32[]{:S(2)}) copy-start(bf16[768,2048]{1,0:T(8,128)(2,1)} %get-tuple-element.10) | copy-start | bytes 9437188
  230.9 4.0 copy-start.6
  241.5 71.4 %copy-start.11 = (f32[2048]{0:T(1024)S(1)}, f32[2048]{0:T(1024)}, u32[]{:S(2)}) copy-start(f32[2048]{0:T(1024)} %param.40) | copy-start | bytes 24580
  303.5 93.0 %all-to-all-start.2 = ((bf16[128,2,1024]{2,1,0:T(2,128)(2,1)}), bf16[128,2,1024]{2,1,0:T(2,128)(2,1)S(1)}, u32[]{:S(2)}, u32[]{:S(2)}) async-start(bf16[128,2,1024]{2,1,0:T(2,128)(2,1)} %reshape.466), calls=%async_computation.3 | async-start | bytes 1048576 | tf_op jit(solution)/shard_map/all_to_all | solution.py:77
  340.0 59.4 %copy-start.1 = (bf16[384,2048]{1,0:T(8,128)(2,1)S(1)}, bf16[384,2048]{1,0:T(8,128)(2,1)}, u32[]{:S(2)}) copy-start(bf16[384,2048]{1,0:T(8,128)(2,1)} %param.39) | copy-start | bytes 4718596
Sparse Core Ops, SparseCore 0:
  40.8 44.6 all-gather.9
  87.7 82.3 all-gather.5
  178.0 31.6 all-gather.7
  241.6 57.3 reduce-scatter.1

commit v5 on v4

--- a/solution.py
+++ b/solution.py
@@ -186,23 +186,13 @@
     hidden_act = (jax.nn.silu(gate_part) * up_part).astype(jnp.bfloat16)
     tail_count = tok_req - fresh_count + 1
     tail_pad = -(-tail_count // 8) * 8
-    hidden_width = hidden_act.shape[1]
-    scatter_rows = jnp.concatenate(
-        [
-            hidden_act.reshape(kv_count, rows_dev, hidden_width),
-            jnp.broadcast_to(hidden_act[None, tok_req - tail_pad :], (kv_count, tail_pad, hidden_width)),
-        ],
-        axis=1,
-    ).reshape(kv_count * (rows_dev + tail_pad), hidden_width)
-    scatter_in = jnp.dot(scatter_rows, down_w, preferred_element_type=jnp.float32)
-    scattered = lax.psum_scatter(scatter_in, "kv", scatter_dimension=0, tiled=True)
-    ffn_part = scattered[:rows_dev]
-    tail_sum = scattered[rows_dev + tail_pad - tail_count :]
-    mine = lax.dynamic_slice_in_dim(resid, kv_index * rows_dev, rows_dev, axis=0)
-    out_rows = (mine.astype(jnp.float32) + ffn_part).astype(jnp.bfloat16)
-    going_back = jnp.zeros_like(out_rows).at[slot_place].set(out_rows)
-    returned = regroup(going_back)
-    layer_out = jnp.zeros_like(hidden_in).at[send_rows].set(returned)
+    down_part = jnp.dot(hidden_act, down_w, preferred_element_type=jnp.float32)
+    ffn_part = lax.psum_scatter(down_part, "kv", scatter_dimension=0, tiled=True)
+    tail_part = jnp.dot(hidden_act[tok_req - tail_pad :], down_w, preferred_element_type=jnp.float32)
+    tail_parts = lax.all_to_all(
+        jnp.broadcast_to(tail_part[None], (kv_count,) + tail_part.shape), "kv", split_axis=0, concat_axis=0, tiled=True
+    )
+    tail_sum = jnp.sum(tail_parts, axis=0)[tail_pad - tail_count :]
     tail_out = (resid[fresh_count - 1 :].astype(jnp.float32) + tail_sum).astype(jnp.bfloat16)
     tail_rows = norm_rows(tail_out, final_gain).astype(jnp.bfloat16)
     local_peaks = jnp.max(
@@ -214,6 +204,12 @@
         axis=1,
     )
     max_logit = lax.pmax(lax.pmax(local_peaks, "kv"), "req")
+    ffn_part, max_logit = lax.optimization_barrier((ffn_part, max_logit))
+    mine = lax.dynamic_slice_in_dim(resid, kv_index * rows_dev, rows_dev, axis=0)
+    out_rows = (mine.astype(jnp.float32) + ffn_part).astype(jnp.bfloat16)
+    going_back = jnp.zeros_like(out_rows).at[slot_place].set(out_rows)
+    returned = regroup(going_back)
+    layer_out = jnp.zeros_like(hidden_in).at[send_rows].set(returned)
     return (layer_out, max_logit)
 
 

time: 411 us -> 389 us (0.946)
  waiting for transfers between devices: 159 us -> 123 us
  blocking collectives: 77.3 us -> 94.6 us
  starting transfers between devices: 25.2 us -> 20.5 us
    reduce_scatter x1, waiting for transfers between devices: 57.5 us -> 0.01 us  [shards(): lax.psum_scatter(down_part, 'kv', scatter_dimension=0, tiled=True)]
    all_to_all x0 -> x1, waiting for transfers between devices: none -> 21.5 us  [shards(): lax.all_to_all(jnp.broadcast_to(tail_part[None], (kv_count,) + tail_part....]
    all_to_all x0 -> x1, blocking collectives: none -> 17.5 us  [regroup(): lax.all_to_all(rows_in, ('req', 'kv'), split_axis=0, concat_axis=0, tiled...]
    all_to_all x2 -> x1, starting transfers between devices: 19.4 us -> 11.1 us  [regroup(): lax.all_to_all(rows_in, ('req', 'kv'), split_axis=0, concat_axis=0, tiled...]
    dot_general x1 -> x2, matrix products: 6.46 us -> 8.23 us  [the longest x1 5.82 us: shards(): down_part = jnp.dot(hidden_act, down_w, preferred_element_type=jnp.float32)]
    all_to_all x2 -> x1, waiting for transfers between devices: 12.8 us -> 12.8 us  [regroup(): lax.all_to_all(rows_in, ('req', 'kv'), split_axis=0, concat_axis=0, tiled...]
  transfers between devices with their start and end apart: 7 -> 7, of which waited for: 5 -> 5; matrix products, arithmetic and copies ran while one was open for 19% -> 21% of each run, Pallas kernels for 0% -> 0%
where the time goes in v5:
time: 389 us; the launch traced here: 384 us
  waiting for transfers between devices  123 us (32%)
  blocking collectives  94.6 us (24%)
  matrix products  76.9 us (20%)
  local copies, waits for them, and re-layouts  29 us (7%)
  other arithmetic  24.3 us (6%)
  starting transfers between devices  20.5 us (5%)
  between operations  15.2 us (4%)
    pmax x2, blocking collectives, shards(): max_logit = lax.pmax(lax.pmax(local_peaks, 'kv'), 'req')  51.3 us
    all_gather x1, waiting for transfers between devices, shards(): weight_all = lax.all_gather(weight_piece, 'req', axis=1, tiled=True)  34.8 us
    all_gather x1, waiting for transfers between devices, shards(): lax.all_gather(pieces.reshape(tok_req, q_cols), 'kv', axis=1, tiled=True)  31.7 us
    all_gather x1, blocking collectives, shards(): lax.all_gather(tail_rows, 'req', axis=0, tiled=True)  25.7 us
    all_gather x1, waiting for transfers between devices, shards(): rows_all = lax.all_gather(owner_rows, 'kv', axis=0, tiled=True)  22.4 us
    all_to_all x1, waiting for transfers between devices, shards(): lax.all_to_all(jnp.broadcast_to(tail_part[None], (kv_count,) + tail_part....  21.5 us
    all_to_all x1, blocking collectives, regroup(): lax.all_to_all(rows_in, ('req', 'kv'), split_axis=0, concat_axis=0, tiled...  17.5 us
    sub x1, matrix products, prefill_full(): expd = jnp.exp(scores - row_peak)  16 us
  transfers between devices with their start and end apart: 7, of which 5 were waited for; matrix products, arithmetic and copies ran while one was open for 21% of the time, Pallas kernels for 0%

profile of v5, /device:TPU:0, one launch (start us, length us, event | category | flops | bytes accessed | tf_op | source)
XLA Modules:
  0.0 383.7 jit_solution(14750509282167342427)
XLA Ops:
  8.3 2.6 gather_fusion
  13.6 11.1 %all-to-all-start = ((bf16[128,2,1024]{2,1,0:T(2,128)(2,1)}), bf16[128,2,1024]{2,1,0:T(2,128)(2,1)S(1)}, u32[]{:S(2)}, u32[]{:S(2)}) async-start(bf16[128,2,1024]{2,1,0:T(2,128)(2,1)} %reshape.456), calls=%async_computation | async-start | bytes 1048576 | tf_op jit(solution)/shard_map/all_to_all | solution.py:77
  25.5 12.8 %all-to-all-done = bf16[128,2,1024]{2,1,0:T(2,128)(2,1)S(1)} async-done(((bf16[128,2,1024]{2,1,0:T(2,128)(2,1)}), bf16[128,2,1024]{2,1,0:T(2,128)(2,1)S(1)}, u32[]{:S(2)}, u32[]{:S(2)}) %all-to-all-start) | async-done | bytes 524320 | tf_op jit(solution)/shard_map/all_to_all | solution.py:77
  39.0 1.7 gather_fusion.1
  40.8 1.9 constant_dynamic-slice_fusion
  44.1 5.6 %broadcast_in_dim.48 = bf16[8,256,2048]{2,1,0:T(8,128)(2,1)} broadcast(bf16[256,2048]{1,0:T(8,128)(2,1)} %param.35), dimensions={1,2} | broadcast | bytes 9437184 | tf_op jit(solution)/shard_map/broadcast_in_dim | solution.py:118
  49.7 5.1 %all-to-all-start.1 = ((bf16[8,256,2048]{2,1,0:T(8,128)(2,1)}), bf16[8,256,2048]{2,1,0:T(8,128)(2,1)}, u32[]{:S(2)}, u32[]{:S(2)}) async-start(bf16[8,256,2048]{2,1,0:T(8,128)(2,1)} %broadcast_in_dim.48), calls=%async_computation.1 | async-start | bytes 16777216 | tf_op jit(solution)/shard_map/all_to_all | solution.py:117
  56.1 2.9 multiply_cosine_fusion
  59.2 4.0 %fusion.4 = pred[1016,3064]{1,0:T(8,128)(4,1)} fusion(s32[3064]{0:T(1024)S(1)} %iota_add_fusion, pred[3064]{0:T(1024)(128)(4,1)S(1)} %get-tuple-element.37, pred[3064]{0:T(1024)(128)(4,1)S(1)} %get-tuple-element.38), kind=kLoop, calls=%fused_computation.15 | loop fusion | flops 6226048 | bytes 3131408 | tf_op jit(solution)/shard_map/jit(_where)/select_n | solution.py:45
  63.2 22.4 %all-gather.10.cloned.1.call-done = bf16[1024,2048]{1,0:T(8,128)(2,1)} async-done(((bf16[128,2048]{1,0:T(8,128)(2,1)}), bf16[1024,2048]{1,0:T(8,128)(2,1)}) %all-gather.10.cloned.1.call-update) | async-done | bytes 4194320 | tf_op jit(solution)/shard_map/all_gather | solution.py:115
  85.6 3.2 fusion.10
  92.5 3.7 multiply_reduce_fusion.1
  102.1 3.8 convolution_convert_fusion
  106.8 16.0 %fusion.77 = (f32[2,1016]{1,0:T(2,128)S(1)}, f32[2,1016,3064]{2,1,0:T(8,128)}) fusion(pred[1016,3064]{1,0:T(8,128)(4,1)} %fusion.4, bf16[1016,128]{1,0:T(8,128)(2,1)S(1)} %copy.59, bf16[2048,128]{1,0:T(8,128)(2,1)S(1)} %bitcast.112, bf16[1024,2,64]{2,0,1:T(8,128)(2,1)S(1)} %get-tuple-element.19, bf16[1024,2,64]{2,0,1:T(8,128)(2,1)S(1)} %get-tuple-element.20), kind=kOutput, calls=%fused_computation.149 | convolution fusion | flops 1621384704 | bytes 29334016 | tf_op jit(solution)/shard_map/sub | solution.py:48
  122.7 12.5 %fusion.18 = bf16[1016,2,128]{2,0,1:T(8,128)(2,1)S(1)} fusion(f32[2,1016,3064]{2,1,0:T(8,128)} %get-tuple-element.34, f32[2,1016]{1,0:T(2,128)S(1)} %get-tuple-element.33, bf16[1016,128]{1,0:T(8,128)(2,1)S(1)} %slice.70, bf16[2048,128]{1,0:T(8,128)(2,1)} %bitcast.113), kind=kOutput, calls=%fused_computation.35 | convolution fusion | flops 1608149248 | bytes 26216896 | tf_op jit(solution)/shard_map/gck,kd->cgd/dot_general | solution.py:50
  135.3 34.8 %all-gather.6.cloned.1.call-done = bf16[3,768,2048]{2,1,0:T(8,128)(2,1)} async-done(((bf16[3,48,2048]{2,1,0:T(8,128)(2,1)}), bf16[3,768,2048]{2,1,0:T(8,128)(2,1)}) %all-gather.6.cloned.1.call-update) | async-done | bytes 9437200 | tf_op jit(solution)/shard_map/all_gather | solution.py:129
  170.2 6.6 %slice_bitcast_fusion = (bf16[768,2048]{1,0:T(8,128)(2,1)}, bf16[768,2048]{1,0:T(8,128)(2,1)}, bf16[768,2048]{1,0:T(8,128)(2,1)}) fusion(bf16[3,768,2048]{2,1,0:T(8,128)(2,1)} %all-gather.6.cloned.1.call-done), kind=kLoop, calls=%fused_computation.27 | loop fusion | bytes 18874368 | tf_op jit(solution)/shard_map/squeeze | solution.py:133
  177.9 31.7 %all-gather.8.cloned.1.call-done = bf16[1024,2048]{0,1:T(8,128)(2,1)} async-done(((bf16[1024,256]{0,1:T(8,128)(2,1)}), bf16[1024,2048]{0,1:T(8,128)(2,1)}) %all-gather.8.cloned.1.call-update) | async-done | bytes 4194320 | tf_op jit(solution)/shard_map/all_gather | solution.py:178
  209.6 14.2 %fusion.7 = (f32[1024]{0:T(1024)S(1)}, bf16[1024,2048]{1,0:T(8,128)(2,1)S(1)}) fusion(bf16[1024,2048]{0,1:T(8,128)(2,1)} %all-gather.8.cloned.1.call-done, bf16[2048,2048]{1,0:T(8,128)(2,1)} %bitcast.28, bf16[1024,2048]{1,0:T(8,128)(2,1)} %all-gather.10.cloned.1.call-done), kind=kOutput, calls=%fused_computation.20 | convolution fusion | flops 8602516480 | bytes 20975616 | tf_op jit(solution)/shard_map/dot_general | solution.py:180
  223.8 7.0 %fusion.20 = f32[1024,768]{1,0:T(8,128)S(1)} fusion(bf16[768,2048]{1,0:T(8,128)(2,1)} %get-tuple-element.11, bf16[1024,2048]{1,0:T(8,128)(2,1)S(1)} %get-tuple-element.36, f32[2048]{0:T(1024)S(1)} %copy-done.18, f32[1024]{0:T(1024)S(1)} %add_rsqrt_fusion.1), kind=kOutput, calls=%fused_computation.36 | convolution fusion | flops 3229614080 | bytes 10498048 | tf_op jit(solution)/shard_map/dot_general | solution.py:184
  230.9 3.9 %multiply_convert_fusion = bf16[1024,768]{1,0:T(8,128)(2,1)S(1)} fusion(f32[1024,768]{1,0:T(8,128)S(1)} %fusion.20, bf16[768,2048]{1,0:T(8,128)(2,1)S(1)} %copy-done.7, bf16[1024,2048]{1,0:T(8,128)(2,1)S(1)} %get-tuple-element.36, f32[2048]{0:T(1024)S(1)} %copy-done.18, f32[1024]{0:T(1024)S(1)} %add_rsqrt_fusion.1), kind=kOutput, calls=%fused_computation.30 | convolution fusion | flops 3234332672 | bytes 12070912 | tf_op jit(solution)/shard_map/dot_general | solution.py:185
  234.8 5.8 %fusion.82 = f32[1024,2048]{1,0:T(8,128)} fusion(bf16[1024,768]{1,0:T(8,128)(2,1)S(1)} %multiply_convert_fusion, bf16[768,2048]{1,0:T(8,128)(2,1)S(1)} %copy-done.4), kind=kOutput, calls=%fused_computation.150 | convolution fusion | flops 3221225472 | bytes 13107200 | tf_op jit(solution)/shard_map/dot_general | solution.py:189
  240.6 2.4 fusion.54
  244.2 3.6 all-to-all-start.2
  247.8 21.5 %all-to-all-done.2 = f32[8,16,2048]{2,1,0:T(8,128)S(1)} async-done(((f32[8,16,2048]{2,1,0:T(8,128)}), f32[8,16,2048]{2,1,0:T(8,128)S(1)}, u32[]{:S(2)}, u32[]{:S(2)}) %all-to-all-start.2) | async-done | bytes 1048608 | tf_op jit(solution)/shard_map/all_to_all | solution.py:192
  271.3 25.7 %all-gather.1 = bf16[16,9,2048]{2,1,0:T(8,128)(2,1)S(1)} all-gather(bf16[1,9,2048]{2,1,0:T(8,128)(2,1)S(1)} %fusion.49), channel_id=1, replica_groups=mesh['req'=16,'kv'=8] {'req'}, dimensions={0}, use_global_device_ids=true | all-gather | bytes 626688 | tf_op jit(solution)/shard_map/all_gather | solution.py:200
  297.3 4.2 %convolution_reduce_fusion = f32[144]{0:T(256)S(1)} fusion(bf16[144,2048]{1,0:T(8,128)(2,1)S(1)} %reshape.447, bf16[2048,1187]{0,1:T(8,128)(2,1)} %param.41), kind=kOutput, calls=%fused_computation.38 | convolution fusion | flops 700291840 | bytes 5452352 | tf_op jit(solution)/shard_map/dot_general | solution.py:199
  301.4 12.4 %pmax.14 = f32[144]{0:T(256)S(1)} all-reduce(f32[144]{0:T(256)S(1)} %convolution_reduce_fusion), channel_id=1, replica_groups=mesh['req'=16,'kv'=8] {'kv'}, use_global_device_ids=true, to_apply=%region_13.14 | all-reduce | flops 144 | bytes 1152 | tf_op jit(solution)/shard_map/pmax | solution.py:206
  313.9 38.9 %pmax.15 = f32[144]{0:T(256)} all-reduce(f32[144]{0:T(256)S(1)} %pmax.14), channel_id=1, replica_groups=mesh['req'=16,'kv'=8] {'req'}, use_global_device_ids=true, to_apply=%region_14.15 | all-reduce | flops 144 | bytes 1152 | tf_op jit(solution)/shard_map/pmax | solution.py:206
  352.8 2.3 scatter_custom_fusion
  356.5 17.5 %all_to_all.34 = bf16[128,2,1024]{2,1,0:T(2,128)(2,1)S(1)} all-to-all(bf16[128,2,1024]{2,1,0:T(2,128)(2,1)S(1)} %reshape.458), channel_id=1, replica_groups=mesh['req'=16,'kv'=8] {'req','kv'}, dimensions={0} | all-to-all | bytes 1048576 | tf_op jit(solution)/shard_map/all_to_all | solution.py:77
  374.4 2.4 scatter_custom_fusion.1
  (105 shorter events, 24.1 us)
Async XLA Ops:
  7.2 36.0 %copy-start = (bf16[384,2048]{1,0:T(8,128)(2,1)S(1)}, bf16[384,2048]{1,0:T(8,128)(2,1)}, u32[]{:S(2)}) copy-start(bf16[384,2048]{1,0:T(8,128)(2,1)} %param.39) | copy-start | bytes 4718596
  13.6 24.7 %all-to-all-start = ((bf16[128,2,1024]{2,1,0:T(2,128)(2,1)}), bf16[128,2,1024]{2,1,0:T(2,128)(2,1)S(1)}, u32[]{:S(2)}, u32[]{:S(2)}) async-start(bf16[128,2,1024]{2,1,0:T(2,128)(2,1)} %reshape.456), calls=%async_computation | async-start | bytes 1048576 | tf_op jit(solution)/shard_map/all_to_all | solution.py:77
  24.7 60.8 %all-gather.10.cloned.1.call-start = ((), (), s32[]{:S(2)}) async-start(), calls=%async_computation.8 | async-start | bytes 4718592 | tf_op jit(solution)/shard_map/all_gather | solution.py:115
  40.8 129.4 %all-gather.6.cloned.1.call-start = ((), (), s32[]{:S(2)}) async-start(), calls=%async_computation.5 | async-start | bytes 10027008 | tf_op jit(solution)/shard_map/all_gather | solution.py:129
  49.7 6.3 %copy-start.12 = (s32[8]{0:T(128)S(1)}, s32[8]{0:T(128)}, u32[]{:S(2)}) copy-start(s32[8]{0:T(128)} %param.23) | copy-start | bytes 100
  49.7 127.1 %all-to-all-start.1 = ((bf16[8,256,2048]{2,1,0:T(8,128)(2,1)}), bf16[8,256,2048]{2,1,0:T(8,128)(2,1)}, u32[]{:S(2)}, u32[]{:S(2)}) async-start(bf16[8,256,2048]{2,1,0:T(8,128)(2,1)} %broadcast_in_dim.48), calls=%async_computation.1 | async-start | bytes 16777216 | tf_op jit(solution)/shard_map/all_to_all | solution.py:117
  54.8 154.8 %all-gather.8.cloned.1.call-start = ((), (), s32[]{:S(2)}) async-start(), calls=%async_computation.6 | async-start | bytes 4718592 | tf_op jit(solution)/shard_map/all_gather | solution.py:178
  56.1 32.7 %copy-start.10 = (f32[2048]{0:T(1024)S(1)}, f32[2048]{0:T(1024)}, u32[]{:S(2)}) copy-start(f32[2048]{0:T(1024)} %param.29) | copy-start | bytes 24580
  85.6 3.4 copy-start.2
  89.0 1.2 copy-start.15
  90.3 1.9 copy-start.3
  90.3 2.3 copy-start.8
  92.2 4.1 %copy-start.13 = (f32[128]{0:T(128)S(1)}, f32[128]{0:T(128)}, u32[]{:S(2)}) copy-start(f32[128]{0:T(128)} %param.34) | copy-start | bytes 1540
  92.5 5.2 %copy-start.14 = (f32[128]{0:T(128)S(1)}, f32[128]{0:T(128)}, u32[]{:S(2)}) copy-start(f32[128]{0:T(128)} %param.33) | copy-start | bytes 1540
  97.7 2.4 copy-start.5
  99.8 2.3 copy-start.16
  102.1 3.9 %copy-start.6 = (bf16[8,2048,128]{2,1,0:T(8,128)(2,1)S(1)}, bf16[8,2048,128]{2,1,0:T(8,128)(2,1)}, u32[]{:S(2)}) copy-start(bf16[8,2048,128]{2,1,0:T(8,128)(2,1)} %param.26) | copy-start | bytes 12582916
  102.1 4.7 %copy-start.17 = (bf16[1,2048,128]{2,1,0:T(8,128)(2,1)S(1)}, bf16[1,2048,128]{2,1,0:T(8,128)(2,1)}, u32[]{:S(2)}) copy-start(bf16[1,2048,128]{2,1,0:T(8,128)(2,1)} %param.27) | copy-start | bytes 1572868
  177.8 46.0 %copy-start.18 = (f32[2048]{0:T(1024)S(1)}, f32[2048]{0:T(1024)}, u32[]{:S(2)}) copy-start(f32[2048]{0:T(1024)} %param.36) | copy-start | bytes 24580
  177.8 175.0 %reduce-scatter.2.cloned.1.call-start = ((), (), s32[]{:S(2)}) async-start(), calls=%async_computation.7 | async-start | bytes 9437184 | tf_op jit(solution)/shard_map/reduce_scatter | solution.py:190
  223.8 7.1 %copy-start.9 = (bf16[1024,2048]{1,0:T(8,128)(2,1)}, bf16[1024,2048]{1,0:T(8,128)(2,1)S(1)}, u32[]{:S(2)}) copy-start(bf16[1024,2048]{1,0:T(8,128)(2,1)S(1)} %get-tuple-element.36) | copy-start | bytes 12582916
  223.8 7.0 %copy-start.7 = (bf16[768,2048]{1,0:T(8,128)(2,1)S(1)}, bf16[768,2048]{1,0:T(8,128)(2,1)}, u32[]{:S(2)}) copy-start(bf16[768,2048]{1,0:T(8,128)(2,1)} %get-tuple-element.12) | copy-start | bytes 9437188
  230.9 3.9 %copy-start.4 = (bf16[768,2048]{1,0:T(8,128)(2,1)S(1)}, bf16[768,2048]{1,0:T(8,128)(2,1)}, u32[]{:S(2)}) copy-start(bf16[768,2048]{1,0:T(8,128)(2,1)} %get-tuple-element.13) | copy-start | bytes 9437188
  240.6 29.7 %copy-start.11 = (f32[2048]{0:T(1024)S(1)}, f32[2048]{0:T(1024)}, u32[]{:S(2)}) copy-start(f32[2048]{0:T(1024)} %param.40) | copy-start | bytes 24580
  244.2 25.1 %all-to-all-start.2 = ((f32[8,16,2048]{2,1,0:T(8,128)}), f32[8,16,2048]{2,1,0:T(8,128)S(1)}, u32[]{:S(2)}, u32[]{:S(2)}) async-start(f32[8,16,2048]{2,1,0:T(8,128)} %broadcast_in_dim.49), calls=%async_computation.3 | async-start | bytes 2097152 | tf_op jit(solution)/shard_map/all_to_all | solution.py:192
  313.9 63.0 %copy-start.1 = (bf16[384,2048]{1,0:T(8,128)(2,1)S(1)}, bf16[384,2048]{1,0:T(8,128)(2,1)}, u32[]{:S(2)}) copy-start(bf16[384,2048]{1,0:T(8,128)(2,1)} %param.39) | copy-start | bytes 4718596
Sparse Core Ops, SparseCore 0:
  40.9 44.6 all-gather.9
  87.7 82.3 all-gather.5
  177.9 31.6 all-gather.7
  240.7 63.3 reduce-scatter.1

commit v6 on v5

--- a/solution.py
+++ b/solution.py
@@ -71,6 +71,31 @@
         summed + own_w.astype(jnp.float32)[..., None] * value_self.astype(jnp.float32)[:, None, :]
     )
     return summed.astype(jnp.bfloat16)
+
+
+def butterfly(value, axis, combine):
+    size = lax.axis_size(axis)
+    step = 1
+    while step < size:
+        pairs = [(i, i ^ step) for i in range(size)]
+        value = combine(value, lax.ppermute(value, axis, pairs))
+        step *= 2
+    return value
+
+
+def butterfly_gather(value, axis):
+    size = lax.axis_size(axis)
+    me = lax.axis_index(axis)
+    step = 1
+    while step < size:
+        pairs = [(i, i ^ step) for i in range(size)]
+        other = lax.ppermute(value, axis, pairs)
+        low = (me // step) % 2 == 0
+        value = jnp.concatenate(
+            [jnp.where(low, value, other), jnp.where(low, other, value)], axis=0
+        )
+        step *= 2
+    return value
 
 
 def regroup(rows_in):
@@ -189,21 +214,18 @@
     down_part = jnp.dot(hidden_act, down_w, preferred_element_type=jnp.float32)
     ffn_part = lax.psum_scatter(down_part, "kv", scatter_dimension=0, tiled=True)
     tail_part = jnp.dot(hidden_act[tok_req - tail_pad :], down_w, preferred_element_type=jnp.float32)
-    tail_parts = lax.all_to_all(
-        jnp.broadcast_to(tail_part[None], (kv_count,) + tail_part.shape), "kv", split_axis=0, concat_axis=0, tiled=True
-    )
-    tail_sum = jnp.sum(tail_parts, axis=0)[tail_pad - tail_count :]
+    tail_sum = butterfly(tail_part, "kv", jnp.add)[tail_pad - tail_count :]
     tail_out = (resid[fresh_count - 1 :].astype(jnp.float32) + tail_sum).astype(jnp.bfloat16)
     tail_rows = norm_rows(tail_out, final_gain).astype(jnp.bfloat16)
     local_peaks = jnp.max(
         jnp.dot(
-            lax.all_gather(tail_rows, "req", axis=0, tiled=True),
+            butterfly_gather(tail_rows, "req"),
             lm_head,
             preferred_element_type=jnp.float32,
         ),
         axis=1,
     )
-    max_logit = lax.pmax(lax.pmax(local_peaks, "kv"), "req")
+    max_logit = butterfly(butterfly(local_peaks, "kv", jnp.maximum), "req", jnp.maximum)
     ffn_part, max_logit = lax.optimization_barrier((ffn_part, max_logit))
     mine = lax.dynamic_slice_in_dim(resid, kv_index * rows_dev, rows_dev, axis=0)
     out_rows = (mine.astype(jnp.float32) + ffn_part).astype(jnp.bfloat16)

time: 389 us -> 359 us (0.923)
  blocking collectives: 94.6 us -> 22.9 us
  starting transfers between devices: 20.5 us -> 41.8 us
  waiting for transfers between devices: 123 us -> 144 us
    pmax x2 -> x0, blocking collectives: 51.3 us -> none  [shards(): max_logit = lax.pmax(lax.pmax(local_peaks, 'kv'), 'req')]
    ppermute x0 -> x14, waiting for transfers between devices: none -> 42.4 us  [the longest x10 28 us: butterfly(): value = combine(value, lax.ppermute(value, axis, pairs))]
    all_gather x1 -> x0, blocking collectives: 25.7 us -> none  [shards(): lax.all_gather(tail_rows, 'req', axis=0, tiled=True)]
    ppermute x0 -> x14, starting transfers between devices: none -> 25.2 us  [the longest x10 15 us: butterfly(): value = combine(value, lax.ppermute(value, axis, pairs))]
    all_to_all x1 -> x0, waiting for transfers between devices: 21.5 us -> none  [shards(): lax.all_to_all(jnp.broadcast_to(tail_part[None], (kv_count,) + tail_part....]
    all_to_all x1, blocking collectives: 17.5 us -> 22.9 us  [regroup(): lax.all_to_all(rows_in, ('req', 'kv'), split_axis=0, concat_axis=0, tiled...]
  transfers between devices with their start and end apart: 7 -> 20, of which waited for: 5 -> 18; matrix products, arithmetic and copies ran while one was open for 21% -> 23% of each run, Pallas kernels for 0% -> 0%
where the time goes in v6:
time: 359 us; the launch traced here: 353 us
  waiting for transfers between devices  144 us (40%)
  matrix products  77.3 us (22%)
  starting transfers between devices  41.8 us (12%)
  local copies, waits for them, and re-layouts  27.6 us (8%)
  other arithmetic  24.5 us (7%)
  blocking collectives  22.9 us (6%)
  between operations  15.1 us (4%)
    all_gather x1, waiting for transfers between devices, shards(): weight_all = lax.all_gather(weight_piece, 'req', axis=1, tiled=True)  34.8 us
    all_gather x1, waiting for transfers between devices, shards(): lax.all_gather(pieces.reshape(tok_req, q_cols), 'kv', axis=1, tiled=True)  31.7 us
    ppermute x10, waiting for transfers between devices, butterfly(): value = combine(value, lax.ppermute(value, axis, pairs))  28 us
    all_to_all x1, blocking collectives, regroup(): lax.all_to_all(rows_in, ('req', 'kv'), split_axis=0, concat_axis=0, tiled...  22.9 us
    all_gather x1, waiting for transfers between devices, shards(): rows_all = lax.all_gather(owner_rows, 'kv', axis=0, tiled=True)  22.5 us
    sub x1, matrix products, prefill_full(): expd = jnp.exp(scores - row_peak)  16 us
    ppermute x10, starting transfers between devices, butterfly(): value = combine(value, lax.ppermute(value, axis, pairs))  15 us
    dot_general x1, matrix products, shards(): jnp.dot(attended, o_full, preferred_element_type=jnp.float32)  14.4 us
  transfers between devices with their start and end apart: 20, of which 18 were waited for; matrix products, arithmetic and copies ran while one was open for 23% of the time, Pallas kernels for 0%

profile of v6, /device:TPU:0, one launch (start us, length us, event | category | flops | bytes accessed | tf_op | source)
XLA Modules:
  0.0 353.4 jit_solution(15696420890278463641)
XLA Ops:
  13.5 11.1 %all-to-all-start = ((bf16[128,2,1024]{2,1,0:T(2,128)(2,1)}), bf16[128,2,1024]{2,1,0:T(2,128)(2,1)S(1)}, u32[]{:S(2)}, u32[]{:S(2)}) async-start(bf16[128,2,1024]{2,1,0:T(2,128)(2,1)} %reshape.453), calls=%async_computation | async-start | bytes 1048576 | tf_op jit(solution)/shard_map/all_to_all | solution.py:102
  25.4 12.8 %all-to-all-done = bf16[128,2,1024]{2,1,0:T(2,128)(2,1)S(1)} async-done(((bf16[128,2,1024]{2,1,0:T(2,128)(2,1)}), bf16[128,2,1024]{2,1,0:T(2,128)(2,1)S(1)}, u32[]{:S(2)}, u32[]{:S(2)}) %all-to-all-start) | async-done | bytes 524320 | tf_op jit(solution)/shard_map/all_to_all | solution.py:102
  44.0 5.6 %broadcast_in_dim.46 = bf16[8,256,2048]{2,1,0:T(8,128)(2,1)} broadcast(bf16[256,2048]{1,0:T(8,128)(2,1)} %param.35), dimensions={1,2} | broadcast | bytes 9437184 | tf_op jit(solution)/shard_map/broadcast_in_dim | solution.py:143
  49.6 5.1 %all-to-all-start.1 = ((bf16[8,256,2048]{2,1,0:T(8,128)(2,1)}), bf16[8,256,2048]{2,1,0:T(8,128)(2,1)}, u32[]{:S(2)}, u32[]{:S(2)}) async-start(bf16[8,256,2048]{2,1,0:T(8,128)(2,1)} %broadcast_in_dim.46), calls=%async_computation.1 | async-start | bytes 16777216 | tf_op jit(solution)/shard_map/all_to_all | solution.py:142
  55.8 3.0 multiply_cosine_fusion
  58.8 4.1 %fusion.4 = pred[1016,3064]{1,0:T(8,128)(4,1)} fusion(s32[3064]{0:T(1024)S(1)} %iota_add_fusion, pred[3064]{0:T(1024)(128)(4,1)S(1)} %get-tuple-element.47, pred[3064]{0:T(1024)(128)(4,1)S(1)} %get-tuple-element.48), kind=kLoop, calls=%fused_computation.15 | loop fusion | flops 6226048 | bytes 3131408 | tf_op jit(solution)/shard_map/jit(_where)/select_n | solution.py:45
  62.9 22.5 %all-gather.9.cloned.1.call-done = bf16[1024,2048]{1,0:T(8,128)(2,1)} async-done(((bf16[128,2048]{1,0:T(8,128)(2,1)}), bf16[1024,2048]{1,0:T(8,128)(2,1)}) %all-gather.9.cloned.1.call-update) | async-done | bytes 4194320 | tf_op jit(solution)/shard_map/all_gather | solution.py:140
  85.4 3.2 fusion.10
  92.4 3.7 %multiply_reduce_fusion.1 = (f32[1024]{0:T(1024)S(1)}, f32[1024,128]{0,1:T(8,128)S(1)}) fusion(bf16[1024,2048]{1,0:T(8,128)(2,1)} %copy-done.3, bf16[2048,128]{1,0:T(8,128)(2,1)S(1)} %copy-done.8), kind=kOutput, calls=%fused_computation.64 | convolution fusion | flops 537132032 | bytes 5246976 | tf_op jit(solution)/shard_map/dot_general | solution.py:164
  101.9 3.8 %convolution_convert_fusion = bf16[1024,128]{1,0:T(8,128)(2,1)S(1)} fusion(bf16[1024,2048]{1,0:T(8,128)(2,1)} %copy-done.3, bf16[2048,128]{1,0:T(8,128)(2,1)S(1)} %copy-done.16), kind=kOutput, calls=%fused_computation.37 | convolution fusion | flops 537001984 | bytes 4980736 | tf_op jit(solution)/shard_map/dot_general | solution.py:165
  106.6 16.0 %fusion.82 = (f32[2,1016]{1,0:T(2,128)S(1)}, f32[2,1016,3064]{2,1,0:T(8,128)}) fusion(pred[1016,3064]{1,0:T(8,128)(4,1)} %fusion.4, bf16[1016,128]{1,0:T(8,128)(2,1)S(1)} %copy.49, bf16[2048,128]{1,0:T(8,128)(2,1)S(1)} %bitcast.109, bf16[1024,2,64]{2,0,1:T(8,128)(2,1)S(1)} %get-tuple-element.21, bf16[1024,2,64]{2,0,1:T(8,128)(2,1)S(1)} %get-tuple-element.22), kind=kOutput, calls=%fused_computation.164 | convolution fusion | flops 1621384704 | bytes 29334016 | tf_op jit(solution)/shard_map/sub | solution.py:48
  122.6 12.5 %fusion.18 = bf16[1016,2,128]{2,0,1:T(8,128)(2,1)S(1)} fusion(f32[2,1016,3064]{2,1,0:T(8,128)} %get-tuple-element.44, f32[2,1016]{1,0:T(2,128)S(1)} %get-tuple-element.43, bf16[1016,128]{1,0:T(8,128)(2,1)S(1)} %slice.70, bf16[2048,128]{1,0:T(8,128)(2,1)} %bitcast.110), kind=kOutput, calls=%fused_computation.35 | convolution fusion | flops 1608149248 | bytes 26216896 | tf_op jit(solution)/shard_map/gck,kd->cgd/dot_general | solution.py:50
  135.2 34.8 %all-gather.5.cloned.1.call-done = bf16[3,768,2048]{2,1,0:T(8,128)(2,1)} async-done(((bf16[3,48,2048]{2,1,0:T(8,128)(2,1)}), bf16[3,768,2048]{2,1,0:T(8,128)(2,1)}) %all-gather.5.cloned.1.call-update) | async-done | bytes 9437200 | tf_op jit(solution)/shard_map/all_gather | solution.py:154
  170.0 6.6 %slice_bitcast_fusion = (bf16[768,2048]{1,0:T(8,128)(2,1)}, bf16[768,2048]{1,0:T(8,128)(2,1)}, bf16[768,2048]{1,0:T(8,128)(2,1)}) fusion(bf16[3,768,2048]{2,1,0:T(8,128)(2,1)} %all-gather.5.cloned.1.call-done), kind=kLoop, calls=%fused_computation.27 | loop fusion | bytes 18874368 | tf_op jit(solution)/shard_map/squeeze | solution.py:158
  177.7 31.7 %all-gather.7.cloned.1.call-done = bf16[1024,2048]{0,1:T(8,128)(2,1)} async-done(((bf16[1024,256]{0,1:T(8,128)(2,1)}), bf16[1024,2048]{0,1:T(8,128)(2,1)}) %all-gather.7.cloned.1.call-update) | async-done | bytes 4194320 | tf_op jit(solution)/shard_map/all_gather | solution.py:203
  209.5 14.4 %fusion.7 = (f32[1024]{0:T(1024)S(1)}, bf16[1024,2048]{1,0:T(8,128)(2,1)S(1)}) fusion(bf16[1024,2048]{0,1:T(8,128)(2,1)} %all-gather.7.cloned.1.call-done, bf16[2048,2048]{1,0:T(8,128)(2,1)} %bitcast.28, bf16[1024,2048]{1,0:T(8,128)(2,1)} %all-gather.9.cloned.1.call-done), kind=kOutput, calls=%fused_computation.20 | convolution fusion | flops 8602516480 | bytes 20975616 | tf_op jit(solution)/shard_map/dot_general | solution.py:205
  223.9 7.0 %fusion.20 = f32[1024,768]{1,0:T(8,128)S(1)} fusion(bf16[768,2048]{1,0:T(8,128)(2,1)} %get-tuple-element.11, bf16[1024,2048]{1,0:T(8,128)(2,1)S(1)} %get-tuple-element.46, f32[2048]{0:T(1024)S(1)} %copy-done.18, f32[1024]{0:T(1024)S(1)} %add_rsqrt_fusion.1), kind=kOutput, calls=%fused_computation.36 | convolution fusion | flops 3229614080 | bytes 10498048 | tf_op jit(solution)/shard_map/dot_general | solution.py:209
  230.9 3.9 %multiply_convert_fusion = bf16[1024,768]{1,0:T(8,128)(2,1)S(1)} fusion(f32[1024,768]{1,0:T(8,128)S(1)} %fusion.20, bf16[768,2048]{1,0:T(8,128)(2,1)S(1)} %copy-done.7, bf16[1024,2048]{1,0:T(8,128)(2,1)S(1)} %get-tuple-element.46, f32[2048]{0:T(1024)S(1)} %copy-done.18, f32[1024]{0:T(1024)S(1)} %add_rsqrt_fusion.1), kind=kOutput, calls=%fused_computation.30 | convolution fusion | flops 3234332672 | bytes 12070912 | tf_op jit(solution)/shard_map/dot_general | solution.py:210
  234.8 5.9 %fusion.87 = f32[1024,2048]{1,0:T(8,128)} fusion(bf16[1024,768]{1,0:T(8,128)(2,1)S(1)} %multiply_convert_fusion, bf16[768,2048]{1,0:T(8,128)(2,1)S(1)} %copy-done.4), kind=kOutput, calls=%fused_computation.165 | convolution fusion | flops 3221225472 | bytes 13107200 | tf_op jit(solution)/shard_map/dot_general | solution.py:214
  245.1 5.2 %collective-permute-done.1 = f32[16,2048]{1,0:T(8,128)S(1)} collective-permute-done((f32[16,2048]{1,0:T(8,128)S(1)}, f32[16,2048]{1,0:T(8,128)S(1)}, u32[]{:S(2)}, u32[]{:S(2)}) %collective-permute-start.1) | collective-permute-done | bytes 131104 | tf_op jit(solution)/shard_map/ppermute | solution.py:81
  252.0 6.8 %collective-permute-done.2 = f32[16,2048]{1,0:T(8,128)S(1)} collective-permute-done((f32[16,2048]{1,0:T(8,128)S(1)}, f32[16,2048]{1,0:T(8,128)S(1)}, u32[]{:S(2)}, u32[]{:S(2)}) %collective-permute-start.2) | collective-permute-done | bytes 131104 | tf_op jit(solution)/shard_map/ppermute | solution.py:81
  264.4 3.1 collective-permute-start.4
  267.5 3.1 collective-permute-done.4
  272.3 3.8 %collective-permute-done.5 = bf16[36,2048]{1,0:T(8,128)(2,1)S(1)} collective-permute-done((bf16[36,2048]{1,0:T(8,128)(2,1)S(1)}, bf16[36,2048]{1,0:T(8,128)(2,1)S(1)}, u32[]{:S(2)}, u32[]{:S(2)}) %collective-permute-start.5) | collective-permute-done | bytes 147488 | tf_op jit(solution)/shard_map/ppermute | solution.py:92
  276.3 3.9 %collective-permute-start.6 = (bf16[72,2048]{1,0:T(8,128)(2,1)S(1)}, bf16[72,2048]{1,0:T(8,128)(2,1)S(1)}, u32[]{:S(2)}, u32[]{:S(2)}) collective-permute-start(bf16[72,2048]{1,0:T(8,128)(2,1)S(1)} %pad_maximum_fusion.2), channel_id=1, source_target_pairs={{0,64},{8,72},{16,80},{24,88},{32,96},{40,104},{48,112},{56,120},{... | collective-permute-start | bytes 884744 | tf_op jit(solution)/shard_map/ppermute | solution.py:92
  280.1 4.7 %collective-permute-done.6 = bf16[72,2048]{1,0:T(8,128)(2,1)S(1)} collective-permute-done((bf16[72,2048]{1,0:T(8,128)(2,1)S(1)}, bf16[72,2048]{1,0:T(8,128)(2,1)S(1)}, u32[]{:S(2)}, u32[]{:S(2)}) %collective-permute-start.6) | collective-permute-done | bytes 294944 | tf_op jit(solution)/shard_map/ppermute | solution.py:92
  285.0 4.3 %convolution_reduce_fusion = f32[144]{0:T(256)S(1)} fusion(bf16[2048,1187]{0,1:T(8,128)(2,1)} %param.41, bf16[72,2048]{1,0:T(8,128)(2,1)S(1)} %get-tuple-element.24, bf16[72,2048]{1,0:T(8,128)(2,1)S(1)} %get-tuple-element.23), kind=kOutput, calls=%fused_computation.38 | convolution fusion | flops 701471488 | bytes 5452352 | tf_op jit(solution)/shard_map/dot_general | solution.py:221
  291.0 3.1 collective-permute-done.8
  296.0 3.2 collective-permute-done.9
  302.7 3.0 collective-permute-start.11
  311.3 3.8 %collective-permute-start.13 = (f32[144]{0:T(256)S(1)}, f32[144]{0:T(256)S(1)}, u32[]{:S(2)}, u32[]{:S(2)}) collective-permute-start(f32[144]{0:T(256)S(1)} %max.30), channel_id=1, source_target_pairs={{0,64},{8,72},{16,80},{24,88},{32,96},{40,104},{48,112},{56,120},{... | collective-permute-start | bytes 1736 | tf_op jit(solution)/shard_map/ppermute | solution.py:81
  321.0 22.9 %all_to_all.29 = bf16[128,2,1024]{2,1,0:T(2,128)(2,1)S(1)} all-to-all(bf16[128,2,1024]{2,1,0:T(2,128)(2,1)S(1)} %reshape.455), channel_id=1, replica_groups=mesh['req'=16,'kv'=8] {'req','kv'}, dimensions={0} | all-to-all | bytes 1048576 | tf_op jit(solution)/shard_map/all_to_all | solution.py:102
  (141 shorter events, 59.9 us)
Async XLA Ops:
  7.2 35.9 %copy-start = (bf16[384,2048]{1,0:T(8,128)(2,1)S(1)}, bf16[384,2048]{1,0:T(8,128)(2,1)}, u32[]{:S(2)}) copy-start(bf16[384,2048]{1,0:T(8,128)(2,1)} %param.39) | copy-start | bytes 4718596
  13.5 24.7 %all-to-all-start = ((bf16[128,2,1024]{2,1,0:T(2,128)(2,1)}), bf16[128,2,1024]{2,1,0:T(2,128)(2,1)S(1)}, u32[]{:S(2)}, u32[]{:S(2)}) async-start(bf16[128,2,1024]{2,1,0:T(2,128)(2,1)} %reshape.453), calls=%async_computation | async-start | bytes 1048576 | tf_op jit(solution)/shard_map/all_to_all | solution.py:102
  24.7 60.7 %all-gather.9.cloned.1.call-start = ((), (), s32[]{:S(2)}) async-start(), calls=%async_computation.7 | async-start | bytes 4718592 | tf_op jit(solution)/shard_map/all_gather | solution.py:140
  40.7 129.3 %all-gather.5.cloned.1.call-start = ((), (), s32[]{:S(2)}) async-start(), calls=%async_computation.4 | async-start | bytes 10027008 | tf_op jit(solution)/shard_map/all_gather | solution.py:154
  49.6 6.0 %copy-start.12 = (s32[8]{0:T(128)S(1)}, s32[8]{0:T(128)}, u32[]{:S(2)}) copy-start(s32[8]{0:T(128)} %param.23) | copy-start | bytes 100
  49.6 127.0 %all-to-all-start.1 = ((bf16[8,256,2048]{2,1,0:T(8,128)(2,1)}), bf16[8,256,2048]{2,1,0:T(8,128)(2,1)}, u32[]{:S(2)}, u32[]{:S(2)}) async-start(bf16[8,256,2048]{2,1,0:T(8,128)(2,1)} %broadcast_in_dim.46), calls=%async_computation.1 | async-start | bytes 16777216 | tf_op jit(solution)/shard_map/all_to_all | solution.py:142
  54.8 154.7 %all-gather.7.cloned.1.call-start = ((), (), s32[]{:S(2)}) async-start(), calls=%async_computation.5 | async-start | bytes 4718592 | tf_op jit(solution)/shard_map/all_gather | solution.py:203
  55.8 32.9 %copy-start.11 = (f32[2048]{0:T(1024)S(1)}, f32[2048]{0:T(1024)}, u32[]{:S(2)}) copy-start(f32[2048]{0:T(1024)} %param.29) | copy-start | bytes 24580
  92.0 4.1 %copy-start.13 = (f32[128]{0:T(128)S(1)}, f32[128]{0:T(128)}, u32[]{:S(2)}) copy-start(f32[128]{0:T(128)} %param.34) | copy-start | bytes 1540
  92.4 5.2 %copy-start.14 = (f32[128]{0:T(128)S(1)}, f32[128]{0:T(128)}, u32[]{:S(2)}) copy-start(f32[128]{0:T(128)} %param.33) | copy-start | bytes 1540
  101.9 3.9 %copy-start.6 = (bf16[8,2048,128]{2,1,0:T(8,128)(2,1)S(1)}, bf16[8,2048,128]{2,1,0:T(8,128)(2,1)}, u32[]{:S(2)}) copy-start(bf16[8,2048,128]{2,1,0:T(8,128)(2,1)} %param.26) | copy-start | bytes 12582916
  101.9 4.7 %copy-start.17 = (bf16[1,2048,128]{2,1,0:T(8,128)(2,1)S(1)}, bf16[1,2048,128]{2,1,0:T(8,128)(2,1)}, u32[]{:S(2)}) copy-start(bf16[1,2048,128]{2,1,0:T(8,128)(2,1)} %param.27) | copy-start | bytes 1572868
  177.7 46.2 %copy-start.18 = (f32[2048]{0:T(1024)S(1)}, f32[2048]{0:T(1024)}, u32[]{:S(2)}) copy-start(f32[2048]{0:T(1024)} %param.36) | copy-start | bytes 24580
  177.7 139.6 %reduce-scatter.2.cloned.1.call-start = ((), (), s32[]{:S(2)}) async-start(), calls=%async_computation.6 | async-start | bytes 9437184 | tf_op jit(solution)/shard_map/reduce_scatter | solution.py:215
  223.9 7.1 %copy-start.9 = (bf16[1024,2048]{1,0:T(8,128)(2,1)}, bf16[1024,2048]{1,0:T(8,128)(2,1)S(1)}, u32[]{:S(2)}) copy-start(bf16[1024,2048]{1,0:T(8,128)(2,1)S(1)} %get-tuple-element.46) | copy-start | bytes 12582916
  223.9 7.0 %copy-start.7 = (bf16[768,2048]{1,0:T(8,128)(2,1)S(1)}, bf16[768,2048]{1,0:T(8,128)(2,1)}, u32[]{:S(2)}) copy-start(bf16[768,2048]{1,0:T(8,128)(2,1)} %get-tuple-element.12) | copy-start | bytes 9437188
  240.7 19.1 %copy-start.10 = (f32[2048]{0:T(1024)S(1)}, f32[2048]{0:T(1024)}, u32[]{:S(2)}) copy-start(f32[2048]{0:T(1024)} %param.40) | copy-start | bytes 24580
  243.1 1.3 collective-permute-start
  244.5 5.7 %collective-permute-start.1 = (f32[16,2048]{1,0:T(8,128)S(1)}, f32[16,2048]{1,0:T(8,128)S(1)}, u32[]{:S(2)}, u32[]{:S(2)}) collective-permute-start(f32[16,2048]{1,0:T(8,128)S(1)} %add.180), channel_id=1, source_target_pairs={{0,2},{1,3},{2,0},{3,1},{4,6},{5,7},{6,4},{7,5},{8,10},{9,11},{10,... | collective-permute-start | bytes 393224 | tf_op jit(solution)/shard_map/ppermute | solution.py:81
  250.3 8.5 %collective-permute-start.2 = (f32[16,2048]{1,0:T(8,128)S(1)}, f32[16,2048]{1,0:T(8,128)S(1)}, u32[]{:S(2)}, u32[]{:S(2)}) collective-permute-start(f32[16,2048]{1,0:T(8,128)S(1)} %add.181), channel_id=1, source_target_pairs={{0,4},{1,5},{2,6},{3,7},{4,0},{5,1},{6,2},{7,3},{8,12},{9,13},{10,... | collective-permute-start | bytes 393224 | tf_op jit(solution)/shard_map/ppermute | solution.py:81
  259.9 4.3 %collective-permute-start.3 = (bf16[9,2048]{1,0:T(8,128)(2,1)S(1)}, bf16[9,2048]{1,0:T(8,128)(2,1)S(1)}, u32[]{:S(2)}, u32[]{:S(2)}) collective-permute-start(bf16[9,2048]{1,0:T(8,128)(2,1)S(1)} %fusion.46), channel_id=1, source_target_pairs={{0,8},{8,0},{16,24},{24,16},{32,40},{40,32},{48,56},{56,48},{64,72... | collective-permute-start | bytes 110600 | tf_op jit(solution)/shard_map/ppermute | solution.py:92
  264.4 6.2 %collective-permute-start.4 = (bf16[18,2048]{1,0:T(8,128)(2,1)S(1)}, bf16[18,2048]{1,0:T(8,128)(2,1)S(1)}, u32[]{:S(2)}, u32[]{:S(2)}) collective-permute-start(bf16[18,2048]{1,0:T(8,128)(2,1)S(1)} %pad_maximum_fusion.4), channel_id=1, source_target_pairs={{0,16},{8,24},{16,0},{24,8},{32,48},{40,56},{48,32},{56,40},{64,80... | collective-permute-start | bytes 221192 | tf_op jit(solution)/shard_map/ppermute | solution.py:92
  270.7 5.4 %collective-permute-start.5 = (bf16[36,2048]{1,0:T(8,128)(2,1)S(1)}, bf16[36,2048]{1,0:T(8,128)(2,1)S(1)}, u32[]{:S(2)}, u32[]{:S(2)}) collective-permute-start(bf16[36,2048]{1,0:T(8,128)(2,1)S(1)} %pad_maximum_fusion.3), channel_id=1, source_target_pairs={{0,32},{8,40},{16,48},{24,56},{32,0},{40,8},{48,16},{56,24},{64,96... | collective-permute-start | bytes 442376 | tf_op jit(solution)/shard_map/ppermute | solution.py:92
  276.3 8.6 %collective-permute-start.6 = (bf16[72,2048]{1,0:T(8,128)(2,1)S(1)}, bf16[72,2048]{1,0:T(8,128)(2,1)S(1)}, u32[]{:S(2)}, u32[]{:S(2)}) collective-permute-start(bf16[72,2048]{1,0:T(8,128)(2,1)S(1)} %pad_maximum_fusion.2), channel_id=1, source_target_pairs={{0,64},{8,72},{16,80},{24,88},{32,96},{40,104},{48,112},{56,120},{... | collective-permute-start | bytes 884744 | tf_op jit(solution)/shard_map/ppermute | solution.py:92
  289.3 1.2 collective-permute-start.7
  290.5 3.6 %collective-permute-start.8 = (f32[144]{0:T(256)S(1)}, f32[144]{0:T(256)S(1)}, u32[]{:S(2)}, u32[]{:S(2)}) collective-permute-start(f32[144]{0:T(256)S(1)} %max.25), channel_id=1, source_target_pairs={{0,2},{1,3},{2,0},{3,1},{4,6},{5,7},{6,4},{7,5},{8,10},{9,11},{10,... | collective-permute-start | bytes 1736 | tf_op jit(solution)/shard_map/ppermute | solution.py:81
  294.0 5.1 %collective-permute-start.9 = (f32[144]{0:T(256)S(1)}, f32[144]{0:T(256)S(1)}, u32[]{:S(2)}, u32[]{:S(2)}) collective-permute-start(f32[144]{0:T(256)S(1)} %max.26), channel_id=1, source_target_pairs={{0,4},{1,5},{2,6},{3,7},{4,0},{5,1},{6,2},{7,3},{8,12},{9,13},{10,... | collective-permute-start | bytes 1736 | tf_op jit(solution)/shard_map/ppermute | solution.py:81
  299.1 3.6 %collective-permute-start.10 = (f32[144]{0:T(256)S(1)}, f32[144]{0:T(256)S(1)}, u32[]{:S(2)}, u32[]{:S(2)}) collective-permute-start(f32[144]{0:T(256)S(1)} %max.27), channel_id=1, source_target_pairs={{0,8},{8,0},{16,24},{24,16},{32,40},{40,32},{48,56},{56,48},{64,72... | collective-permute-start | bytes 1736 | tf_op jit(solution)/shard_map/ppermute | solution.py:81
  302.7 5.1 %collective-permute-start.11 = (f32[144]{0:T(256)S(1)}, f32[144]{0:T(256)S(1)}, u32[]{:S(2)}, u32[]{:S(2)}) collective-permute-start(f32[144]{0:T(256)S(1)} %max.28), channel_id=1, source_target_pairs={{0,16},{8,24},{16,0},{24,8},{32,48},{40,56},{48,32},{56,40},{64,80... | collective-permute-start | bytes 1736 | tf_op jit(solution)/shard_map/ppermute | solution.py:81
  307.8 3.6 %collective-permute-start.12 = (f32[144]{0:T(256)S(1)}, f32[144]{0:T(256)S(1)}, u32[]{:S(2)}, u32[]{:S(2)}) collective-permute-start(f32[144]{0:T(256)S(1)} %max.29), channel_id=1, source_target_pairs={{0,32},{8,40},{16,48},{24,56},{32,0},{40,8},{48,16},{56,24},{64,96... | collective-permute-start | bytes 1736 | tf_op jit(solution)/shard_map/ppermute | solution.py:81
  311.3 5.4 %collective-permute-start.13 = (f32[144]{0:T(256)S(1)}, f32[144]{0:T(256)S(1)}, u32[]{:S(2)}, u32[]{:S(2)}) collective-permute-start(f32[144]{0:T(256)S(1)} %max.30), channel_id=1, source_target_pairs={{0,64},{8,72},{16,80},{24,88},{32,96},{40,104},{48,112},{56,120},{... | collective-permute-start | bytes 1736 | tf_op jit(solution)/shard_map/ppermute | solution.py:81
  316.7 30.0 %copy-start.1 = (bf16[384,2048]{1,0:T(8,128)(2,1)S(1)}, bf16[384,2048]{1,0:T(8,128)(2,1)}, u32[]{:S(2)}) copy-start(bf16[384,2048]{1,0:T(8,128)(2,1)} %param.39) | copy-start | bytes 4718596
  (7 other events, 17.5 us)
Sparse Core Ops, SparseCore 0:
  40.8 44.5 all-gather.8
  87.5 82.4 all-gather.4
  177.8 31.6 all-gather.6
  240.8 55.1 reduce-scatter.1

commit v7 on v5

--- a/solution.py
+++ b/solution.py
@@ -71,6 +71,27 @@
         summed + own_w.astype(jnp.float32)[..., None] * value_self.astype(jnp.float32)[:, None, :]
     )
     return summed.astype(jnp.bfloat16)
+
+
+def direct_reduce(value, axis, combine):
+    size = lax.axis_size(axis)
+    total = value
+    for shift in range(1, size):
+        pairs = [(i, (i + shift) % size) for i in range(size)]
+        total = combine(total, lax.ppermute(value, axis, pairs))
+    return total
+
+
+def direct_gather(value, axis):
+    size = lax.axis_size(axis)
+    me = lax.axis_index(axis)
+    received = [value]
+    for shift in range(1, size):
+        pairs = [(i, (i + shift) % size) for i in range(size)]
+        received.append(lax.ppermute(value, axis, pairs))
+    order = (me - jnp.arange(size, dtype=jnp.int32)) % size
+    stacked = jnp.stack(received)[order]
+    return stacked.reshape((size * value.shape[0],) + value.shape[1:])
 
 
 def regroup(rows_in):
@@ -189,21 +210,18 @@
     down_part = jnp.dot(hidden_act, down_w, preferred_element_type=jnp.float32)
     ffn_part = lax.psum_scatter(down_part, "kv", scatter_dimension=0, tiled=True)
     tail_part = jnp.dot(hidden_act[tok_req - tail_pad :], down_w, preferred_element_type=jnp.float32)
-    tail_parts = lax.all_to_all(
-        jnp.broadcast_to(tail_part[None], (kv_count,) + tail_part.shape), "kv", split_axis=0, concat_axis=0, tiled=True
-    )
-    tail_sum = jnp.sum(tail_parts, axis=0)[tail_pad - tail_count :]
+    tail_sum = direct_reduce(tail_part, "kv", jnp.add)[tail_pad - tail_count :]
     tail_out = (resid[fresh_count - 1 :].astype(jnp.float32) + tail_sum).astype(jnp.bfloat16)
     tail_rows = norm_rows(tail_out, final_gain).astype(jnp.bfloat16)
     local_peaks = jnp.max(
         jnp.dot(
-            lax.all_gather(tail_rows, "req", axis=0, tiled=True),
+            direct_gather(tail_rows, "req"),
             lm_head,
             preferred_element_type=jnp.float32,
         ),
         axis=1,
     )
-    max_logit = lax.pmax(lax.pmax(local_peaks, "kv"), "req")
+    max_logit = direct_reduce(direct_reduce(local_peaks, "kv", jnp.maximum), "req", jnp.maximum)
     ffn_part, max_logit = lax.optimization_barrier((ffn_part, max_logit))
     mine = lax.dynamic_slice_in_dim(resid, kv_index * rows_dev, rows_dev, axis=0)
     out_rows = (mine.astype(jnp.float32) + ffn_part).astype(jnp.bfloat16)

time: 389 us -> 388 us (level)
  blocking collectives: 94.6 us -> 18.2 us
  starting transfers between devices: 20.5 us -> 89.9 us
  waiting for transfers between devices: 123 us -> 129 us
    ppermute x0 -> x44, starting transfers between devices: none -> 73.3 us  [the longest x29 42 us: direct_reduce(): total = combine(total, lax.ppermute(value, axis, pairs))]
    pmax x2 -> x0, blocking collectives: 51.3 us -> none  [shards(): max_logit = lax.pmax(lax.pmax(local_peaks, 'kv'), 'req')]
    ppermute x0 -> x44, waiting for transfers between devices: none -> 27.3 us  [the longest x29 24.2 us: direct_reduce(): total = combine(total, lax.ppermute(value, axis, pairs))]
    all_gather x1 -> x0, blocking collectives: 25.7 us -> none  [shards(): lax.all_gather(tail_rows, 'req', axis=0, tiled=True)]
    all_to_all x1 -> x0, waiting for transfers between devices: 21.5 us -> none  [shards(): lax.all_to_all(jnp.broadcast_to(tail_part[None], (kv_count,) + tail_part....]
  transfers between devices with their start and end apart: 7 -> 50, of which waited for: 5 -> 18; matrix products, arithmetic and copies ran while one was open for 21% -> 21% of each run, Pallas kernels for 0% -> 0%
where the time goes in v7:
time: 388 us; the launch traced here: 383 us
  waiting for transfers between devices  129 us (33%)
  starting transfers between devices  89.9 us (23%)
  matrix products  77.2 us (20%)
  local copies, waits for them, and re-layouts  28.7 us (7%)
  other arithmetic  24.1 us (6%)
  blocking collectives  18.2 us (5%)
  between operations  15.5 us (4%)
    ppermute x29, starting transfers between devices, direct_reduce(): total = combine(total, lax.ppermute(value, axis, pairs))  42 us
    all_gather x1, waiting for transfers between devices, shards(): weight_all = lax.all_gather(weight_piece, 'req', axis=1, tiled=True)  34.6 us
    all_gather x1, waiting for transfers between devices, shards(): lax.all_gather(pieces.reshape(tok_req, q_cols), 'kv', axis=1, tiled=True)  31.7 us
    ppermute x15, starting transfers between devices, direct_gather(): received.append(lax.ppermute(value, axis, pairs))  31.3 us
    ppermute x29, waiting for transfers between devices, direct_reduce(): total = combine(total, lax.ppermute(value, axis, pairs))  24.2 us
    all_gather x1, waiting for transfers between devices, shards(): rows_all = lax.all_gather(owner_rows, 'kv', axis=0, tiled=True)  22.5 us
    all_to_all x1, blocking collectives, regroup(): lax.all_to_all(rows_in, ('req', 'kv'), split_axis=0, concat_axis=0, tiled...  18.2 us
    sub x1, matrix products, prefill_full(): expd = jnp.exp(scores - row_peak)  16.2 us
  transfers between devices with their start and end apart: 50, of which 18 were waited for; matrix products, arithmetic and copies ran while one was open for 21% of the time, Pallas kernels for 0%

profile of v7, /device:TPU:0, one launch (start us, length us, event | category | flops | bytes accessed | tf_op | source)
XLA Modules:
  0.0 382.7 jit_solution(14286350138027126640)
XLA Ops:
  13.6 11.1 %all-to-all-start = ((bf16[128,2,1024]{2,1,0:T(2,128)(2,1)}), bf16[128,2,1024]{2,1,0:T(2,128)(2,1)S(1)}, u32[]{:S(2)}, u32[]{:S(2)}) async-start(bf16[128,2,1024]{2,1,0:T(2,128)(2,1)} %reshape.514), calls=%async_computation | async-start | bytes 1048576 | tf_op jit(solution)/shard_map/all_to_all | solution.py:98
  25.5 12.8 %all-to-all-done = bf16[128,2,1024]{2,1,0:T(2,128)(2,1)S(1)} async-done(((bf16[128,2,1024]{2,1,0:T(2,128)(2,1)}), bf16[128,2,1024]{2,1,0:T(2,128)(2,1)S(1)}, u32[]{:S(2)}, u32[]{:S(2)}) %all-to-all-start) | async-done | bytes 524320 | tf_op jit(solution)/shard_map/all_to_all | solution.py:98
  44.1 5.6 %broadcast_in_dim.46 = bf16[8,256,2048]{2,1,0:T(8,128)(2,1)} broadcast(bf16[256,2048]{1,0:T(8,128)(2,1)} %param.35), dimensions={1,2} | broadcast | bytes 9437184 | tf_op jit(solution)/shard_map/broadcast_in_dim | solution.py:139
  49.7 5.1 %all-to-all-start.1 = ((bf16[8,256,2048]{2,1,0:T(8,128)(2,1)}), bf16[8,256,2048]{2,1,0:T(8,128)(2,1)}, u32[]{:S(2)}, u32[]{:S(2)}) async-start(bf16[8,256,2048]{2,1,0:T(8,128)(2,1)} %broadcast_in_dim.46), calls=%async_computation.1 | async-start | bytes 16777216 | tf_op jit(solution)/shard_map/all_to_all | solution.py:138
  58.9 4.1 %fusion.4 = pred[1016,3064]{1,0:T(8,128)(4,1)} fusion(s32[3064]{0:T(1024)S(1)} %iota_add_fusion, pred[3064]{0:T(1024)(128)(4,1)S(1)} %get-tuple-element.41, pred[3064]{0:T(1024)(128)(4,1)S(1)} %get-tuple-element.42), kind=kLoop, calls=%fused_computation.16 | loop fusion | flops 6226048 | bytes 3131408 | tf_op jit(solution)/shard_map/jit(_where)/select_n | solution.py:45
  63.0 22.5 %all-gather.9.cloned.1.call-done = bf16[1024,2048]{1,0:T(8,128)(2,1)} async-done(((bf16[128,2048]{1,0:T(8,128)(2,1)}), bf16[1024,2048]{1,0:T(8,128)(2,1)}) %all-gather.9.cloned.1.call-update) | async-done | bytes 4194320 | tf_op jit(solution)/shard_map/all_gather | solution.py:136
  85.5 3.2 fusion.10
  92.5 3.7 multiply_reduce_fusion.1
  102.1 3.8 convolution_convert_fusion
  106.7 16.2 %fusion.81 = (f32[2,1016]{1,0:T(2,128)S(1)}, f32[2,1016,3064]{2,1,0:T(8,128)}) fusion(pred[1016,3064]{1,0:T(8,128)(4,1)} %fusion.4, bf16[1016,128]{1,0:T(8,128)(2,1)S(1)} %copy.49, bf16[2048,128]{1,0:T(8,128)(2,1)S(1)} %bitcast.144, bf16[1024,2,64]{2,0,1:T(8,128)(2,1)S(1)} %get-tuple-element.23, bf16[1024,2,64]{2,0,1:T(8,128)(2,1)S(1)} %get-tuple-element.24), kind=kOutput, calls=%fused_computation.180 | convolution fusion | flops 1621384704 | bytes 29334016 | tf_op jit(solution)/shard_map/sub | solution.py:48
  122.9 12.5 %fusion.18 = bf16[1016,2,128]{2,0,1:T(8,128)(2,1)S(1)} fusion(f32[2,1016,3064]{2,1,0:T(8,128)} %get-tuple-element.38, f32[2,1016]{1,0:T(2,128)S(1)} %get-tuple-element.37, bf16[1016,128]{1,0:T(8,128)(2,1)S(1)} %slice.72, bf16[2048,128]{1,0:T(8,128)(2,1)} %bitcast.145), kind=kOutput, calls=%fused_computation.36 | convolution fusion | flops 1608149248 | bytes 26216896 | tf_op jit(solution)/shard_map/gck,kd->cgd/dot_general | solution.py:50
  135.5 34.6 %all-gather.5.cloned.1.call-done = bf16[3,768,2048]{2,1,0:T(8,128)(2,1)} async-done(((bf16[3,48,2048]{2,1,0:T(8,128)(2,1)}), bf16[3,768,2048]{2,1,0:T(8,128)(2,1)}) %all-gather.5.cloned.1.call-update) | async-done | bytes 9437200 | tf_op jit(solution)/shard_map/all_gather | solution.py:150
  170.2 6.7 %slice_bitcast_fusion = (bf16[768,2048]{1,0:T(8,128)(2,1)}, bf16[768,2048]{1,0:T(8,128)(2,1)}, bf16[768,2048]{1,0:T(8,128)(2,1)}) fusion(bf16[3,768,2048]{2,1,0:T(8,128)(2,1)} %all-gather.5.cloned.1.call-done), kind=kLoop, calls=%fused_computation.28 | loop fusion | bytes 18874368 | tf_op jit(solution)/shard_map/squeeze | solution.py:154
  177.9 31.7 %all-gather.7.cloned.1.call-done = bf16[1024,2048]{0,1:T(8,128)(2,1)} async-done(((bf16[1024,256]{0,1:T(8,128)(2,1)}), bf16[1024,2048]{0,1:T(8,128)(2,1)}) %all-gather.7.cloned.1.call-update) | async-done | bytes 4194320 | tf_op jit(solution)/shard_map/all_gather | solution.py:199
  209.7 14.1 %fusion.7 = (f32[1024]{0:T(1024)S(1)}, bf16[1024,2048]{1,0:T(8,128)(2,1)S(1)}) fusion(bf16[1024,2048]{0,1:T(8,128)(2,1)} %all-gather.7.cloned.1.call-done, bf16[2048,2048]{1,0:T(8,128)(2,1)} %bitcast.28, bf16[1024,2048]{1,0:T(8,128)(2,1)} %all-gather.9.cloned.1.call-done), kind=kOutput, calls=%fused_computation.21 | convolution fusion | flops 8602516480 | bytes 20975616 | tf_op jit(solution)/shard_map/dot_general | solution.py:201
  223.9 7.0 %fusion.20 = f32[1024,768]{1,0:T(8,128)S(1)} fusion(bf16[768,2048]{1,0:T(8,128)(2,1)} %get-tuple-element.11, bf16[1024,2048]{1,0:T(8,128)(2,1)S(1)} %get-tuple-element.40, f32[2048]{0:T(1024)S(1)} %copy-done.18, f32[1024]{0:T(1024)S(1)} %add_rsqrt_fusion.1), kind=kOutput, calls=%fused_computation.37 | convolution fusion | flops 3229614080 | bytes 10498048 | tf_op jit(solution)/shard_map/dot_general | solution.py:205
  230.9 3.9 %multiply_convert_fusion = bf16[1024,768]{1,0:T(8,128)(2,1)S(1)} fusion(f32[1024,768]{1,0:T(8,128)S(1)} %fusion.20, bf16[768,2048]{1,0:T(8,128)(2,1)S(1)} %copy-done.7, bf16[1024,2048]{1,0:T(8,128)(2,1)S(1)} %get-tuple-element.40, f32[2048]{0:T(1024)S(1)} %copy-done.18, f32[1024]{0:T(1024)S(1)} %add_rsqrt_fusion.1), kind=kOutput, calls=%fused_computation.31 | convolution fusion | flops 3234332672 | bytes 12070912 | tf_op jit(solution)/shard_map/dot_general | solution.py:206
  234.8 5.8 %fusion.86 = f32[1024,2048]{1,0:T(8,128)} fusion(bf16[1024,768]{1,0:T(8,128)(2,1)S(1)} %multiply_convert_fusion, bf16[768,2048]{1,0:T(8,128)(2,1)S(1)} %copy-done.4), kind=kOutput, calls=%fused_computation.181 | convolution fusion | flops 3221225472 | bytes 13107200 | tf_op jit(solution)/shard_map/dot_general | solution.py:210
  246.9 3.1 collective-permute-start.3
  250.9 3.1 collective-permute-done.4
  254.0 4.7 %collective-permute-done.3 = f32[16,2048]{1,0:T(8,128)S(1)} collective-permute-done((f32[16,2048]{1,0:T(8,128)S(1)}, f32[16,2048]{1,0:T(8,128)S(1)}, u32[]{:S(2)}, u32[]{:S(2)}) %collective-permute-start.3) | collective-permute-done | bytes 131104 | tf_op jit(solution)/shard_map/ppermute | solution.py:81
  259.9 3.7 collective-permute-done.1
  275.9 3.5 collective-permute-start.13
  283.4 3.5 collective-permute-start.16
  286.9 3.2 collective-permute-start.17
  300.3 4.3 %convolution_reduce_fusion = f32[144]{0:T(256)S(1)} fusion(bf16[144,2048]{1,0:T(8,128)(2,1)S(1)} %reshape.464, bf16[2048,1187]{0,1:T(8,128)(2,1)} %param.41), kind=kOutput, calls=%fused_computation.39 | convolution fusion | flops 700291840 | bytes 5452352 | tf_op jit(solution)/shard_map/dot_general | solution.py:217
  315.4 5.1 %collective-permute-start.43 = (f32[144]{0:T(256)S(1)}, f32[144]{0:T(256)S(1)}, u32[]{:S(2)}, u32[]{:S(2)}) collective-permute-start(f32[144]{0:T(256)S(1)} %maximum_maximum_fusion.1), channel_id=1, source_target_pairs={{0,120},{8,0},{16,8},{24,16},{32,24},{40,32},{48,40},{56,48},{64,5... | collective-permute-start | bytes 1736 | tf_op jit(solution)/shard_map/ppermute | solution.py:81
  321.7 4.0 %collective-permute-start.39 = (f32[144]{0:T(256)S(1)}, f32[144]{0:T(256)S(1)}, u32[]{:S(2)}, u32[]{:S(2)}) collective-permute-start(f32[144]{0:T(256)S(1)} %maximum_maximum_fusion.1), channel_id=1, source_target_pairs={{0,88},{8,96},{16,104},{24,112},{32,120},{40,0},{48,8},{56,16},{64... | collective-permute-start | bytes 1736 | tf_op jit(solution)/shard_map/ppermute | solution.py:81
  331.5 3.1 collective-permute-start.35
  338.4 4.0 %collective-permute-start.31 = (f32[144]{0:T(256)S(1)}, f32[144]{0:T(256)S(1)}, u32[]{:S(2)}, u32[]{:S(2)}) collective-permute-start(f32[144]{0:T(256)S(1)} %maximum_maximum_fusion.1), channel_id=1, source_target_pairs={{0,24},{8,32},{16,40},{24,48},{32,56},{40,64},{48,72},{56,80},{64,... | collective-permute-start | bytes 1736 | tf_op jit(solution)/shard_map/ppermute | solution.py:81
  344.8 4.7 %collective-permute-done.30 = f32[144]{0:T(256)S(1)} collective-permute-done((f32[144]{0:T(256)S(1)}, f32[144]{0:T(256)S(1)}, u32[]{:S(2)}, u32[]{:S(2)}) %collective-permute-start.30) | collective-permute-done | bytes 608 | tf_op jit(solution)/shard_map/ppermute | solution.py:81
  354.6 18.2 %all_to_all.29 = bf16[128,2,1024]{2,1,0:T(2,128)(2,1)S(1)} all-to-all(bf16[128,2,1024]{2,1,0:T(2,128)(2,1)S(1)} %reshape.516), channel_id=1, replica_groups=mesh['req'=16,'kv'=8] {'req','kv'}, dimensions={0} | all-to-all | bytes 1048576 | tf_op jit(solution)/shard_map/all_to_all | solution.py:98
  (207 shorter events, 94.2 us)
Async XLA Ops:
  13.6 24.7 %all-to-all-start = ((bf16[128,2,1024]{2,1,0:T(2,128)(2,1)}), bf16[128,2,1024]{2,1,0:T(2,128)(2,1)S(1)}, u32[]{:S(2)}, u32[]{:S(2)}) async-start(bf16[128,2,1024]{2,1,0:T(2,128)(2,1)} %reshape.514), calls=%async_computation | async-start | bytes 1048576 | tf_op jit(solution)/shard_map/all_to_all | solution.py:98
  24.7 60.8 %all-gather.9.cloned.1.call-start = ((), (), s32[]{:S(2)}) async-start(), calls=%async_computation.7 | async-start | bytes 4718592 | tf_op jit(solution)/shard_map/all_gather | solution.py:136
  40.8 129.4 %all-gather.5.cloned.1.call-start = ((), (), s32[]{:S(2)}) async-start(), calls=%async_computation.4 | async-start | bytes 10027008 | tf_op jit(solution)/shard_map/all_gather | solution.py:150
  49.7 127.1 %all-to-all-start.1 = ((bf16[8,256,2048]{2,1,0:T(8,128)(2,1)}), bf16[8,256,2048]{2,1,0:T(8,128)(2,1)}, u32[]{:S(2)}, u32[]{:S(2)}) async-start(bf16[8,256,2048]{2,1,0:T(8,128)(2,1)} %broadcast_in_dim.46), calls=%async_computation.1 | async-start | bytes 16777216 | tf_op jit(solution)/shard_map/all_to_all | solution.py:138
  54.8 154.9 %all-gather.7.cloned.1.call-start = ((), (), s32[]{:S(2)}) async-start(), calls=%async_computation.5 | async-start | bytes 4718592 | tf_op jit(solution)/shard_map/all_gather | solution.py:199
  177.9 173.0 %reduce-scatter.2.cloned.1.call-start = ((), (), s32[]{:S(2)}) async-start(), calls=%async_computation.6 | async-start | bytes 9437184 | tf_op jit(solution)/shard_map/reduce_scatter | solution.py:211
  245.2 8.9 %collective-permute-start.4 = (f32[16,2048]{1,0:T(8,128)S(1)}, f32[16,2048]{1,0:T(8,128)S(1)}, u32[]{:S(2)}, u32[]{:S(2)}) collective-permute-start(f32[16,2048]{1,0:T(8,128)S(1)} %fusion.54), channel_id=1, source_target_pairs={{0,5},{1,6},{2,7},{3,0},{4,1},{5,2},{6,3},{7,4},{8,13},{9,14},{10,... | collective-permute-start | bytes 393224 | tf_op jit(solution)/shard_map/ppermute | solution.py:81
  246.9 11.8 %collective-permute-start.3 = (f32[16,2048]{1,0:T(8,128)S(1)}, f32[16,2048]{1,0:T(8,128)S(1)}, u32[]{:S(2)}, u32[]{:S(2)}) collective-permute-start(f32[16,2048]{1,0:T(8,128)S(1)} %fusion.54), channel_id=1, source_target_pairs={{0,4},{1,5},{2,6},{3,7},{4,0},{5,1},{6,2},{7,3},{8,12},{9,13},{10,... | collective-permute-start | bytes 393224 | tf_op jit(solution)/shard_map/ppermute | solution.py:81
  250.0 9.9 %collective-permute-start.2 = (f32[16,2048]{1,0:T(8,128)S(1)}, f32[16,2048]{1,0:T(8,128)S(1)}, u32[]{:S(2)}, u32[]{:S(2)}) collective-permute-start(f32[16,2048]{1,0:T(8,128)S(1)} %fusion.54), channel_id=1, source_target_pairs={{0,3},{1,4},{2,5},{3,6},{4,7},{5,0},{6,1},{7,2},{8,11},{9,12},{10,... | collective-permute-start | bytes 393224 | tf_op jit(solution)/shard_map/ppermute | solution.py:81
  250.0 13.6 %collective-permute-start.1 = (f32[16,2048]{1,0:T(8,128)S(1)}, f32[16,2048]{1,0:T(8,128)S(1)}, u32[]{:S(2)}, u32[]{:S(2)}) collective-permute-start(f32[16,2048]{1,0:T(8,128)S(1)} %fusion.54), channel_id=1, source_target_pairs={{0,2},{1,3},{2,4},{3,5},{4,6},{5,7},{6,0},{7,1},{8,10},{9,11},{10,... | collective-permute-start | bytes 393224 | tf_op jit(solution)/shard_map/ppermute | solution.py:81
  264.8 9.6 %collective-permute-start.7 = (bf16[9,2048]{1,0:T(8,128)(2,1)S(1)}, bf16[9,2048]{1,0:T(8,128)(2,1)S(1)}, u32[]{:S(2)}, u32[]{:S(2)}) collective-permute-start(bf16[9,2048]{1,0:T(8,128)(2,1)S(1)} %get-tuple-element.17), channel_id=1, source_target_pairs={{0,8},{8,16},{16,24},{24,32},{32,40},{40,48},{48,56},{56,64},{64,7... | collective-permute-start | bytes 110600 | tf_op jit(solution)/shard_map/ppermute | solution.py:91
  266.3 9.5 %collective-permute-start.8 = (bf16[9,2048]{1,0:T(8,128)(2,1)S(1)}, bf16[9,2048]{1,0:T(8,128)(2,1)S(1)}, u32[]{:S(2)}, u32[]{:S(2)}) collective-permute-start(bf16[9,2048]{1,0:T(8,128)(2,1)S(1)} %get-tuple-element.17), channel_id=1, source_target_pairs={{0,16},{8,24},{16,32},{24,40},{32,48},{40,56},{48,64},{56,72},{64,... | collective-permute-start | bytes 110600 | tf_op jit(solution)/shard_map/ppermute | solution.py:91
  269.1 10.3 %collective-permute-start.9 = (bf16[9,2048]{1,0:T(8,128)(2,1)S(1)}, bf16[9,2048]{1,0:T(8,128)(2,1)S(1)}, u32[]{:S(2)}, u32[]{:S(2)}) collective-permute-start(bf16[9,2048]{1,0:T(8,128)(2,1)S(1)} %get-tuple-element.17), channel_id=1, source_target_pairs={{0,24},{8,32},{16,40},{24,48},{32,56},{40,64},{48,72},{56,80},{64,... | collective-permute-start | bytes 110600 | tf_op jit(solution)/shard_map/ppermute | solution.py:91
  271.5 9.9 %collective-permute-start.10 = (bf16[9,2048]{1,0:T(8,128)(2,1)S(1)}, bf16[9,2048]{1,0:T(8,128)(2,1)S(1)}, u32[]{:S(2)}, u32[]{:S(2)}) collective-permute-start(bf16[9,2048]{1,0:T(8,128)(2,1)S(1)} %get-tuple-element.17), channel_id=1, source_target_pairs={{0,32},{8,40},{16,48},{24,56},{32,64},{40,72},{48,80},{56,88},{64,... | collective-permute-start | bytes 110600 | tf_op jit(solution)/shard_map/ppermute | solution.py:91
  273.0 10.4 %collective-permute-start.11 = (bf16[9,2048]{1,0:T(8,128)(2,1)S(1)}, bf16[9,2048]{1,0:T(8,128)(2,1)S(1)}, u32[]{:S(2)}, u32[]{:S(2)}) collective-permute-start(bf16[9,2048]{1,0:T(8,128)(2,1)S(1)} %get-tuple-element.17), channel_id=1, source_target_pairs={{0,40},{8,48},{16,56},{24,64},{32,72},{40,80},{48,88},{56,96},{64,... | collective-permute-start | bytes 110600 | tf_op jit(solution)/shard_map/ppermute | solution.py:91
  274.3 12.6 %collective-permute-start.12 = (bf16[9,2048]{1,0:T(8,128)(2,1)S(1)}, bf16[9,2048]{1,0:T(8,128)(2,1)S(1)}, u32[]{:S(2)}, u32[]{:S(2)}) collective-permute-start(bf16[9,2048]{1,0:T(8,128)(2,1)S(1)} %get-tuple-element.17), channel_id=1, source_target_pairs={{0,48},{8,56},{16,64},{24,72},{32,80},{40,88},{48,96},{56,104},{64... | collective-permute-start | bytes 110600 | tf_op jit(solution)/shard_map/ppermute | solution.py:91
  275.9 14.3 %collective-permute-start.13 = (bf16[9,2048]{1,0:T(8,128)(2,1)S(1)}, bf16[9,2048]{1,0:T(8,128)(2,1)S(1)}, u32[]{:S(2)}, u32[]{:S(2)}) collective-permute-start(bf16[9,2048]{1,0:T(8,128)(2,1)S(1)} %get-tuple-element.17), channel_id=1, source_target_pairs={{0,56},{8,64},{16,72},{24,80},{32,88},{40,96},{48,104},{56,112},{6... | collective-permute-start | bytes 110600 | tf_op jit(solution)/shard_map/ppermute | solution.py:91
  279.4 13.2 %collective-permute-start.14 = (bf16[9,2048]{1,0:T(8,128)(2,1)S(1)}, bf16[9,2048]{1,0:T(8,128)(2,1)S(1)}, u32[]{:S(2)}, u32[]{:S(2)}) collective-permute-start(bf16[9,2048]{1,0:T(8,128)(2,1)S(1)} %get-tuple-element.17), channel_id=1, source_target_pairs={{0,64},{8,72},{16,80},{24,88},{32,96},{40,104},{48,112},{56,120},{... | collective-permute-start | bytes 110600 | tf_op jit(solution)/shard_map/ppermute | solution.py:91
  281.4 11.3 %collective-permute-start.15 = (bf16[9,2048]{1,0:T(8,128)(2,1)S(1)}, bf16[9,2048]{1,0:T(8,128)(2,1)S(1)}, u32[]{:S(2)}, u32[]{:S(2)}) collective-permute-start(bf16[9,2048]{1,0:T(8,128)(2,1)S(1)} %get-tuple-element.17), channel_id=1, source_target_pairs={{0,72},{8,80},{16,88},{24,96},{32,104},{40,112},{48,120},{56,0},{6... | collective-permute-start | bytes 110600 | tf_op jit(solution)/shard_map/ppermute | solution.py:91
  283.4 10.2 %collective-permute-start.16 = (bf16[9,2048]{1,0:T(8,128)(2,1)S(1)}, bf16[9,2048]{1,0:T(8,128)(2,1)S(1)}, u32[]{:S(2)}, u32[]{:S(2)}) collective-permute-start(bf16[9,2048]{1,0:T(8,128)(2,1)S(1)} %get-tuple-element.17), channel_id=1, source_target_pairs={{0,80},{8,88},{16,96},{24,104},{32,112},{40,120},{48,0},{56,8},{64... | collective-permute-start | bytes 110600 | tf_op jit(solution)/shard_map/ppermute | solution.py:91
  286.9 9.3 %collective-permute-start.17 = (bf16[9,2048]{1,0:T(8,128)(2,1)S(1)}, bf16[9,2048]{1,0:T(8,128)(2,1)S(1)}, u32[]{:S(2)}, u32[]{:S(2)}) collective-permute-start(bf16[9,2048]{1,0:T(8,128)(2,1)S(1)} %get-tuple-element.17), channel_id=1, source_target_pairs={{0,88},{8,96},{16,104},{24,112},{32,120},{40,0},{48,8},{56,16},{64... | collective-permute-start | bytes 110600 | tf_op jit(solution)/shard_map/ppermute | solution.py:91
  315.4 10.3 %collective-permute-start.43 = (f32[144]{0:T(256)S(1)}, f32[144]{0:T(256)S(1)}, u32[]{:S(2)}, u32[]{:S(2)}) collective-permute-start(f32[144]{0:T(256)S(1)} %maximum_maximum_fusion.1), channel_id=1, source_target_pairs={{0,120},{8,0},{16,8},{24,16},{32,24},{40,32},{48,40},{56,48},{64,5... | collective-permute-start | bytes 1736 | tf_op jit(solution)/shard_map/ppermute | solution.py:81
  320.6 8.0 %collective-permute-start.42 = (f32[144]{0:T(256)S(1)}, f32[144]{0:T(256)S(1)}, u32[]{:S(2)}, u32[]{:S(2)}) collective-permute-start(f32[144]{0:T(256)S(1)} %maximum_maximum_fusion.1), channel_id=1, source_target_pairs={{0,112},{8,120},{16,0},{24,8},{32,16},{40,24},{48,32},{56,40},{64,... | collective-permute-start | bytes 1736 | tf_op jit(solution)/shard_map/ppermute | solution.py:81
  320.6 8.6 %collective-permute-start.41 = (f32[144]{0:T(256)S(1)}, f32[144]{0:T(256)S(1)}, u32[]{:S(2)}, u32[]{:S(2)}) collective-permute-start(f32[144]{0:T(256)S(1)} %maximum_maximum_fusion.1), channel_id=1, source_target_pairs={{0,104},{8,112},{16,120},{24,0},{32,8},{40,16},{48,24},{56,32},{64... | collective-permute-start | bytes 1736 | tf_op jit(solution)/shard_map/ppermute | solution.py:81
  320.6 10.9 %collective-permute-start.40 = (f32[144]{0:T(256)S(1)}, f32[144]{0:T(256)S(1)}, u32[]{:S(2)}, u32[]{:S(2)}) collective-permute-start(f32[144]{0:T(256)S(1)} %maximum_maximum_fusion.1), channel_id=1, source_target_pairs={{0,96},{8,104},{16,112},{24,120},{32,0},{40,8},{48,16},{56,24},{64... | collective-permute-start | bytes 1736 | tf_op jit(solution)/shard_map/ppermute | solution.py:81
  321.7 12.9 %collective-permute-start.39 = (f32[144]{0:T(256)S(1)}, f32[144]{0:T(256)S(1)}, u32[]{:S(2)}, u32[]{:S(2)}) collective-permute-start(f32[144]{0:T(256)S(1)} %maximum_maximum_fusion.1), channel_id=1, source_target_pairs={{0,88},{8,96},{16,104},{24,112},{32,120},{40,0},{48,8},{56,16},{64... | collective-permute-start | bytes 1736 | tf_op jit(solution)/shard_map/ppermute | solution.py:81
  325.7 9.6 %collective-permute-start.38 = (f32[144]{0:T(256)S(1)}, f32[144]{0:T(256)S(1)}, u32[]{:S(2)}, u32[]{:S(2)}) collective-permute-start(f32[144]{0:T(256)S(1)} %maximum_maximum_fusion.1), channel_id=1, source_target_pairs={{0,80},{8,88},{16,96},{24,104},{32,112},{40,120},{48,0},{56,8},{64... | collective-permute-start | bytes 1736 | tf_op jit(solution)/shard_map/ppermute | solution.py:81
  328.5 8.3 %collective-permute-start.37 = (f32[144]{0:T(256)S(1)}, f32[144]{0:T(256)S(1)}, u32[]{:S(2)}, u32[]{:S(2)}) collective-permute-start(f32[144]{0:T(256)S(1)} %maximum_maximum_fusion.1), channel_id=1, source_target_pairs={{0,72},{8,80},{16,88},{24,96},{32,104},{40,112},{48,120},{56,0},{6... | collective-permute-start | bytes 1736 | tf_op jit(solution)/shard_map/ppermute | solution.py:81
  329.1 9.2 %collective-permute-start.36 = (f32[144]{0:T(256)S(1)}, f32[144]{0:T(256)S(1)}, u32[]{:S(2)}, u32[]{:S(2)}) collective-permute-start(f32[144]{0:T(256)S(1)} %maximum_maximum_fusion.1), channel_id=1, source_target_pairs={{0,64},{8,72},{16,80},{24,88},{32,96},{40,104},{48,112},{56,120},{... | collective-permute-start | bytes 1736 | tf_op jit(solution)/shard_map/ppermute | solution.py:81
  331.5 10.9 %collective-permute-start.35 = (f32[144]{0:T(256)S(1)}, f32[144]{0:T(256)S(1)}, u32[]{:S(2)}, u32[]{:S(2)}) collective-permute-start(f32[144]{0:T(256)S(1)} %maximum_maximum_fusion.1), channel_id=1, source_target_pairs={{0,56},{8,64},{16,72},{24,80},{32,88},{40,96},{48,104},{56,112},{6... | collective-permute-start | bytes 1736 | tf_op jit(solution)/shard_map/ppermute | solution.py:81
  334.6 8.9 %collective-permute-start.34 = (f32[144]{0:T(256)S(1)}, f32[144]{0:T(256)S(1)}, u32[]{:S(2)}, u32[]{:S(2)}) collective-permute-start(f32[144]{0:T(256)S(1)} %maximum_maximum_fusion.1), channel_id=1, source_target_pairs={{0,48},{8,56},{16,64},{24,72},{32,80},{40,88},{48,96},{56,104},{64... | collective-permute-start | bytes 1736 | tf_op jit(solution)/shard_map/ppermute | solution.py:81
  335.4 8.1 %collective-permute-start.33 = (f32[144]{0:T(256)S(1)}, f32[144]{0:T(256)S(1)}, u32[]{:S(2)}, u32[]{:S(2)}) collective-permute-start(f32[144]{0:T(256)S(1)} %maximum_maximum_fusion.1), channel_id=1, source_target_pairs={{0,40},{8,48},{16,56},{24,64},{32,72},{40,80},{48,88},{56,96},{64,... | collective-permute-start | bytes 1736 | tf_op jit(solution)/shard_map/ppermute | solution.py:81
  (37 other events, 327.0 us)
Sparse Core Ops, SparseCore 0:
  40.9 44.5 all-gather.8
  87.7 82.4 all-gather.4
  178.0 31.6 all-gather.6
  240.8 60.6 reduce-scatter.1

commit v8 on v6

--- a/solution.py
+++ b/solution.py
@@ -139,9 +139,10 @@
     owner_rows = arrived[slot_place]
     rows_all = lax.all_gather(owner_rows, "kv", axis=0, tiled=True)
     normed = norm_rows(rows_all, attn_gain).astype(jnp.bfloat16)
+    o_local, rows_all = lax.optimization_barrier((o_proj, rows_all))
     o_full = lax.all_to_all(
-        jnp.broadcast_to(o_proj[None], (kv_count,) + o_proj.shape), "kv", split_axis=0, concat_axis=0, tiled=True
-    ).reshape(kv_count * o_proj.shape[0], o_proj.shape[1])
+        jnp.broadcast_to(o_local[None], (kv_count,) + o_proj.shape), "kv", split_axis=0, concat_axis=0, tiled=True
+    ).reshape(kv_count * o_local.shape[0], o_local.shape[1])
     ff_dev = w_gate.shape[1]
     ff_piece = ff_dev // kv_count
     weight_piece = jnp.stack(
@@ -153,9 +154,6 @@
     )
     weight_all = lax.all_gather(weight_piece, "req", axis=1, tiled=True)
     model_dim = w_gate.shape[0]
-    gate_w = weight_all[0]
-    up_w = weight_all[1]
-    down_w = weight_all[2]
     q_cols = q_proj.shape[1]
     kv_cols = k_proj.shape[1]
     projected = jnp.concatenate(
@@ -199,7 +197,10 @@
         cache_len,
     )
     pieces = jnp.concatenate([pre_out, dec_out], axis=0)
-    pieces, gate_w, up_w, down_w, o_full = lax.optimization_barrier((pieces, gate_w, up_w, down_w, o_full))
+    pieces, weight_all, o_full = lax.optimization_barrier((pieces, weight_all, o_full))
+    gate_w = weight_all[0]
+    up_w = weight_all[1]
+    down_w = weight_all[2]
     attended = lax.all_gather(pieces.reshape(tok_req, q_cols), "kv", axis=1, tiled=True)
     resid = (
         rows_all.astype(jnp.float32) + jnp.dot(attended, o_full, preferred_element_type=jnp.float32)

time: 359 us -> 369 us (1.028)
  waiting for transfers between devices: 144 us -> 163 us
  local copies, waits for them, and re-layouts: 27.6 us -> 22.5 us
    all_to_all x1, waiting for transfers between devices: 0.01 us -> 57.7 us  [shards(): lax.all_to_all(jnp.broadcast_to(o_local[None], (kv_count,) + o_proj.shape...]
    all_gather x1, waiting for transfers between devices: 34.8 us -> 0.01 us  [shards(): weight_all = lax.all_gather(weight_piece, 'req', axis=1, tiled=True)]
    squeeze x1 -> x0, local copies, waits for them, and re-layouts: 6.62 us -> none  [shards(): down_w = weight_all[2]]
    all_gather x1, waiting for transfers between devices: 22.5 us -> 18 us  [shards(): rows_all = lax.all_gather(owner_rows, 'kv', axis=0, tiled=True)]
  transfers between devices with their start and end apart: 20 -> 20, of which waited for: 18 -> 18; matrix products, arithmetic and copies ran while one was open for 23% -> 20% of each run, Pallas kernels for 0% -> 0%
where the time goes in v8:
time: 369 us; the launch traced here: 365 us
  waiting for transfers between devices  163 us (44%)
  matrix products  77.6 us (21%)
  starting transfers between devices  41.7 us (11%)
  blocking collectives  22.9 us (6%)
  local copies, waits for them, and re-layouts  22.5 us (6%)
  other arithmetic  22 us (6%)
  between operations  15.1 us (4%)
    all_to_all x1, waiting for transfers between devices, shards(): lax.all_to_all(jnp.broadcast_to(o_local[None], (kv_count,) + o_proj.shape...  57.7 us
    all_gather x1, waiting for transfers between devices, shards(): lax.all_gather(pieces.reshape(tok_req, q_cols), 'kv', axis=1, tiled=True)  31.6 us
    ppermute x10, waiting for transfers between devices, butterfly(): value = combine(value, lax.ppermute(value, axis, pairs))  28.4 us
    all_to_all x1, blocking collectives, regroup(): lax.all_to_all(rows_in, ('req', 'kv'), split_axis=0, concat_axis=0, tiled...  22.9 us
    all_gather x1, waiting for transfers between devices, shards(): rows_all = lax.all_gather(owner_rows, 'kv', axis=0, tiled=True)  18 us
    sub x1, matrix products, prefill_full(): expd = jnp.exp(scores - row_peak)  15.9 us
    ppermute x10, starting transfers between devices, butterfly(): value = combine(value, lax.ppermute(value, axis, pairs))  14.8 us
    dot_general x1, matrix products, shards(): jnp.dot(attended, o_full, preferred_element_type=jnp.float32)  14.5 us
  transfers between devices with their start and end apart: 20, of which 18 were waited for; matrix products, arithmetic and copies ran while one was open for 20% of the time, Pallas kernels for 0%

profile of v8, /device:TPU:0, one launch (start us, length us, event | category | flops | bytes accessed | tf_op | source)
XLA Modules:
  0.0 364.8 jit_solution(4169541533971957055)
XLA Ops:
  8.3 2.6 gather_fusion
  13.4 11.1 %all-to-all-start = ((bf16[128,2,1024]{2,1,0:T(2,128)(2,1)}), bf16[128,2,1024]{2,1,0:T(2,128)(2,1)S(1)}, u32[]{:S(2)}, u32[]{:S(2)}) async-start(bf16[128,2,1024]{2,1,0:T(2,128)(2,1)} %reshape.453), calls=%async_computation | async-start | bytes 1048576 | tf_op jit(solution)/shard_map/all_to_all | solution.py:102
  25.3 12.8 %all-to-all-done = bf16[128,2,1024]{2,1,0:T(2,128)(2,1)S(1)} async-done(((bf16[128,2,1024]{2,1,0:T(2,128)(2,1)}), bf16[128,2,1024]{2,1,0:T(2,128)(2,1)S(1)}, u32[]{:S(2)}, u32[]{:S(2)}) %all-to-all-start) | async-done | bytes 524320 | tf_op jit(solution)/shard_map/all_to_all | solution.py:102
  46.9 4.1 %fusion.4 = pred[1016,3064]{1,0:T(8,128)(4,1)} fusion(s32[3064]{0:T(1024)S(1)} %iota_add_fusion, pred[3064]{0:T(1024)(128)(4,1)S(1)} %get-tuple-element.44, pred[3064]{0:T(1024)(128)(4,1)S(1)} %get-tuple-element.45), kind=kLoop, calls=%fused_computation.12 | loop fusion | flops 6226048 | bytes 3131408 | tf_op jit(solution)/shard_map/jit(_where)/select_n | solution.py:45
  50.9 18.0 %all-gather.9.cloned.1.call-done = bf16[1024,2048]{1,0:T(8,128)(2,1)} async-done(((bf16[128,2048]{1,0:T(8,128)(2,1)}), bf16[1024,2048]{1,0:T(8,128)(2,1)}) %all-gather.9.cloned.1.call-update) | async-done | bytes 4194320 | tf_op jit(solution)/shard_map/all_gather | solution.py:140
  68.9 3.2 fusion.7
  77.5 3.7 %multiply_reduce_fusion.1 = (f32[1024]{0:T(1024)S(1)}, f32[1024,128]{0,1:T(8,128)S(1)}) fusion(bf16[1024,2048]{1,0:T(8,128)(2,1)} %copy-done.3, bf16[2048,128]{1,0:T(8,128)(2,1)S(1)} %copy-done.6), kind=kOutput, calls=%fused_computation.71 | convolution fusion | flops 537132032 | bytes 5246976 | tf_op jit(solution)/shard_map/dot_general | solution.py:162
  82.6 5.6 %broadcast_in_dim.46 = bf16[8,256,2048]{2,1,0:T(8,128)(2,1)} broadcast(bf16[256,2048]{1,0:T(8,128)(2,1)} %param.35), dimensions={1,2} | broadcast | bytes 9437184 | tf_op jit(solution)/shard_map/broadcast_in_dim | solution.py:144
  88.3 5.1 %all-to-all-start.1 = ((bf16[8,256,2048]{2,1,0:T(8,128)(2,1)}), bf16[8,256,2048]{2,1,0:T(8,128)(2,1)}, u32[]{:S(2)}, u32[]{:S(2)}) async-start(bf16[8,256,2048]{2,1,0:T(8,128)(2,1)} %broadcast_in_dim.46), calls=%async_computation.1 | async-start | bytes 16777216 | tf_op jit(solution)/shard_map/all_to_all | solution.py:143
  97.8 3.6 convolution_convert_fusion
  102.3 15.9 %fusion.93 = (f32[2,1016]{1,0:T(2,128)S(1)}, f32[2,1016,3064]{2,1,0:T(8,128)}) fusion(pred[1016,3064]{1,0:T(8,128)(4,1)} %fusion.4, bf16[1016,128]{1,0:T(8,128)(2,1)S(1)} %copy.49, bf16[2048,128]{1,0:T(8,128)(2,1)S(1)} %bitcast.114, bf16[1024,2,64]{2,0,1:T(8,128)(2,1)S(1)} %get-tuple-element.18, bf16[1024,2,64]{2,0,1:T(8,128)(2,1)S(1)} %get-tuple-element.19), kind=kOutput, calls=%fused_computation.170 | convolution fusion | flops 1621384704 | bytes 29334016 | tf_op jit(solution)/shard_map/sub | solution.py:48
  118.1 12.1 %fusion.31 = bf16[1016,2,128]{2,0,1:T(8,128)(2,1)S(1)} fusion(f32[2,1016,3064]{2,1,0:T(8,128)} %get-tuple-element.41, f32[2,1016]{1,0:T(2,128)S(1)} %get-tuple-element.40, bf16[1016,128]{1,0:T(8,128)(2,1)S(1)} %slice.70, bf16[2048,128]{1,0:T(8,128)(2,1)S(1)} %bitcast.115), kind=kOutput, calls=%fused_computation.43 | convolution fusion | flops 1608149248 | bytes 26216896 | tf_op jit(solution)/shard_map/gck,kd->cgd/dot_general | solution.py:50
  130.3 57.7 %all-to-all-done.1 = bf16[8,256,2048]{2,1,0:T(8,128)(2,1)} async-done(((bf16[8,256,2048]{2,1,0:T(8,128)(2,1)}), bf16[8,256,2048]{2,1,0:T(8,128)(2,1)}, u32[]{:S(2)}, u32[]{:S(2)}) %all-to-all-start.1) | async-done | bytes 8388640 | tf_op jit(solution)/shard_map/all_to_all | solution.py:143
  189.1 31.6 %all-gather.7.cloned.1.call-done = bf16[1024,2048]{0,1:T(8,128)(2,1)} async-done(((bf16[1024,256]{0,1:T(8,128)(2,1)}), bf16[1024,2048]{0,1:T(8,128)(2,1)}) %all-gather.7.cloned.1.call-update) | async-done | bytes 4194320 | tf_op jit(solution)/shard_map/all_gather | solution.py:204
  220.7 14.5 %fusion.10 = (f32[1024]{0:T(1024)S(1)}, bf16[1024,2048]{1,0:T(8,128)(2,1)S(1)}) fusion(bf16[1024,2048]{0,1:T(8,128)(2,1)} %all-gather.7.cloned.1.call-done, bf16[2048,2048]{1,0:T(8,128)(2,1)} %bitcast.25, bf16[1024,2048]{1,0:T(8,128)(2,1)} %all-gather.9.cloned.1.call-done), kind=kOutput, calls=%fused_computation.22 | convolution fusion | flops 8602516480 | bytes 20975616 | tf_op jit(solution)/shard_map/dot_general | solution.py:206
  235.3 7.0 %fusion.17 = f32[1024,768]{1,0:T(8,128)S(1)} fusion(bf16[3,768,2048]{2,1,0:T(8,128)(2,1)} %all-gather.5.cloned.1.call-done, bf16[1024,2048]{1,0:T(8,128)(2,1)S(1)} %get-tuple-element.43, f32[2048]{0:T(1024)S(1)} %copy-done.17, f32[1024]{0:T(1024)S(1)} %add_rsqrt_fusion.1), kind=kOutput, calls=%fused_computation.30 | convolution fusion | flops 3229614080 | bytes 10498048 | tf_op jit(solution)/shard_map/dot_general | solution.py:211
  242.4 3.9 %multiply_convert_fusion = bf16[1024,768]{1,0:T(8,128)(2,1)S(1)} fusion(f32[1024,768]{1,0:T(8,128)S(1)} %fusion.17, bf16[3,768,2048]{2,1,0:T(8,128)(2,1)S(1)} %bitcast.107, bf16[1024,2048]{1,0:T(8,128)(2,1)S(1)} %get-tuple-element.43, f32[2048]{0:T(1024)S(1)} %copy-done.17, f32[1024]{0:T(1024)S(1)} %add_rsqrt_fusion.1), kind=kOutput, calls=%fused_computation.34 | convolution fusion | flops 3234332672 | bytes 12070912 | tf_op jit(solution)/shard_map/dot_general | solution.py:210
  246.3 5.7 %fusion.15 = f32[1024,2048]{1,0:T(8,128)} fusion(bf16[1024,768]{1,0:T(8,128)(2,1)S(1)} %multiply_convert_fusion, bf16[3,768,2048]{2,1,0:T(8,128)(2,1)S(1)} %bitcast.107), kind=kOutput, calls=%fused_computation.28 | convolution fusion | flops 3221225472 | bytes 13107200 | tf_op jit(solution)/shard_map/dot_general | solution.py:215
  256.5 5.2 %collective-permute-done.1 = f32[16,2048]{1,0:T(8,128)S(1)} collective-permute-done((f32[16,2048]{1,0:T(8,128)S(1)}, f32[16,2048]{1,0:T(8,128)S(1)}, u32[]{:S(2)}, u32[]{:S(2)}) %collective-permute-start.1) | collective-permute-done | bytes 131104 | tf_op jit(solution)/shard_map/ppermute | solution.py:81
  263.5 6.8 %collective-permute-done.2 = f32[16,2048]{1,0:T(8,128)S(1)} collective-permute-done((f32[16,2048]{1,0:T(8,128)S(1)}, f32[16,2048]{1,0:T(8,128)S(1)}, u32[]{:S(2)}, u32[]{:S(2)}) %collective-permute-start.2) | collective-permute-done | bytes 131104 | tf_op jit(solution)/shard_map/ppermute | solution.py:81
  273.0 2.8 collective-permute-done.3
  275.9 3.1 collective-permute-start.4
  279.0 3.1 collective-permute-done.4
  283.8 3.8 %collective-permute-done.5 = bf16[36,2048]{1,0:T(8,128)(2,1)S(1)} collective-permute-done((bf16[36,2048]{1,0:T(8,128)(2,1)S(1)}, bf16[36,2048]{1,0:T(8,128)(2,1)S(1)}, u32[]{:S(2)}, u32[]{:S(2)}) %collective-permute-start.5) | collective-permute-done | bytes 147488 | tf_op jit(solution)/shard_map/ppermute | solution.py:92
  287.8 3.9 %collective-permute-start.6 = (bf16[72,2048]{1,0:T(8,128)(2,1)S(1)}, bf16[72,2048]{1,0:T(8,128)(2,1)S(1)}, u32[]{:S(2)}, u32[]{:S(2)}) collective-permute-start(bf16[72,2048]{1,0:T(8,128)(2,1)S(1)} %pad_maximum_fusion.2), channel_id=1, source_target_pairs={{0,64},{8,72},{16,80},{24,88},{32,96},{40,104},{48,112},{56,120},{... | collective-permute-start | bytes 884744 | tf_op jit(solution)/shard_map/ppermute | solution.py:92
  291.7 4.7 %collective-permute-done.6 = bf16[72,2048]{1,0:T(8,128)(2,1)S(1)} collective-permute-done((bf16[72,2048]{1,0:T(8,128)(2,1)S(1)}, bf16[72,2048]{1,0:T(8,128)(2,1)S(1)}, u32[]{:S(2)}, u32[]{:S(2)}) %collective-permute-start.6) | collective-permute-done | bytes 294944 | tf_op jit(solution)/shard_map/ppermute | solution.py:92
  296.5 4.3 %convolution_reduce_fusion = f32[144]{0:T(256)S(1)} fusion(bf16[2048,1187]{0,1:T(8,128)(2,1)} %param.41, bf16[72,2048]{1,0:T(8,128)(2,1)S(1)} %get-tuple-element.21, bf16[72,2048]{1,0:T(8,128)(2,1)S(1)} %get-tuple-element.20), kind=kOutput, calls=%fused_computation.45 | convolution fusion | flops 701471488 | bytes 5452352 | tf_op jit(solution)/shard_map/dot_general | solution.py:222
  302.4 3.2 collective-permute-done.8
  307.4 3.2 collective-permute-done.9
  314.2 2.9 collective-permute-start.11
  322.9 3.7 %collective-permute-start.13 = (f32[144]{0:T(256)S(1)}, f32[144]{0:T(256)S(1)}, u32[]{:S(2)}, u32[]{:S(2)}) collective-permute-start(f32[144]{0:T(256)S(1)} %max.30), channel_id=1, source_target_pairs={{0,64},{8,72},{16,80},{24,88},{32,96},{40,104},{48,112},{56,120},{... | collective-permute-start | bytes 1736 | tf_op jit(solution)/shard_map/ppermute | solution.py:81
  332.3 22.9 %all_to_all.29 = bf16[128,2,1024]{2,1,0:T(2,128)(2,1)S(1)} all-to-all(bf16[128,2,1024]{2,1,0:T(2,128)(2,1)S(1)} %reshape.455), channel_id=1, replica_groups=mesh['req'=16,'kv'=8] {'req','kv'}, dimensions={0} | all-to-all | bytes 1048576 | tf_op jit(solution)/shard_map/all_to_all | solution.py:102
  (145 shorter events, 57.9 us)
Async XLA Ops:
  7.2 36.0 %copy-start = (bf16[384,2048]{1,0:T(8,128)(2,1)S(1)}, bf16[384,2048]{1,0:T(8,128)(2,1)}, u32[]{:S(2)}) copy-start(bf16[384,2048]{1,0:T(8,128)(2,1)} %param.39) | copy-start | bytes 4718596
  13.4 24.7 %all-to-all-start = ((bf16[128,2,1024]{2,1,0:T(2,128)(2,1)}), bf16[128,2,1024]{2,1,0:T(2,128)(2,1)S(1)}, u32[]{:S(2)}, u32[]{:S(2)}) async-start(bf16[128,2,1024]{2,1,0:T(2,128)(2,1)} %reshape.453), calls=%async_computation | async-start | bytes 1048576 | tf_op jit(solution)/shard_map/all_to_all | solution.py:102
  24.5 44.3 %all-gather.9.cloned.1.call-start = ((), (), s32[]{:S(2)}) async-start(), calls=%async_computation.7 | async-start | bytes 4718592 | tf_op jit(solution)/shard_map/all_gather | solution.py:140
  40.6 147.4 %all-gather.5.cloned.1.call-start = ((), (), s32[]{:S(2)}) async-start(), calls=%async_computation.4 | async-start | bytes 10027008 | tf_op jit(solution)/shard_map/all_gather | solution.py:155
  44.9 27.2 %copy-start.9 = (f32[2048]{0:T(1024)S(1)}, f32[2048]{0:T(1024)}, u32[]{:S(2)}) copy-start(f32[2048]{0:T(1024)} %param.29) | copy-start | bytes 24580
  75.9 5.3 %copy-start.11 = (f32[128]{0:T(128)S(1)}, f32[128]{0:T(128)}, u32[]{:S(2)}) copy-start(f32[128]{0:T(128)} %param.34) | copy-start | bytes 1540
  88.3 5.4 %copy-start.12 = (f32[128]{0:T(128)S(1)}, f32[128]{0:T(128)}, u32[]{:S(2)}) copy-start(f32[128]{0:T(128)} %param.33) | copy-start | bytes 1540
  88.3 99.7 %all-to-all-start.1 = ((bf16[8,256,2048]{2,1,0:T(8,128)(2,1)}), bf16[8,256,2048]{2,1,0:T(8,128)(2,1)}, u32[]{:S(2)}, u32[]{:S(2)}) async-start(bf16[8,256,2048]{2,1,0:T(8,128)(2,1)} %broadcast_in_dim.46), calls=%async_computation.1 | async-start | bytes 16777216 | tf_op jit(solution)/shard_map/all_to_all | solution.py:143
  93.4 127.3 %all-gather.7.cloned.1.call-start = ((), (), s32[]{:S(2)}) async-start(), calls=%async_computation.5 | async-start | bytes 4718592 | tf_op jit(solution)/shard_map/all_gather | solution.py:204
  102.2 15.9 %copy-start.16 = (bf16[1,2048,128]{2,1,0:T(8,128)(2,1)S(1)}, bf16[1,2048,128]{2,1,0:T(8,128)(2,1)}, u32[]{:S(2)}) copy-start(bf16[1,2048,128]{2,1,0:T(8,128)(2,1)} %param.28) | copy-start | bytes 1572868
  189.0 46.3 %copy-start.17 = (f32[2048]{0:T(1024)S(1)}, f32[2048]{0:T(1024)}, u32[]{:S(2)}) copy-start(f32[2048]{0:T(1024)} %param.36) | copy-start | bytes 24580
  189.0 139.7 %reduce-scatter.2.cloned.1.call-start = ((), (), s32[]{:S(2)}) async-start(), calls=%async_computation.6 | async-start | bytes 9437184 | tf_op jit(solution)/shard_map/reduce_scatter | solution.py:216
  220.7 21.6 %slice-start = ((s8[9437184]{0:T(1024)(128)(4,1)}), s8[1048576]{0:T(1024)(128)(4,1)S(1)}, s32[]{:S(2)}) async-start(s8[9437184]{0:T(1024)(128)(4,1)} %bitcast.106), calls=%async_computation.8 | async-start | bytes 2097152
  220.7 21.6 %slice-start.1 = ((s8[9437184]{0:T(1024)(128)(4,1)}), s8[4194304]{0:T(1024)(128)(4,1)S(1)}, s32[]{:S(2)}) async-start(s8[9437184]{0:T(1024)(128)(4,1)} %bitcast.106), calls=%async_computation.9 | async-start | bytes 8388608
  235.3 7.1 %copy-start.7 = (bf16[1024,2048]{1,0:T(8,128)(2,1)}, bf16[1024,2048]{1,0:T(8,128)(2,1)S(1)}, u32[]{:S(2)}) copy-start(bf16[1024,2048]{1,0:T(8,128)(2,1)S(1)} %get-tuple-element.43) | copy-start | bytes 12582916
  235.3 7.0 %slice-start.2 = ((s8[9437184]{0:T(1024)(128)(4,1)}), s8[4194304]{0:T(1024)(128)(4,1)S(1)}, s32[]{:S(2)}) async-start(s8[9437184]{0:T(1024)(128)(4,1)} %bitcast.106), calls=%async_computation.10 | async-start | bytes 8388608
  252.0 19.3 %copy-start.8 = (f32[2048]{0:T(1024)S(1)}, f32[2048]{0:T(1024)}, u32[]{:S(2)}) copy-start(f32[2048]{0:T(1024)} %param.40) | copy-start | bytes 24580
  254.4 1.3 collective-permute-start
  255.8 5.9 %collective-permute-start.1 = (f32[16,2048]{1,0:T(8,128)S(1)}, f32[16,2048]{1,0:T(8,128)S(1)}, u32[]{:S(2)}, u32[]{:S(2)}) collective-permute-start(f32[16,2048]{1,0:T(8,128)S(1)} %add.180), channel_id=1, source_target_pairs={{0,2},{1,3},{2,0},{3,1},{4,6},{5,7},{6,4},{7,5},{8,10},{9,11},{10,... | collective-permute-start | bytes 393224 | tf_op jit(solution)/shard_map/ppermute | solution.py:81
  261.8 8.6 %collective-permute-start.2 = (f32[16,2048]{1,0:T(8,128)S(1)}, f32[16,2048]{1,0:T(8,128)S(1)}, u32[]{:S(2)}, u32[]{:S(2)}) collective-permute-start(f32[16,2048]{1,0:T(8,128)S(1)} %add.181), channel_id=1, source_target_pairs={{0,4},{1,5},{2,6},{3,7},{4,0},{5,1},{6,2},{7,3},{8,12},{9,13},{10,... | collective-permute-start | bytes 393224 | tf_op jit(solution)/shard_map/ppermute | solution.py:81
  271.4 4.3 %collective-permute-start.3 = (bf16[9,2048]{1,0:T(8,128)(2,1)S(1)}, bf16[9,2048]{1,0:T(8,128)(2,1)S(1)}, u32[]{:S(2)}, u32[]{:S(2)}) collective-permute-start(bf16[9,2048]{1,0:T(8,128)(2,1)S(1)} %fusion.58), channel_id=1, source_target_pairs={{0,8},{8,0},{16,24},{24,16},{32,40},{40,32},{48,56},{56,48},{64,72... | collective-permute-start | bytes 110600 | tf_op jit(solution)/shard_map/ppermute | solution.py:92
  275.9 6.2 %collective-permute-start.4 = (bf16[18,2048]{1,0:T(8,128)(2,1)S(1)}, bf16[18,2048]{1,0:T(8,128)(2,1)S(1)}, u32[]{:S(2)}, u32[]{:S(2)}) collective-permute-start(bf16[18,2048]{1,0:T(8,128)(2,1)S(1)} %pad_maximum_fusion.4), channel_id=1, source_target_pairs={{0,16},{8,24},{16,0},{24,8},{32,48},{40,56},{48,32},{56,40},{64,80... | collective-permute-start | bytes 221192 | tf_op jit(solution)/shard_map/ppermute | solution.py:92
  282.2 5.4 %collective-permute-start.5 = (bf16[36,2048]{1,0:T(8,128)(2,1)S(1)}, bf16[36,2048]{1,0:T(8,128)(2,1)S(1)}, u32[]{:S(2)}, u32[]{:S(2)}) collective-permute-start(bf16[36,2048]{1,0:T(8,128)(2,1)S(1)} %pad_maximum_fusion.3), channel_id=1, source_target_pairs={{0,32},{8,40},{16,48},{24,56},{32,0},{40,8},{48,16},{56,24},{64,96... | collective-permute-start | bytes 442376 | tf_op jit(solution)/shard_map/ppermute | solution.py:92
  287.8 8.6 %collective-permute-start.6 = (bf16[72,2048]{1,0:T(8,128)(2,1)S(1)}, bf16[72,2048]{1,0:T(8,128)(2,1)S(1)}, u32[]{:S(2)}, u32[]{:S(2)}) collective-permute-start(bf16[72,2048]{1,0:T(8,128)(2,1)S(1)} %pad_maximum_fusion.2), channel_id=1, source_target_pairs={{0,64},{8,72},{16,80},{24,88},{32,96},{40,104},{48,112},{56,120},{... | collective-permute-start | bytes 884744 | tf_op jit(solution)/shard_map/ppermute | solution.py:92
  300.8 1.2 collective-permute-start.7
  302.0 3.6 collective-permute-start.8
  305.6 5.1 %collective-permute-start.9 = (f32[144]{0:T(256)S(1)}, f32[144]{0:T(256)S(1)}, u32[]{:S(2)}, u32[]{:S(2)}) collective-permute-start(f32[144]{0:T(256)S(1)} %max.26), channel_id=1, source_target_pairs={{0,4},{1,5},{2,6},{3,7},{4,0},{5,1},{6,2},{7,3},{8,12},{9,13},{10,... | collective-permute-start | bytes 1736 | tf_op jit(solution)/shard_map/ppermute | solution.py:81
  310.6 3.6 collective-permute-start.10
  314.2 5.1 %collective-permute-start.11 = (f32[144]{0:T(256)S(1)}, f32[144]{0:T(256)S(1)}, u32[]{:S(2)}, u32[]{:S(2)}) collective-permute-start(f32[144]{0:T(256)S(1)} %max.28), channel_id=1, source_target_pairs={{0,16},{8,24},{16,0},{24,8},{32,48},{40,56},{48,32},{56,40},{64,80... | collective-permute-start | bytes 1736 | tf_op jit(solution)/shard_map/ppermute | solution.py:81
  319.3 3.6 collective-permute-start.12
  322.9 5.3 %collective-permute-start.13 = (f32[144]{0:T(256)S(1)}, f32[144]{0:T(256)S(1)}, u32[]{:S(2)}, u32[]{:S(2)}) collective-permute-start(f32[144]{0:T(256)S(1)} %max.30), channel_id=1, source_target_pairs={{0,64},{8,72},{16,80},{24,88},{32,96},{40,104},{48,112},{56,120},{... | collective-permute-start | bytes 1736 | tf_op jit(solution)/shard_map/ppermute | solution.py:81
  328.2 30.0 %copy-start.1 = (bf16[384,2048]{1,0:T(8,128)(2,1)S(1)}, bf16[384,2048]{1,0:T(8,128)(2,1)}, u32[]{:S(2)}) copy-start(bf16[384,2048]{1,0:T(8,128)(2,1)} %param.39) | copy-start | bytes 4718596
  (9 other events, 28.8 us)
Sparse Core Ops, SparseCore 0:
  40.7 28.1 all-gather.8
  71.0 75.6 all-gather.4
  189.1 31.5 all-gather.6
  252.1 55.1 reduce-scatter.1

commit v9 on v8

--- a/solution.py
+++ b/solution.py
@@ -139,10 +139,9 @@
     owner_rows = arrived[slot_place]
     rows_all = lax.all_gather(owner_rows, "kv", axis=0, tiled=True)
     normed = norm_rows(rows_all, attn_gain).astype(jnp.bfloat16)
-    o_local, rows_all = lax.optimization_barrier((o_proj, rows_all))
     o_full = lax.all_to_all(
-        jnp.broadcast_to(o_local[None], (kv_count,) + o_proj.shape), "kv", split_axis=0, concat_axis=0, tiled=True
-    ).reshape(kv_count * o_local.shape[0], o_local.shape[1])
+        jnp.broadcast_to(o_proj[None], (kv_count,) + o_proj.shape), "kv", split_axis=0, concat_axis=0, tiled=True
+    ).reshape(kv_count * o_proj.shape[0], o_proj.shape[1])
     ff_dev = w_gate.shape[1]
     ff_piece = ff_dev // kv_count
     weight_piece = jnp.stack(

time: 369 us -> 353 us (0.957)
  waiting for transfers between devices: 163 us -> 146 us
    all_to_all x1, waiting for transfers between devices: 57.7 us -> 21 us  [shards(): lax.all_to_all(jnp.broadcast_to(o_proj[None], (kv_count,) + o_proj.shape)...]
    all_gather x1, waiting for transfers between devices: 0.01 us -> 12.5 us  [shards(): weight_all = lax.all_gather(weight_piece, 'req', axis=1, tiled=True)]
    all_gather x1, waiting for transfers between devices: 18 us -> 23.6 us  [shards(): rows_all = lax.all_gather(owner_rows, 'kv', axis=0, tiled=True)]
  transfers between devices with their start and end apart: 20 -> 20, of which waited for: 18 -> 19; matrix products, arithmetic and copies ran while one was open for 20% -> 21% of each run, Pallas kernels for 0% -> 0%
where the time goes in v9:
time: 353 us; the launch traced here: 348 us
  waiting for transfers between devices  146 us (41%)
  matrix products  78.2 us (22%)
  starting transfers between devices  41.5 us (12%)
  blocking collectives  22.9 us (6%)
  local copies, waits for them, and re-layouts  22.5 us (6%)
  other arithmetic  22.2 us (6%)
  between operations  15.1 us (4%)
    all_gather x1, waiting for transfers between devices, shards(): lax.all_gather(pieces.reshape(tok_req, q_cols), 'kv', axis=1, tiled=True)  32.9 us
    ppermute x10, waiting for transfers between devices, butterfly(): value = combine(value, lax.ppermute(value, axis, pairs))  28.4 us
    all_gather x1, waiting for transfers between devices, shards(): rows_all = lax.all_gather(owner_rows, 'kv', axis=0, tiled=True)  23.6 us
    all_to_all x1, blocking collectives, regroup(): lax.all_to_all(rows_in, ('req', 'kv'), split_axis=0, concat_axis=0, tiled...  22.9 us
    all_to_all x1, waiting for transfers between devices, shards(): lax.all_to_all(jnp.broadcast_to(o_proj[None], (kv_count,) + o_proj.shape)...  21 us
    sub x1, matrix products, prefill_full(): expd = jnp.exp(scores - row_peak)  15.9 us
    ppermute x10, starting transfers between devices, butterfly(): value = combine(value, lax.ppermute(value, axis, pairs))  14.8 us
    dot_general x1, matrix products, shards(): jnp.dot(attended, o_full, preferred_element_type=jnp.float32)  14.5 us
  transfers between devices with their start and end apart: 20, of which 19 were waited for; matrix products, arithmetic and copies ran while one was open for 21% of the time, Pallas kernels for 0%

profile of v9, /device:TPU:0, one launch (start us, length us, event | category | flops | bytes accessed | tf_op | source)
XLA Modules:
  0.0 348.0 jit_solution(8045263994068943234)
XLA Ops:
  13.4 11.1 %all-to-all-start = ((bf16[128,2,1024]{2,1,0:T(2,128)(2,1)}), bf16[128,2,1024]{2,1,0:T(2,128)(2,1)S(1)}, u32[]{:S(2)}, u32[]{:S(2)}) async-start(bf16[128,2,1024]{2,1,0:T(2,128)(2,1)} %reshape.453), calls=%async_computation | async-start | bytes 1048576 | tf_op jit(solution)/shard_map/all_to_all | solution.py:102
  25.3 12.8 %all-to-all-done = bf16[128,2,1024]{2,1,0:T(2,128)(2,1)S(1)} async-done(((bf16[128,2,1024]{2,1,0:T(2,128)(2,1)}), bf16[128,2,1024]{2,1,0:T(2,128)(2,1)S(1)}, u32[]{:S(2)}, u32[]{:S(2)}) %all-to-all-start) | async-done | bytes 524320 | tf_op jit(solution)/shard_map/all_to_all | solution.py:102
  43.9 5.6 %broadcast_in_dim.46 = bf16[8,256,2048]{2,1,0:T(8,128)(2,1)} broadcast(bf16[256,2048]{1,0:T(8,128)(2,1)} %param.35), dimensions={1,2} | broadcast | bytes 9437184 | tf_op jit(solution)/shard_map/broadcast_in_dim | solution.py:143
  49.5 5.1 %all-to-all-start.1 = ((bf16[8,256,2048]{2,1,0:T(8,128)(2,1)}), bf16[8,256,2048]{2,1,0:T(8,128)(2,1)}, u32[]{:S(2)}, u32[]{:S(2)}) async-start(bf16[8,256,2048]{2,1,0:T(8,128)(2,1)} %broadcast_in_dim.46), calls=%async_computation.1 | async-start | bytes 16777216 | tf_op jit(solution)/shard_map/all_to_all | solution.py:142
  57.6 4.1 %fusion.4 = pred[1016,3064]{1,0:T(8,128)(4,1)} fusion(s32[3064]{0:T(1024)S(1)} %iota_add_fusion, pred[3064]{0:T(1024)(128)(4,1)S(1)} %get-tuple-element.40, pred[3064]{0:T(1024)(128)(4,1)S(1)} %get-tuple-element.41), kind=kLoop, calls=%fused_computation.15 | loop fusion | flops 6226048 | bytes 3131408 | tf_op jit(solution)/shard_map/jit(_where)/select_n | solution.py:45
  61.7 23.6 %all-gather.9.cloned.1.call-done = bf16[1024,2048]{1,0:T(8,128)(2,1)} async-done(((bf16[128,2048]{1,0:T(8,128)(2,1)}), bf16[1024,2048]{1,0:T(8,128)(2,1)}) %all-gather.9.cloned.1.call-update) | async-done | bytes 4194320 | tf_op jit(solution)/shard_map/all_gather | solution.py:140
  85.3 3.2 fusion.10
  93.9 3.7 %multiply_reduce_fusion.1 = (f32[1024]{0:T(1024)S(1)}, f32[1024,128]{0,1:T(8,128)S(1)}) fusion(bf16[1024,2048]{1,0:T(8,128)(2,1)} %copy-done.3, bf16[2048,128]{1,0:T(8,128)(2,1)S(1)} %copy-done.6), kind=kOutput, calls=%fused_computation.72 | convolution fusion | flops 537132032 | bytes 5246976 | tf_op jit(solution)/shard_map/dot_general | solution.py:161
  103.4 3.9 %convolution_convert_fusion = bf16[1024,128]{1,0:T(8,128)(2,1)S(1)} fusion(bf16[1024,2048]{1,0:T(8,128)(2,1)} %copy-done.3, bf16[2048,128]{1,0:T(8,128)(2,1)S(1)} %copy-done.14), kind=kOutput, calls=%fused_computation.45 | convolution fusion | flops 537001984 | bytes 4980736 | tf_op jit(solution)/shard_map/dot_general | solution.py:162
  108.1 15.9 %fusion.94 = (f32[2,1016]{1,0:T(2,128)S(1)}, f32[2,1016,3064]{2,1,0:T(8,128)}) fusion(pred[1016,3064]{1,0:T(8,128)(4,1)} %fusion.4, bf16[1016,128]{1,0:T(8,128)(2,1)S(1)} %copy.49, bf16[2048,128]{1,0:T(8,128)(2,1)S(1)} %bitcast.114, bf16[1024,2,64]{2,0,1:T(8,128)(2,1)S(1)} %get-tuple-element.14, bf16[1024,2,64]{2,0,1:T(8,128)(2,1)S(1)} %get-tuple-element.15), kind=kOutput, calls=%fused_computation.171 | convolution fusion | flops 1621384704 | bytes 29334016 | tf_op jit(solution)/shard_map/sub | solution.py:48
  124.0 12.3 %fusion.32 = bf16[1016,2,128]{2,0,1:T(8,128)(2,1)S(1)} fusion(f32[2,1016,3064]{2,1,0:T(8,128)} %get-tuple-element.37, f32[2,1016]{1,0:T(2,128)S(1)} %get-tuple-element.36, bf16[1016,128]{1,0:T(8,128)(2,1)S(1)} %slice.70, bf16[2048,128]{1,0:T(8,128)(2,1)S(1)} %bitcast.115), kind=kOutput, calls=%fused_computation.44 | convolution fusion | flops 1608149248 | bytes 26216896 | tf_op jit(solution)/shard_map/gck,kd->cgd/dot_general | solution.py:50
  136.4 21.0 %all-to-all-done.1 = bf16[8,256,2048]{2,1,0:T(8,128)(2,1)} async-done(((bf16[8,256,2048]{2,1,0:T(8,128)(2,1)}), bf16[8,256,2048]{2,1,0:T(8,128)(2,1)}, u32[]{:S(2)}, u32[]{:S(2)}) %all-to-all-start.1) | async-done | bytes 8388640 | tf_op jit(solution)/shard_map/all_to_all | solution.py:142
  157.4 12.5 %all-gather.5.cloned.1.call-done = bf16[3,768,2048]{2,1,0:T(8,128)(2,1)} async-done(((bf16[3,48,2048]{2,1,0:T(8,128)(2,1)}), bf16[3,768,2048]{2,1,0:T(8,128)(2,1)}) %all-gather.5.cloned.1.call-update) | async-done | bytes 9437200 | tf_op jit(solution)/shard_map/all_gather | solution.py:154
  171.0 32.9 %all-gather.7.cloned.1.call-done = bf16[1024,2048]{0,1:T(8,128)(2,1)} async-done(((bf16[1024,256]{0,1:T(8,128)(2,1)}), bf16[1024,2048]{0,1:T(8,128)(2,1)}) %all-gather.7.cloned.1.call-update) | async-done | bytes 4194320 | tf_op jit(solution)/shard_map/all_gather | solution.py:203
  203.9 14.5 %fusion.7 = (f32[1024]{0:T(1024)S(1)}, bf16[1024,2048]{1,0:T(8,128)(2,1)S(1)}) fusion(bf16[1024,2048]{0,1:T(8,128)(2,1)} %all-gather.7.cloned.1.call-done, bf16[2048,2048]{1,0:T(8,128)(2,1)} %bitcast.25, bf16[1024,2048]{1,0:T(8,128)(2,1)} %all-gather.9.cloned.1.call-done), kind=kOutput, calls=%fused_computation.20 | convolution fusion | flops 8602516480 | bytes 20975616 | tf_op jit(solution)/shard_map/dot_general | solution.py:205
  218.5 7.0 %fusion.18 = f32[1024,768]{1,0:T(8,128)S(1)} fusion(bf16[3,768,2048]{2,1,0:T(8,128)(2,1)} %all-gather.5.cloned.1.call-done, bf16[1024,2048]{1,0:T(8,128)(2,1)S(1)} %get-tuple-element.39, f32[2048]{0:T(1024)S(1)} %copy-done.17, f32[1024]{0:T(1024)S(1)} %add_rsqrt_fusion.1), kind=kOutput, calls=%fused_computation.31 | convolution fusion | flops 3229614080 | bytes 10498048 | tf_op jit(solution)/shard_map/dot_general | solution.py:210
  225.6 3.9 %multiply_convert_fusion = bf16[1024,768]{1,0:T(8,128)(2,1)S(1)} fusion(f32[1024,768]{1,0:T(8,128)S(1)} %fusion.18, bf16[3,768,2048]{2,1,0:T(8,128)(2,1)S(1)} %bitcast.107, bf16[1024,2048]{1,0:T(8,128)(2,1)S(1)} %get-tuple-element.39, f32[2048]{0:T(1024)S(1)} %copy-done.17, f32[1024]{0:T(1024)S(1)} %add_rsqrt_fusion.1), kind=kOutput, calls=%fused_computation.35 | convolution fusion | flops 3234332672 | bytes 12070912 | tf_op jit(solution)/shard_map/dot_general | solution.py:209
  229.5 5.7 %fusion.16 = f32[1024,2048]{1,0:T(8,128)} fusion(bf16[1024,768]{1,0:T(8,128)(2,1)S(1)} %multiply_convert_fusion, bf16[3,768,2048]{2,1,0:T(8,128)(2,1)S(1)} %bitcast.107), kind=kOutput, calls=%fused_computation.29 | convolution fusion | flops 3221225472 | bytes 13107200 | tf_op jit(solution)/shard_map/dot_general | solution.py:214
  239.7 5.2 %collective-permute-done.1 = f32[16,2048]{1,0:T(8,128)S(1)} collective-permute-done((f32[16,2048]{1,0:T(8,128)S(1)}, f32[16,2048]{1,0:T(8,128)S(1)}, u32[]{:S(2)}, u32[]{:S(2)}) %collective-permute-start.1) | collective-permute-done | bytes 131104 | tf_op jit(solution)/shard_map/ppermute | solution.py:81
  246.7 6.8 %collective-permute-done.2 = f32[16,2048]{1,0:T(8,128)S(1)} collective-permute-done((f32[16,2048]{1,0:T(8,128)S(1)}, f32[16,2048]{1,0:T(8,128)S(1)}, u32[]{:S(2)}, u32[]{:S(2)}) %collective-permute-start.2) | collective-permute-done | bytes 131104 | tf_op jit(solution)/shard_map/ppermute | solution.py:81
  256.2 2.8 collective-permute-done.3
  259.1 3.1 collective-permute-start.4
  262.2 3.1 collective-permute-done.4
  267.0 3.8 %collective-permute-done.5 = bf16[36,2048]{1,0:T(8,128)(2,1)S(1)} collective-permute-done((bf16[36,2048]{1,0:T(8,128)(2,1)S(1)}, bf16[36,2048]{1,0:T(8,128)(2,1)S(1)}, u32[]{:S(2)}, u32[]{:S(2)}) %collective-permute-start.5) | collective-permute-done | bytes 147488 | tf_op jit(solution)/shard_map/ppermute | solution.py:92
  270.9 3.9 %collective-permute-start.6 = (bf16[72,2048]{1,0:T(8,128)(2,1)S(1)}, bf16[72,2048]{1,0:T(8,128)(2,1)S(1)}, u32[]{:S(2)}, u32[]{:S(2)}) collective-permute-start(bf16[72,2048]{1,0:T(8,128)(2,1)S(1)} %pad_maximum_fusion.2), channel_id=1, source_target_pairs={{0,64},{8,72},{16,80},{24,88},{32,96},{40,104},{48,112},{56,120},{... | collective-permute-start | bytes 884744 | tf_op jit(solution)/shard_map/ppermute | solution.py:92
  274.9 4.7 %collective-permute-done.6 = bf16[72,2048]{1,0:T(8,128)(2,1)S(1)} collective-permute-done((bf16[72,2048]{1,0:T(8,128)(2,1)S(1)}, bf16[72,2048]{1,0:T(8,128)(2,1)S(1)}, u32[]{:S(2)}, u32[]{:S(2)}) %collective-permute-start.6) | collective-permute-done | bytes 294944 | tf_op jit(solution)/shard_map/ppermute | solution.py:92
  279.7 4.3 %convolution_reduce_fusion = f32[144]{0:T(256)S(1)} fusion(bf16[2048,1187]{0,1:T(8,128)(2,1)} %param.41, bf16[72,2048]{1,0:T(8,128)(2,1)S(1)} %get-tuple-element.17, bf16[72,2048]{1,0:T(8,128)(2,1)S(1)} %get-tuple-element.16), kind=kOutput, calls=%fused_computation.46 | convolution fusion | flops 701471488 | bytes 5452352 | tf_op jit(solution)/shard_map/dot_general | solution.py:221
  285.6 3.2 collective-permute-done.8
  290.6 3.2 collective-permute-done.9
  297.4 2.9 collective-permute-start.11
  306.1 3.7 %collective-permute-start.13 = (f32[144]{0:T(256)S(1)}, f32[144]{0:T(256)S(1)}, u32[]{:S(2)}, u32[]{:S(2)}) collective-permute-start(f32[144]{0:T(256)S(1)} %max.30), channel_id=1, source_target_pairs={{0,64},{8,72},{16,80},{24,88},{32,96},{40,104},{48,112},{56,120},{... | collective-permute-start | bytes 1736 | tf_op jit(solution)/shard_map/ppermute | solution.py:81
  315.5 22.9 %all_to_all.29 = bf16[128,2,1024]{2,1,0:T(2,128)(2,1)S(1)} all-to-all(bf16[128,2,1024]{2,1,0:T(2,128)(2,1)S(1)} %reshape.455), channel_id=1, replica_groups=mesh['req'=16,'kv'=8] {'req','kv'}, dimensions={0} | all-to-all | bytes 1048576 | tf_op jit(solution)/shard_map/all_to_all | solution.py:102
  (145 shorter events, 60.4 us)
Async XLA Ops:
  7.2 35.8 %copy-start = (bf16[384,2048]{1,0:T(8,128)(2,1)S(1)}, bf16[384,2048]{1,0:T(8,128)(2,1)}, u32[]{:S(2)}) copy-start(bf16[384,2048]{1,0:T(8,128)(2,1)} %param.39) | copy-start | bytes 4718596
  13.4 24.7 %all-to-all-start = ((bf16[128,2,1024]{2,1,0:T(2,128)(2,1)}), bf16[128,2,1024]{2,1,0:T(2,128)(2,1)S(1)}, u32[]{:S(2)}, u32[]{:S(2)}) async-start(bf16[128,2,1024]{2,1,0:T(2,128)(2,1)} %reshape.453), calls=%async_computation | async-start | bytes 1048576 | tf_op jit(solution)/shard_map/all_to_all | solution.py:102
  24.5 60.7 %all-gather.9.cloned.1.call-start = ((), (), s32[]{:S(2)}) async-start(), calls=%async_computation.7 | async-start | bytes 4718592 | tf_op jit(solution)/shard_map/all_gather | solution.py:140
  40.6 129.3 %all-gather.5.cloned.1.call-start = ((), (), s32[]{:S(2)}) async-start(), calls=%async_computation.4 | async-start | bytes 10027008 | tf_op jit(solution)/shard_map/all_gather | solution.py:154
  49.5 6.0 %copy-start.10 = (s32[8]{0:T(128)S(1)}, s32[8]{0:T(128)}, u32[]{:S(2)}) copy-start(s32[8]{0:T(128)} %param.23) | copy-start | bytes 100
  49.5 107.9 %all-to-all-start.1 = ((bf16[8,256,2048]{2,1,0:T(8,128)(2,1)}), bf16[8,256,2048]{2,1,0:T(8,128)(2,1)}, u32[]{:S(2)}, u32[]{:S(2)}) async-start(bf16[8,256,2048]{2,1,0:T(8,128)(2,1)} %broadcast_in_dim.46), calls=%async_computation.1 | async-start | bytes 16777216 | tf_op jit(solution)/shard_map/all_to_all | solution.py:142
  54.7 149.2 %all-gather.7.cloned.1.call-start = ((), (), s32[]{:S(2)}) async-start(), calls=%async_computation.5 | async-start | bytes 4718592 | tf_op jit(solution)/shard_map/all_gather | solution.py:203
  55.6 32.9 %copy-start.9 = (f32[2048]{0:T(1024)S(1)}, f32[2048]{0:T(1024)}, u32[]{:S(2)}) copy-start(f32[2048]{0:T(1024)} %param.29) | copy-start | bytes 24580
  93.9 5.4 %copy-start.12 = (f32[128]{0:T(128)S(1)}, f32[128]{0:T(128)}, u32[]{:S(2)}) copy-start(f32[128]{0:T(128)} %param.33) | copy-start | bytes 1540
  108.1 15.9 %copy-start.16 = (bf16[1,2048,128]{2,1,0:T(8,128)(2,1)S(1)}, bf16[1,2048,128]{2,1,0:T(8,128)(2,1)}, u32[]{:S(2)}) copy-start(bf16[1,2048,128]{2,1,0:T(8,128)(2,1)} %param.28) | copy-start | bytes 1572868
  170.9 47.5 %copy-start.17 = (f32[2048]{0:T(1024)S(1)}, f32[2048]{0:T(1024)}, u32[]{:S(2)}) copy-start(f32[2048]{0:T(1024)} %param.36) | copy-start | bytes 24580
  171.0 141.0 %reduce-scatter.2.cloned.1.call-start = ((), (), s32[]{:S(2)}) async-start(), calls=%async_computation.6 | async-start | bytes 9437184 | tf_op jit(solution)/shard_map/reduce_scatter | solution.py:215
  203.9 21.6 %slice-start = ((s8[9437184]{0:T(1024)(128)(4,1)}), s8[1048576]{0:T(1024)(128)(4,1)S(1)}, s32[]{:S(2)}) async-start(s8[9437184]{0:T(1024)(128)(4,1)} %bitcast.106), calls=%async_computation.8 | async-start | bytes 2097152
  203.9 21.6 %slice-start.1 = ((s8[9437184]{0:T(1024)(128)(4,1)}), s8[4194304]{0:T(1024)(128)(4,1)S(1)}, s32[]{:S(2)}) async-start(s8[9437184]{0:T(1024)(128)(4,1)} %bitcast.106), calls=%async_computation.9 | async-start | bytes 8388608
  218.5 7.1 %copy-start.7 = (bf16[1024,2048]{1,0:T(8,128)(2,1)}, bf16[1024,2048]{1,0:T(8,128)(2,1)S(1)}, u32[]{:S(2)}) copy-start(bf16[1024,2048]{1,0:T(8,128)(2,1)S(1)} %get-tuple-element.39) | copy-start | bytes 12582916
  218.5 7.0 %slice-start.2 = ((s8[9437184]{0:T(1024)(128)(4,1)}), s8[4194304]{0:T(1024)(128)(4,1)S(1)}, s32[]{:S(2)}) async-start(s8[9437184]{0:T(1024)(128)(4,1)} %bitcast.106), calls=%async_computation.10 | async-start | bytes 8388608
  235.2 19.3 %copy-start.8 = (f32[2048]{0:T(1024)S(1)}, f32[2048]{0:T(1024)}, u32[]{:S(2)}) copy-start(f32[2048]{0:T(1024)} %param.40) | copy-start | bytes 24580
  237.6 1.3 collective-permute-start
  239.0 5.9 %collective-permute-start.1 = (f32[16,2048]{1,0:T(8,128)S(1)}, f32[16,2048]{1,0:T(8,128)S(1)}, u32[]{:S(2)}, u32[]{:S(2)}) collective-permute-start(f32[16,2048]{1,0:T(8,128)S(1)} %add.180), channel_id=1, source_target_pairs={{0,2},{1,3},{2,0},{3,1},{4,6},{5,7},{6,4},{7,5},{8,10},{9,11},{10,... | collective-permute-start | bytes 393224 | tf_op jit(solution)/shard_map/ppermute | solution.py:81
  244.9 8.6 %collective-permute-start.2 = (f32[16,2048]{1,0:T(8,128)S(1)}, f32[16,2048]{1,0:T(8,128)S(1)}, u32[]{:S(2)}, u32[]{:S(2)}) collective-permute-start(f32[16,2048]{1,0:T(8,128)S(1)} %add.181), channel_id=1, source_target_pairs={{0,4},{1,5},{2,6},{3,7},{4,0},{5,1},{6,2},{7,3},{8,12},{9,13},{10,... | collective-permute-start | bytes 393224 | tf_op jit(solution)/shard_map/ppermute | solution.py:81
  254.6 4.3 %collective-permute-start.3 = (bf16[9,2048]{1,0:T(8,128)(2,1)S(1)}, bf16[9,2048]{1,0:T(8,128)(2,1)S(1)}, u32[]{:S(2)}, u32[]{:S(2)}) collective-permute-start(bf16[9,2048]{1,0:T(8,128)(2,1)S(1)} %fusion.59), channel_id=1, source_target_pairs={{0,8},{8,0},{16,24},{24,16},{32,40},{40,32},{48,56},{56,48},{64,72... | collective-permute-start | bytes 110600 | tf_op jit(solution)/shard_map/ppermute | solution.py:92
  259.1 6.2 %collective-permute-start.4 = (bf16[18,2048]{1,0:T(8,128)(2,1)S(1)}, bf16[18,2048]{1,0:T(8,128)(2,1)S(1)}, u32[]{:S(2)}, u32[]{:S(2)}) collective-permute-start(bf16[18,2048]{1,0:T(8,128)(2,1)S(1)} %pad_maximum_fusion.4), channel_id=1, source_target_pairs={{0,16},{8,24},{16,0},{24,8},{32,48},{40,56},{48,32},{56,40},{64,80... | collective-permute-start | bytes 221192 | tf_op jit(solution)/shard_map/ppermute | solution.py:92
  265.4 5.4 %collective-permute-start.5 = (bf16[36,2048]{1,0:T(8,128)(2,1)S(1)}, bf16[36,2048]{1,0:T(8,128)(2,1)S(1)}, u32[]{:S(2)}, u32[]{:S(2)}) collective-permute-start(bf16[36,2048]{1,0:T(8,128)(2,1)S(1)} %pad_maximum_fusion.3), channel_id=1, source_target_pairs={{0,32},{8,40},{16,48},{24,56},{32,0},{40,8},{48,16},{56,24},{64,96... | collective-permute-start | bytes 442376 | tf_op jit(solution)/shard_map/ppermute | solution.py:92
  270.9 8.6 %collective-permute-start.6 = (bf16[72,2048]{1,0:T(8,128)(2,1)S(1)}, bf16[72,2048]{1,0:T(8,128)(2,1)S(1)}, u32[]{:S(2)}, u32[]{:S(2)}) collective-permute-start(bf16[72,2048]{1,0:T(8,128)(2,1)S(1)} %pad_maximum_fusion.2), channel_id=1, source_target_pairs={{0,64},{8,72},{16,80},{24,88},{32,96},{40,104},{48,112},{56,120},{... | collective-permute-start | bytes 884744 | tf_op jit(solution)/shard_map/ppermute | solution.py:92
  284.0 1.2 collective-permute-start.7
  285.2 3.6 %collective-permute-start.8 = (f32[144]{0:T(256)S(1)}, f32[144]{0:T(256)S(1)}, u32[]{:S(2)}, u32[]{:S(2)}) collective-permute-start(f32[144]{0:T(256)S(1)} %max.25), channel_id=1, source_target_pairs={{0,2},{1,3},{2,0},{3,1},{4,6},{5,7},{6,4},{7,5},{8,10},{9,11},{10,... | collective-permute-start | bytes 1736 | tf_op jit(solution)/shard_map/ppermute | solution.py:81
  288.8 5.1 %collective-permute-start.9 = (f32[144]{0:T(256)S(1)}, f32[144]{0:T(256)S(1)}, u32[]{:S(2)}, u32[]{:S(2)}) collective-permute-start(f32[144]{0:T(256)S(1)} %max.26), channel_id=1, source_target_pairs={{0,4},{1,5},{2,6},{3,7},{4,0},{5,1},{6,2},{7,3},{8,12},{9,13},{10,... | collective-permute-start | bytes 1736 | tf_op jit(solution)/shard_map/ppermute | solution.py:81
  293.8 3.6 %collective-permute-start.10 = (f32[144]{0:T(256)S(1)}, f32[144]{0:T(256)S(1)}, u32[]{:S(2)}, u32[]{:S(2)}) collective-permute-start(f32[144]{0:T(256)S(1)} %max.27), channel_id=1, source_target_pairs={{0,8},{8,0},{16,24},{24,16},{32,40},{40,32},{48,56},{56,48},{64,72... | collective-permute-start | bytes 1736 | tf_op jit(solution)/shard_map/ppermute | solution.py:81
  297.4 5.1 %collective-permute-start.11 = (f32[144]{0:T(256)S(1)}, f32[144]{0:T(256)S(1)}, u32[]{:S(2)}, u32[]{:S(2)}) collective-permute-start(f32[144]{0:T(256)S(1)} %max.28), channel_id=1, source_target_pairs={{0,16},{8,24},{16,0},{24,8},{32,48},{40,56},{48,32},{56,40},{64,80... | collective-permute-start | bytes 1736 | tf_op jit(solution)/shard_map/ppermute | solution.py:81
  302.5 3.6 %collective-permute-start.12 = (f32[144]{0:T(256)S(1)}, f32[144]{0:T(256)S(1)}, u32[]{:S(2)}, u32[]{:S(2)}) collective-permute-start(f32[144]{0:T(256)S(1)} %max.29), channel_id=1, source_target_pairs={{0,32},{8,40},{16,48},{24,56},{32,0},{40,8},{48,16},{56,24},{64,96... | collective-permute-start | bytes 1736 | tf_op jit(solution)/shard_map/ppermute | solution.py:81
  306.1 5.3 %collective-permute-start.13 = (f32[144]{0:T(256)S(1)}, f32[144]{0:T(256)S(1)}, u32[]{:S(2)}, u32[]{:S(2)}) collective-permute-start(f32[144]{0:T(256)S(1)} %max.30), channel_id=1, source_target_pairs={{0,64},{8,72},{16,80},{24,88},{32,96},{40,104},{48,112},{56,120},{... | collective-permute-start | bytes 1736 | tf_op jit(solution)/shard_map/ppermute | solution.py:81
  311.4 30.0 %copy-start.1 = (bf16[384,2048]{1,0:T(8,128)(2,1)S(1)}, bf16[384,2048]{1,0:T(8,128)(2,1)}, u32[]{:S(2)}) copy-start(bf16[384,2048]{1,0:T(8,128)(2,1)} %param.39) | copy-start | bytes 4718596
  (9 other events, 30.4 us)
Sparse Core Ops, SparseCore 0:
  40.7 44.5 all-gather.8
  87.4 82.4 all-gather.4
  172.2 31.6 all-gather.6
  235.3 55.1 reduce-scatter.1

commit v10 on v9

--- a/solution.py
+++ b/solution.py
@@ -148,10 +148,17 @@
         [
             lax.dynamic_slice_in_dim(w_gate, kv_index * ff_piece, ff_piece, axis=1).T,
             lax.dynamic_slice_in_dim(w_up, kv_index * ff_piece, ff_piece, axis=1).T,
-            lax.dynamic_slice_in_dim(w_down, kv_index * ff_piece, ff_piece, axis=0),
         ]
     )
     weight_all = lax.all_gather(weight_piece, "req", axis=1, tiled=True)
+    down_piece = lax.dynamic_slice_in_dim(w_down, kv_index * ff_piece, ff_piece, axis=0)
+    down_all = lax.all_to_all(
+        jnp.broadcast_to(down_piece[None], (req_count,) + down_piece.shape),
+        "req",
+        split_axis=0,
+        concat_axis=0,
+        tiled=True,
+    )
     model_dim = w_gate.shape[0]
     q_cols = q_proj.shape[1]
     kv_cols = k_proj.shape[1]
@@ -196,10 +203,10 @@
         cache_len,
     )
     pieces = jnp.concatenate([pre_out, dec_out], axis=0)
-    pieces, weight_all, o_full = lax.optimization_barrier((pieces, weight_all, o_full))
+    pieces, weight_all, down_all, o_full = lax.optimization_barrier((pieces, weight_all, down_all, o_full))
     gate_w = weight_all[0]
     up_w = weight_all[1]
-    down_w = weight_all[2]
+    down_w = down_all.reshape(req_count * ff_piece, model_dim)
     attended = lax.all_gather(pieces.reshape(tok_req, q_cols), "kv", axis=1, tiled=True)
     resid = (
         rows_all.astype(jnp.float32) + jnp.dot(attended, o_full, preferred_element_type=jnp.float32)

time: 353 us -> 384 us (1.088)
  waiting for transfers between devices: 146 us -> 164 us
  local copies, waits for them, and re-layouts: 22.5 us -> 33.9 us
  starting transfers between devices: 41.5 us -> 46.7 us
  matrix products: 78.2 us -> 74.3 us
    all_to_all x1, waiting for transfers between devices: 21 us -> 57.8 us  [shards(): lax.all_to_all(jnp.broadcast_to(o_proj[None], (kv_count,) + o_proj.shape)...]
    all_to_all x0 -> x1, waiting for transfers between devices: none -> 19.8 us  [shards(): lax.all_to_all(jnp.broadcast_to(down_piece[None], (req_count,) + down_pie...]
    all_gather x1, waiting for transfers between devices: 23.6 us -> 9.96 us  [shards(): rows_all = lax.all_gather(owner_rows, 'kv', axis=0, tiled=True)]
    all_gather x1, waiting for transfers between devices: 12.5 us -> 0.01 us  [shards(): weight_all = lax.all_gather(weight_piece, 'req', axis=1, tiled=True)]
    all_gather x1, waiting for transfers between devices: 32.9 us -> 20.7 us  [shards(): lax.all_gather(pieces.reshape(tok_req, q_cols), 'kv', axis=1, tiled=True)]
    optimization_barrier x1 -> x2, local copies, waits for them, and re-layouts: 1.01 us -> 9.29 us  [shards(): lax.optimization_barrier((pieces, weight_all, down_all, o_full))]
    all_to_all x0 -> x1, starting transfers between devices: none -> 4.51 us  [shards(): lax.all_to_all(jnp.broadcast_to(down_piece[None], (req_count,) + down_pie...]
  transfers between devices with their start and end apart: 20 -> 21, of which waited for: 19 -> 19; matrix products, arithmetic and copies ran while one was open for 21% -> 22% of each run, Pallas kernels for 0% -> 0%
where the time goes in v10:
time: 384 us; the launch traced here: 379 us
  waiting for transfers between devices  164 us (43%)
  matrix products  74.3 us (19%)
  starting transfers between devices  46.7 us (12%)
  local copies, waits for them, and re-layouts  33.9 us (9%)
  blocking collectives  22.9 us (6%)
  other arithmetic  22.4 us (6%)
  between operations  15.2 us (4%)
    all_to_all x1, waiting for transfers between devices, shards(): lax.all_to_all(jnp.broadcast_to(o_proj[None], (kv_count,) + o_proj.shape)...  57.8 us
    ppermute x10, waiting for transfers between devices, butterfly(): value = combine(value, lax.ppermute(value, axis, pairs))  28.3 us
    all_to_all x1, blocking collectives, regroup(): lax.all_to_all(rows_in, ('req', 'kv'), split_axis=0, concat_axis=0, tiled...  22.9 us
    all_gather x1, waiting for transfers between devices, shards(): lax.all_gather(pieces.reshape(tok_req, q_cols), 'kv', axis=1, tiled=True)  20.7 us
    all_to_all x1, waiting for transfers between devices, shards(): lax.all_to_all(jnp.broadcast_to(down_piece[None], (req_count,) + down_pie...  19.8 us
    sub x1, matrix products, prefill_full(): expd = jnp.exp(scores - row_peak)  15.9 us
    ppermute x10, starting transfers between devices, butterfly(): value = combine(value, lax.ppermute(value, axis, pairs))  14.9 us
    ppermute x4, waiting for transfers between devices, butterfly_gather(): other = lax.ppermute(value, axis, pairs)  14.3 us
  transfers between devices with their start and end apart: 21, of which 19 were waited for; matrix products, arithmetic and copies ran while one was open for 22% of the time, Pallas kernels for 0%

profile of v10, /device:TPU:0, one launch (start us, length us, event | category | flops | bytes accessed | tf_op | source)
XLA Modules:
  0.0 379.1 jit_solution(18041660837785122143)
XLA Ops:
  13.5 11.1 %all-to-all-start = ((bf16[128,2,1024]{2,1,0:T(2,128)(2,1)}), bf16[128,2,1024]{2,1,0:T(2,128)(2,1)S(1)}, u32[]{:S(2)}, u32[]{:S(2)}) async-start(bf16[128,2,1024]{2,1,0:T(2,128)(2,1)} %reshape.458), calls=%async_computation | async-start | bytes 1048576 | tf_op jit(solution)/shard_map/all_to_all | solution.py:102
  25.5 12.8 %all-to-all-done = bf16[128,2,1024]{2,1,0:T(2,128)(2,1)S(1)} async-done(((bf16[128,2,1024]{2,1,0:T(2,128)(2,1)}), bf16[128,2,1024]{2,1,0:T(2,128)(2,1)S(1)}, u32[]{:S(2)}, u32[]{:S(2)}) %all-to-all-start) | async-done | bytes 524320 | tf_op jit(solution)/shard_map/all_to_all | solution.py:102
  42.9 4.5 %all-to-all-start.1 = ((bf16[16,48,2048]{2,1,0:T(8,128)(2,1)}), bf16[16,48,2048]{2,1,0:T(8,128)(2,1)}, u32[]{:S(2)}, u32[]{:S(2)}) async-start(bf16[16,48,2048]{2,1,0:T(8,128)(2,1)} %broadcast_in_dim.44), calls=%async_computation.1 | async-start | bytes 6291456 | tf_op jit(solution)/shard_map/all_to_all | solution.py:155
  55.0 4.0 %fusion.4 = pred[1016,3064]{1,0:T(8,128)(4,1)} fusion(s32[3064]{0:T(1024)S(1)} %iota_add_fusion, pred[3064]{0:T(1024)(128)(4,1)S(1)} %get-tuple-element.42, pred[3064]{0:T(1024)(128)(4,1)S(1)} %get-tuple-element.43), kind=kLoop, calls=%fused_computation.15 | loop fusion | flops 6226048 | bytes 3131408 | tf_op jit(solution)/shard_map/jit(_where)/select_n | solution.py:45
  59.0 10.0 %all-gather.9.cloned.1.call-done = bf16[1024,2048]{1,0:T(8,128)(2,1)} async-done(((bf16[128,2048]{1,0:T(8,128)(2,1)}), bf16[1024,2048]{1,0:T(8,128)(2,1)}) %all-gather.9.cloned.1.call-update) | async-done | bytes 4194320 | tf_op jit(solution)/shard_map/all_gather | solution.py:140
  69.0 3.2 fusion.10
  76.0 3.7 multiply_reduce_fusion.1
  81.5 19.8 %all-to-all-done.1 = bf16[16,48,2048]{2,1,0:T(8,128)(2,1)} async-done(((bf16[16,48,2048]{2,1,0:T(8,128)(2,1)}), bf16[16,48,2048]{2,1,0:T(8,128)(2,1)}, u32[]{:S(2)}, u32[]{:S(2)}) %all-to-all-start.1) | async-done | bytes 3145760 | tf_op jit(solution)/shard_map/all_to_all | solution.py:155
  101.4 5.6 %broadcast_in_dim.49 = bf16[8,256,2048]{2,1,0:T(8,128)(2,1)} broadcast(bf16[256,2048]{1,0:T(8,128)(2,1)} %param.35), dimensions={1,2} | broadcast | bytes 9437184 | tf_op jit(solution)/shard_map/broadcast_in_dim | solution.py:143
  107.0 5.2 %all-to-all-start.2 = ((bf16[8,256,2048]{2,1,0:T(8,128)(2,1)}), bf16[8,256,2048]{2,1,0:T(8,128)(2,1)}, u32[]{:S(2)}, u32[]{:S(2)}) async-start(bf16[8,256,2048]{2,1,0:T(8,128)(2,1)} %broadcast_in_dim.49), calls=%async_computation.2 | async-start | bytes 16777216 | tf_op jit(solution)/shard_map/all_to_all | solution.py:142
  116.8 3.7 convolution_convert_fusion
  121.3 15.9 %fusion.83 = (f32[2,1016]{1,0:T(2,128)S(1)}, f32[2,1016,3064]{2,1,0:T(8,128)}) fusion(pred[1016,3064]{1,0:T(8,128)(4,1)} %fusion.4, bf16[1016,128]{1,0:T(8,128)(2,1)S(1)} %copy.48, bf16[2048,128]{1,0:T(8,128)(2,1)S(1)} %bitcast.108, bf16[1024,2,64]{2,0,1:T(8,128)(2,1)S(1)} %get-tuple-element.16, bf16[1024,2,64]{2,0,1:T(8,128)(2,1)S(1)} %get-tuple-element.17), kind=kOutput, calls=%fused_computation.164 | convolution fusion | flops 1621384704 | bytes 29334016 | tf_op jit(solution)/shard_map/sub | solution.py:48
  137.2 11.7 %fusion.20 = bf16[1016,2,128]{2,0,1:T(8,128)(2,1)S(1)} fusion(f32[2,1016,3064]{2,1,0:T(8,128)} %get-tuple-element.39, f32[2,1016]{1,0:T(2,128)S(1)} %get-tuple-element.38, bf16[1016,128]{1,0:T(8,128)(2,1)S(1)} %slice.66, bf16[2048,128]{1,0:T(8,128)(2,1)} %bitcast.109), kind=kOutput, calls=%fused_computation.36 | convolution fusion | flops 1608149248 | bytes 26216896 | tf_op jit(solution)/shard_map/gck,kd->cgd/dot_general | solution.py:50
  149.0 57.8 %all-to-all-done.2 = bf16[8,256,2048]{2,1,0:T(8,128)(2,1)} async-done(((bf16[8,256,2048]{2,1,0:T(8,128)(2,1)}), bf16[8,256,2048]{2,1,0:T(8,128)(2,1)}, u32[]{:S(2)}, u32[]{:S(2)}) %all-to-all-start.2) | async-done | bytes 8388640 | tf_op jit(solution)/shard_map/all_to_all | solution.py:142
  207.8 8.3 %copy.57 = bf16[2,768,2048]{2,1,0:T(8,128)(2,1)} copy(bf16[2,768,2048]{2,0,1:T(2,128)(2,1)} %all-gather.5.cloned.1.call-done) | data formatting | bytes 12582912 | tf_op jit(solution)/shard_map/optimization_barrier | solution.py:206
  216.1 20.7 %all-gather.7.cloned.1.call-done = bf16[1024,2048]{0,1:T(8,128)(2,1)} async-done(((bf16[1024,256]{0,1:T(8,128)(2,1)}), bf16[1024,2048]{0,1:T(8,128)(2,1)}) %all-gather.7.cloned.1.call-update) | async-done | bytes 4194320 | tf_op jit(solution)/shard_map/all_gather | solution.py:210
  236.8 14.3 %fusion.7 = (f32[1024]{0:T(1024)S(1)}, bf16[1024,2048]{1,0:T(8,128)(2,1)S(1)}) fusion(bf16[1024,2048]{0,1:T(8,128)(2,1)} %all-gather.7.cloned.1.call-done, bf16[2048,2048]{1,0:T(8,128)(2,1)} %bitcast.24, bf16[1024,2048]{1,0:T(8,128)(2,1)} %all-gather.9.cloned.1.call-done), kind=kOutput, calls=%fused_computation.20 | convolution fusion | flops 8602516480 | bytes 20975616 | tf_op jit(solution)/shard_map/dot_general | solution.py:212
  251.1 3.5 fusion.14
  254.6 3.9 %multiply_convert_fusion = bf16[1024,768]{1,0:T(8,128)(2,1)S(1)} fusion(f32[1024,768]{1,0:T(8,128)S(1)} %fusion.14, bf16[2,768,2048]{2,1,0:T(8,128)(2,1)S(1)} %copy-done.4, bf16[1024,2048]{1,0:T(8,128)(2,1)S(1)} %get-tuple-element.41, f32[2048]{0:T(1024)S(1)} %copy-done.18, f32[1024]{0:T(1024)S(1)} %add_rsqrt_fusion.1), kind=kOutput, calls=%fused_computation.31 | convolution fusion | flops 3234332672 | bytes 12070912 | tf_op jit(solution)/shard_map/dot_general | solution.py:216
  258.6 7.5 %fusion.88 = f32[1024,2048]{1,0:T(8,128)} fusion(bf16[1024,768]{1,0:T(8,128)(2,1)S(1)} %multiply_convert_fusion, bf16[768,2048]{1,0:T(8,128)(2,1)} %bitcast.28), kind=kOutput, calls=%fused_computation.165 | convolution fusion | flops 3221225472 | bytes 13107200 | tf_op jit(solution)/shard_map/dot_general | solution.py:221
  270.7 5.2 %collective-permute-done.1 = f32[16,2048]{1,0:T(8,128)S(1)} collective-permute-done((f32[16,2048]{1,0:T(8,128)S(1)}, f32[16,2048]{1,0:T(8,128)S(1)}, u32[]{:S(2)}, u32[]{:S(2)}) %collective-permute-start.1) | collective-permute-done | bytes 131104 | tf_op jit(solution)/shard_map/ppermute | solution.py:81
  277.6 6.8 %collective-permute-done.2 = f32[16,2048]{1,0:T(8,128)S(1)} collective-permute-done((f32[16,2048]{1,0:T(8,128)S(1)}, f32[16,2048]{1,0:T(8,128)S(1)}, u32[]{:S(2)}, u32[]{:S(2)}) %collective-permute-start.2) | collective-permute-done | bytes 131104 | tf_op jit(solution)/shard_map/ppermute | solution.py:81
  290.0 3.1 collective-permute-start.4
  293.1 3.1 collective-permute-done.4
  297.9 3.8 collective-permute-done.5
  301.8 3.9 %collective-permute-start.6 = (bf16[72,2048]{1,0:T(8,128)(2,1)S(1)}, bf16[72,2048]{1,0:T(8,128)(2,1)S(1)}, u32[]{:S(2)}, u32[]{:S(2)}) collective-permute-start(bf16[72,2048]{1,0:T(8,128)(2,1)S(1)} %pad_maximum_fusion.2), channel_id=1, source_target_pairs={{0,64},{8,72},{16,80},{24,88},{32,96},{40,104},{48,112},{56,120},{... | collective-permute-start | bytes 884744 | tf_op jit(solution)/shard_map/ppermute | solution.py:92
  305.8 4.7 %collective-permute-done.6 = bf16[72,2048]{1,0:T(8,128)(2,1)S(1)} collective-permute-done((bf16[72,2048]{1,0:T(8,128)(2,1)S(1)}, bf16[72,2048]{1,0:T(8,128)(2,1)S(1)}, u32[]{:S(2)}, u32[]{:S(2)}) %collective-permute-start.6) | collective-permute-done | bytes 294944 | tf_op jit(solution)/shard_map/ppermute | solution.py:92
  310.6 4.3 %convolution_reduce_fusion = f32[144]{0:T(256)S(1)} fusion(bf16[2048,1187]{0,1:T(8,128)(2,1)} %param.41, bf16[72,2048]{1,0:T(8,128)(2,1)S(1)} %get-tuple-element.19, bf16[72,2048]{1,0:T(8,128)(2,1)S(1)} %get-tuple-element.18), kind=kOutput, calls=%fused_computation.38 | convolution fusion | flops 701471488 | bytes 5452352 | tf_op jit(solution)/shard_map/dot_general | solution.py:228
  316.6 3.1 collective-permute-done.8
  321.5 3.3 collective-permute-done.9
  337.0 3.8 %collective-permute-start.13 = (f32[144]{0:T(256)S(1)}, f32[144]{0:T(256)S(1)}, u32[]{:S(2)}, u32[]{:S(2)}) collective-permute-start(f32[144]{0:T(256)S(1)} %max.30), channel_id=1, source_target_pairs={{0,64},{8,72},{16,80},{24,88},{32,96},{40,104},{48,112},{56,120},{... | collective-permute-start | bytes 1736 | tf_op jit(solution)/shard_map/ppermute | solution.py:81
  346.6 22.9 %all_to_all.34 = bf16[128,2,1024]{2,1,0:T(2,128)(2,1)S(1)} all-to-all(bf16[128,2,1024]{2,1,0:T(2,128)(2,1)S(1)} %reshape.460), channel_id=1, replica_groups=mesh['req'=16,'kv'=8] {'req','kv'}, dimensions={0} | all-to-all | bytes 1048576 | tf_op jit(solution)/shard_map/all_to_all | solution.py:102
  (145 shorter events, 68.8 us)
Async XLA Ops:
  7.2 33.6 %copy-start = (bf16[384,2048]{1,0:T(8,128)(2,1)S(1)}, bf16[384,2048]{1,0:T(8,128)(2,1)}, u32[]{:S(2)}) copy-start(bf16[384,2048]{1,0:T(8,128)(2,1)} %param.39) | copy-start | bytes 4718596
  13.5 24.7 %all-to-all-start = ((bf16[128,2,1024]{2,1,0:T(2,128)(2,1)}), bf16[128,2,1024]{2,1,0:T(2,128)(2,1)S(1)}, u32[]{:S(2)}, u32[]{:S(2)}) async-start(bf16[128,2,1024]{2,1,0:T(2,128)(2,1)} %reshape.458), calls=%async_computation | async-start | bytes 1048576 | tf_op jit(solution)/shard_map/all_to_all | solution.py:102
  24.7 44.3 %all-gather.9.cloned.1.call-start = ((), (), s32[]{:S(2)}) async-start(), calls=%async_computation.8 | async-start | bytes 4718592 | tf_op jit(solution)/shard_map/all_gather | solution.py:140
  42.9 58.5 %all-to-all-start.1 = ((bf16[16,48,2048]{2,1,0:T(8,128)(2,1)}), bf16[16,48,2048]{2,1,0:T(8,128)(2,1)}, u32[]{:S(2)}, u32[]{:S(2)}) async-start(bf16[16,48,2048]{2,1,0:T(8,128)(2,1)} %broadcast_in_dim.44), calls=%async_computation.1 | async-start | bytes 6291456 | tf_op jit(solution)/shard_map/all_to_all | solution.py:155
  47.4 4.5 %copy-start.12 = (s32[8]{0:T(128)S(1)}, s32[8]{0:T(128)}, u32[]{:S(2)}) copy-start(s32[8]{0:T(128)} %param.23) | copy-start | bytes 100
  47.4 159.4 %all-gather.5.cloned.1.call-start = ((), (), s32[]{:S(2)}) async-start(), calls=%async_computation.5 | async-start | bytes 6684672 | tf_op jit(solution)/shard_map/all_gather | solution.py:153
  52.0 20.2 %copy-start.11 = (f32[2048]{0:T(1024)S(1)}, f32[2048]{0:T(1024)}, u32[]{:S(2)}) copy-start(f32[2048]{0:T(1024)} %param.29) | copy-start | bytes 24580
  75.6 4.1 %copy-start.13 = (f32[128]{0:T(128)S(1)}, f32[128]{0:T(128)}, u32[]{:S(2)}) copy-start(f32[128]{0:T(128)} %param.34) | copy-start | bytes 1540
  76.0 5.2 %copy-start.14 = (f32[128]{0:T(128)S(1)}, f32[128]{0:T(128)}, u32[]{:S(2)}) copy-start(f32[128]{0:T(128)} %param.33) | copy-start | bytes 1540
  107.0 5.6 %copy-start.7 = (f32[1024,64]{1,0:T(8,128)S(1)}, f32[1024,64]{1,0:T(8,128)}, u32[]{:S(2)}) copy-start(f32[1024,64]{1,0:T(8,128)} %get-tuple-element.31) | copy-start | bytes 786436
  107.0 99.8 %all-to-all-start.2 = ((bf16[8,256,2048]{2,1,0:T(8,128)(2,1)}), bf16[8,256,2048]{2,1,0:T(8,128)(2,1)}, u32[]{:S(2)}, u32[]{:S(2)}) async-start(bf16[8,256,2048]{2,1,0:T(8,128)(2,1)} %broadcast_in_dim.49), calls=%async_computation.2 | async-start | bytes 16777216 | tf_op jit(solution)/shard_map/all_to_all | solution.py:142
  112.1 124.7 %all-gather.7.cloned.1.call-start = ((), (), s32[]{:S(2)}) async-start(), calls=%async_computation.6 | async-start | bytes 4718592 | tf_op jit(solution)/shard_map/all_gather | solution.py:210
  116.8 4.5 %copy-start.17 = (bf16[1,2048,128]{2,1,0:T(8,128)(2,1)S(1)}, bf16[1,2048,128]{2,1,0:T(8,128)(2,1)}, u32[]{:S(2)}) copy-start(bf16[1,2048,128]{2,1,0:T(8,128)(2,1)} %param.27) | copy-start | bytes 1572868
  207.8 135.1 %reduce-scatter.2.cloned.1.call-start = ((), (), s32[]{:S(2)}) async-start(), calls=%async_computation.7 | async-start | bytes 9437184 | tf_op jit(solution)/shard_map/reduce_scatter | solution.py:222
  216.1 35.0 %copy-start.18 = (f32[2048]{0:T(1024)S(1)}, f32[2048]{0:T(1024)}, u32[]{:S(2)}) copy-start(f32[2048]{0:T(1024)} %param.36) | copy-start | bytes 24580
  236.8 14.3 %copy-start.4 = (bf16[2,768,2048]{2,1,0:T(8,128)(2,1)S(1)}, bf16[2,768,2048]{2,1,0:T(8,128)(2,1)}, u32[]{:S(2)}) copy-start(bf16[2,768,2048]{2,1,0:T(8,128)(2,1)} %copy.57) | copy-start | bytes 18874372
  266.1 19.3 %copy-start.10 = (f32[2048]{0:T(1024)S(1)}, f32[2048]{0:T(1024)}, u32[]{:S(2)}) copy-start(f32[2048]{0:T(1024)} %param.40) | copy-start | bytes 24580
  268.5 1.3 collective-permute-start
  269.9 5.9 %collective-permute-start.1 = (f32[16,2048]{1,0:T(8,128)S(1)}, f32[16,2048]{1,0:T(8,128)S(1)}, u32[]{:S(2)}, u32[]{:S(2)}) collective-permute-start(f32[16,2048]{1,0:T(8,128)S(1)} %add.180), channel_id=1, source_target_pairs={{0,2},{1,3},{2,0},{3,1},{4,6},{5,7},{6,4},{7,5},{8,10},{9,11},{10,... | collective-permute-start | bytes 393224 | tf_op jit(solution)/shard_map/ppermute | solution.py:81
  275.9 8.6 %collective-permute-start.2 = (f32[16,2048]{1,0:T(8,128)S(1)}, f32[16,2048]{1,0:T(8,128)S(1)}, u32[]{:S(2)}, u32[]{:S(2)}) collective-permute-start(f32[16,2048]{1,0:T(8,128)S(1)} %add.181), channel_id=1, source_target_pairs={{0,4},{1,5},{2,6},{3,7},{4,0},{5,1},{6,2},{7,3},{8,12},{9,13},{10,... | collective-permute-start | bytes 393224 | tf_op jit(solution)/shard_map/ppermute | solution.py:81
  285.5 4.3 %collective-permute-start.3 = (bf16[9,2048]{1,0:T(8,128)(2,1)S(1)}, bf16[9,2048]{1,0:T(8,128)(2,1)S(1)}, u32[]{:S(2)}, u32[]{:S(2)}) collective-permute-start(bf16[9,2048]{1,0:T(8,128)(2,1)S(1)} %fusion.47), channel_id=1, source_target_pairs={{0,8},{8,0},{16,24},{24,16},{32,40},{40,32},{48,56},{56,48},{64,72... | collective-permute-start | bytes 110600 | tf_op jit(solution)/shard_map/ppermute | solution.py:92
  290.0 6.2 %collective-permute-start.4 = (bf16[18,2048]{1,0:T(8,128)(2,1)S(1)}, bf16[18,2048]{1,0:T(8,128)(2,1)S(1)}, u32[]{:S(2)}, u32[]{:S(2)}) collective-permute-start(bf16[18,2048]{1,0:T(8,128)(2,1)S(1)} %pad_maximum_fusion.4), channel_id=1, source_target_pairs={{0,16},{8,24},{16,0},{24,8},{32,48},{40,56},{48,32},{56,40},{64,80... | collective-permute-start | bytes 221192 | tf_op jit(solution)/shard_map/ppermute | solution.py:92
  296.3 5.4 %collective-permute-start.5 = (bf16[36,2048]{1,0:T(8,128)(2,1)S(1)}, bf16[36,2048]{1,0:T(8,128)(2,1)S(1)}, u32[]{:S(2)}, u32[]{:S(2)}) collective-permute-start(bf16[36,2048]{1,0:T(8,128)(2,1)S(1)} %pad_maximum_fusion.3), channel_id=1, source_target_pairs={{0,32},{8,40},{16,48},{24,56},{32,0},{40,8},{48,16},{56,24},{64,96... | collective-permute-start | bytes 442376 | tf_op jit(solution)/shard_map/ppermute | solution.py:92
  301.8 8.6 %collective-permute-start.6 = (bf16[72,2048]{1,0:T(8,128)(2,1)S(1)}, bf16[72,2048]{1,0:T(8,128)(2,1)S(1)}, u32[]{:S(2)}, u32[]{:S(2)}) collective-permute-start(bf16[72,2048]{1,0:T(8,128)(2,1)S(1)} %pad_maximum_fusion.2), channel_id=1, source_target_pairs={{0,64},{8,72},{16,80},{24,88},{32,96},{40,104},{48,112},{56,120},{... | collective-permute-start | bytes 884744 | tf_op jit(solution)/shard_map/ppermute | solution.py:92
  314.9 1.2 collective-permute-start.7
  316.1 3.6 collective-permute-start.8
  319.7 5.1 %collective-permute-start.9 = (f32[144]{0:T(256)S(1)}, f32[144]{0:T(256)S(1)}, u32[]{:S(2)}, u32[]{:S(2)}) collective-permute-start(f32[144]{0:T(256)S(1)} %max.26), channel_id=1, source_target_pairs={{0,4},{1,5},{2,6},{3,7},{4,0},{5,1},{6,2},{7,3},{8,12},{9,13},{10,... | collective-permute-start | bytes 1736 | tf_op jit(solution)/shard_map/ppermute | solution.py:81
  324.8 3.6 collective-permute-start.10
  328.3 5.1 %collective-permute-start.11 = (f32[144]{0:T(256)S(1)}, f32[144]{0:T(256)S(1)}, u32[]{:S(2)}, u32[]{:S(2)}) collective-permute-start(f32[144]{0:T(256)S(1)} %max.28), channel_id=1, source_target_pairs={{0,16},{8,24},{16,0},{24,8},{32,48},{40,56},{48,32},{56,40},{64,80... | collective-permute-start | bytes 1736 | tf_op jit(solution)/shard_map/ppermute | solution.py:81
  333.4 3.6 collective-permute-start.12
  337.0 5.4 %collective-permute-start.13 = (f32[144]{0:T(256)S(1)}, f32[144]{0:T(256)S(1)}, u32[]{:S(2)}, u32[]{:S(2)}) collective-permute-start(f32[144]{0:T(256)S(1)} %max.30), channel_id=1, source_target_pairs={{0,64},{8,72},{16,80},{24,88},{32,96},{40,104},{48,112},{56,120},{... | collective-permute-start | bytes 1736 | tf_op jit(solution)/shard_map/ppermute | solution.py:81
  342.3 30.0 %copy-start.1 = (bf16[384,2048]{1,0:T(8,128)(2,1)S(1)}, bf16[384,2048]{1,0:T(8,128)(2,1)}, u32[]{:S(2)}) copy-start(bf16[384,2048]{1,0:T(8,128)(2,1)} %param.39) | copy-start | bytes 4718596
  (8 other events, 22.2 us)
Sparse Core Ops, SparseCore 0:
  40.8 28.0 all-gather.8
  71.1 64.1 all-gather.4
  207.9 28.8 all-gather.6
  266.2 55.1 reduce-scatter.1

commit v11 on v9

--- a/solution.py
+++ b/solution.py
@@ -95,6 +95,37 @@
             [jnp.where(low, value, other), jnp.where(low, other, value)], axis=0
         )
         step *= 2
+    return value
+
+
+def radix_exchange(value, axis, step, radix):
+    size = lax.axis_size(axis)
+    got = [value]
+    for digit in range(1, radix):
+        pairs = [(i, i ^ (digit * step)) for i in range(size)]
+        got.append(lax.ppermute(value, axis, pairs))
+    return got
+
+
+def radix_reduce(value, axis, combine, radix):
+    size = lax.axis_size(axis)
+    step = 1
+    while step < size:
+        for other in radix_exchange(value, axis, step, radix)[1:]:
+            value = combine(value, other)
+        step *= radix
+    return value
+
+
+def radix_gather(value, axis, radix):
+    size = lax.axis_size(axis)
+    me = lax.axis_index(axis)
+    step = 1
+    while step < size:
+        got = radix_exchange(value, axis, step, radix)
+        order = jnp.arange(radix, dtype=jnp.int32) ^ ((me // step) % radix)
+        value = jnp.stack(got)[order].reshape((radix * value.shape[0],) + value.shape[1:])
+        step *= radix
     return value
 
 
@@ -219,13 +250,13 @@
     tail_rows = norm_rows(tail_out, final_gain).astype(jnp.bfloat16)
     local_peaks = jnp.max(
         jnp.dot(
-            butterfly_gather(tail_rows, "req"),
+            radix_gather(tail_rows, "req", 4),
             lm_head,
             preferred_element_type=jnp.float32,
         ),
         axis=1,
     )
-    max_logit = butterfly(butterfly(local_peaks, "kv", jnp.maximum), "req", jnp.maximum)
+    max_logit = radix_reduce(butterfly(local_peaks, "kv", jnp.maximum), "req", jnp.maximum, 4)
     ffn_part, max_logit = lax.optimization_barrier((ffn_part, max_logit))
     mine = lax.dynamic_slice_in_dim(resid, kv_index * rows_dev, rows_dev, axis=0)
     out_rows = (mine.astype(jnp.float32) + ffn_part).astype(jnp.bfloat16)

time: 353 us -> 342 us (0.969)
  waiting for transfers between devices: 146 us -> 139 us
    ppermute x10 -> x6, starting transfers between devices: 14.8 us -> 4.92 us  [butterfly(): value = combine(value, lax.ppermute(value, axis, pairs))]
    ppermute x10 -> x6, waiting for transfers between devices: 28.4 us -> 20.9 us  [butterfly(): value = combine(value, lax.ppermute(value, axis, pairs))]
    ppermute x4 -> x12, starting transfers between devices: 10.2 us -> 16.6 us  [radix_exchange(): got.append(lax.ppermute(value, axis, pairs))]
    ppermute x4 -> x12, waiting for transfers between devices: 14.4 us -> 15.6 us  [radix_exchange(): got.append(lax.ppermute(value, axis, pairs))]
  transfers between devices with their start and end apart: 20 -> 24, of which waited for: 19 -> 19; matrix products, arithmetic and copies ran while one was open for 21% -> 22% of each run, Pallas kernels for 0% -> 0%
where the time goes in v11:
time: 342 us; the launch traced here: 336 us
  waiting for transfers between devices  139 us (41%)
  matrix products  78.2 us (23%)
  starting transfers between devices  38.1 us (11%)
  local copies, waits for them, and re-layouts  23.8 us (7%)
  other arithmetic  22 us (6%)
  blocking collectives  19.8 us (6%)
  between operations  15.2 us (4%)
    all_gather x1, waiting for transfers between devices, shards(): lax.all_gather(pieces.reshape(tok_req, q_cols), 'kv', axis=1, tiled=True)  32.9 us
    all_gather x1, waiting for transfers between devices, shards(): rows_all = lax.all_gather(owner_rows, 'kv', axis=0, tiled=True)  23.6 us
    all_to_all x1, waiting for transfers between devices, shards(): lax.all_to_all(jnp.broadcast_to(o_proj[None], (kv_count,) + o_proj.shape)...  21 us
    ppermute x6, waiting for transfers between devices, butterfly(): value = combine(value, lax.ppermute(value, axis, pairs))  20.9 us
    all_to_all x1, blocking collectives, regroup(): lax.all_to_all(rows_in, ('req', 'kv'), split_axis=0, concat_axis=0, tiled...  19.8 us
    ppermute x12, starting transfers between devices, radix_exchange(): got.append(lax.ppermute(value, axis, pairs))  16.6 us
    sub x1, matrix products, prefill_full(): expd = jnp.exp(scores - row_peak)  15.9 us
    ppermute x12, waiting for transfers between devices, radix_exchange(): got.append(lax.ppermute(value, axis, pairs))  15.6 us
  transfers between devices with their start and end apart: 24, of which 19 were waited for; matrix products, arithmetic and copies ran while one was open for 22% of the time, Pallas kernels for 0%

profile of v11, /device:TPU:0, one launch (start us, length us, event | category | flops | bytes accessed | tf_op | source)
XLA Modules:
  0.0 336.4 jit_solution(17691168459678659464)
XLA Ops:
  8.3 2.6 gather_fusion
  13.4 11.1 %all-to-all-start = ((bf16[128,2,1024]{2,1,0:T(2,128)(2,1)}), bf16[128,2,1024]{2,1,0:T(2,128)(2,1)S(1)}, u32[]{:S(2)}, u32[]{:S(2)}) async-start(bf16[128,2,1024]{2,1,0:T(2,128)(2,1)} %reshape.509), calls=%async_computation | async-start | bytes 1048576 | tf_op jit(solution)/shard_map/all_to_all | solution.py:133
  25.3 12.8 %all-to-all-done = bf16[128,2,1024]{2,1,0:T(2,128)(2,1)S(1)} async-done(((bf16[128,2,1024]{2,1,0:T(2,128)(2,1)}), bf16[128,2,1024]{2,1,0:T(2,128)(2,1)S(1)}, u32[]{:S(2)}, u32[]{:S(2)}) %all-to-all-start) | async-done | bytes 524320 | tf_op jit(solution)/shard_map/all_to_all | solution.py:133
  43.9 5.6 %broadcast_in_dim.46 = bf16[8,256,2048]{2,1,0:T(8,128)(2,1)} broadcast(bf16[256,2048]{1,0:T(8,128)(2,1)} %param.35), dimensions={1,2} | broadcast | bytes 9437184 | tf_op jit(solution)/shard_map/broadcast_in_dim | solution.py:174
  49.5 5.1 %all-to-all-start.1 = ((bf16[8,256,2048]{2,1,0:T(8,128)(2,1)}), bf16[8,256,2048]{2,1,0:T(8,128)(2,1)}, u32[]{:S(2)}, u32[]{:S(2)}) async-start(bf16[8,256,2048]{2,1,0:T(8,128)(2,1)} %broadcast_in_dim.46), calls=%async_computation.1 | async-start | bytes 16777216 | tf_op jit(solution)/shard_map/all_to_all | solution.py:173
  57.6 4.1 %fusion.4 = pred[1016,3064]{1,0:T(8,128)(4,1)} fusion(s32[3064]{0:T(1024)S(1)} %iota_add_fusion, pred[3064]{0:T(1024)(128)(4,1)S(1)} %get-tuple-element.32, pred[3064]{0:T(1024)(128)(4,1)S(1)} %get-tuple-element.33), kind=kLoop, calls=%fused_computation.17 | loop fusion | flops 6226048 | bytes 3131408 | tf_op jit(solution)/shard_map/jit(_where)/select_n | solution.py:45
  61.7 23.6 %all-gather.9.cloned.1.call-done = bf16[1024,2048]{1,0:T(8,128)(2,1)} async-done(((bf16[128,2048]{1,0:T(8,128)(2,1)}), bf16[1024,2048]{1,0:T(8,128)(2,1)}) %all-gather.9.cloned.1.call-update) | async-done | bytes 4194320 | tf_op jit(solution)/shard_map/all_gather | solution.py:171
  85.3 3.2 fusion.10
  93.9 3.7 %multiply_reduce_fusion.1 = (f32[1024]{0:T(1024)S(1)}, f32[1024,128]{0,1:T(8,128)S(1)}) fusion(bf16[1024,2048]{1,0:T(8,128)(2,1)} %copy-done.3, bf16[2048,128]{1,0:T(8,128)(2,1)S(1)} %copy-done.6), kind=kOutput, calls=%fused_computation.72 | convolution fusion | flops 537132032 | bytes 5246976 | tf_op jit(solution)/shard_map/dot_general | solution.py:192
  103.4 3.9 %convolution_convert_fusion = bf16[1024,128]{1,0:T(8,128)(2,1)S(1)} fusion(bf16[1024,2048]{1,0:T(8,128)(2,1)} %copy-done.3, bf16[2048,128]{1,0:T(8,128)(2,1)S(1)} %copy-done.14), kind=kOutput, calls=%fused_computation.47 | convolution fusion | flops 537001984 | bytes 4980736 | tf_op jit(solution)/shard_map/dot_general | solution.py:193
  108.1 15.9 %fusion.92 = (f32[2,1016]{1,0:T(2,128)S(1)}, f32[2,1016,3064]{2,1,0:T(8,128)}) fusion(pred[1016,3064]{1,0:T(8,128)(4,1)} %fusion.4, bf16[1016,128]{1,0:T(8,128)(2,1)S(1)} %copy.49, bf16[2048,128]{1,0:T(8,128)(2,1)S(1)} %bitcast.133, bf16[1024,2,64]{2,0,1:T(8,128)(2,1)S(1)} %get-tuple-element.14, bf16[1024,2,64]{2,0,1:T(8,128)(2,1)S(1)} %get-tuple-element.15), kind=kOutput, calls=%fused_computation.168 | convolution fusion | flops 1621384704 | bytes 29334016 | tf_op jit(solution)/shard_map/sub | solution.py:48
  124.0 12.3 %fusion.32 = bf16[1016,2,128]{2,0,1:T(8,128)(2,1)S(1)} fusion(f32[2,1016,3064]{2,1,0:T(8,128)} %get-tuple-element.29, f32[2,1016]{1,0:T(2,128)S(1)} %get-tuple-element.28, bf16[1016,128]{1,0:T(8,128)(2,1)S(1)} %slice.74, bf16[2048,128]{1,0:T(8,128)(2,1)S(1)} %bitcast.134), kind=kOutput, calls=%fused_computation.46 | convolution fusion | flops 1608149248 | bytes 26216896 | tf_op jit(solution)/shard_map/gck,kd->cgd/dot_general | solution.py:50
  136.4 21.0 %all-to-all-done.1 = bf16[8,256,2048]{2,1,0:T(8,128)(2,1)} async-done(((bf16[8,256,2048]{2,1,0:T(8,128)(2,1)}), bf16[8,256,2048]{2,1,0:T(8,128)(2,1)}, u32[]{:S(2)}, u32[]{:S(2)}) %all-to-all-start.1) | async-done | bytes 8388640 | tf_op jit(solution)/shard_map/all_to_all | solution.py:173
  157.4 12.5 %all-gather.5.cloned.1.call-done = bf16[3,768,2048]{2,1,0:T(8,128)(2,1)} async-done(((bf16[3,48,2048]{2,1,0:T(8,128)(2,1)}), bf16[3,768,2048]{2,1,0:T(8,128)(2,1)}) %all-gather.5.cloned.1.call-update) | async-done | bytes 9437200 | tf_op jit(solution)/shard_map/all_gather | solution.py:185
  171.0 32.9 %all-gather.7.cloned.1.call-done = bf16[1024,2048]{0,1:T(8,128)(2,1)} async-done(((bf16[1024,256]{0,1:T(8,128)(2,1)}), bf16[1024,2048]{0,1:T(8,128)(2,1)}) %all-gather.7.cloned.1.call-update) | async-done | bytes 4194320 | tf_op jit(solution)/shard_map/all_gather | solution.py:234
  203.9 14.5 %fusion.7 = (f32[1024]{0:T(1024)S(1)}, bf16[1024,2048]{1,0:T(8,128)(2,1)S(1)}) fusion(bf16[1024,2048]{0,1:T(8,128)(2,1)} %all-gather.7.cloned.1.call-done, bf16[2048,2048]{1,0:T(8,128)(2,1)} %bitcast.25, bf16[1024,2048]{1,0:T(8,128)(2,1)} %all-gather.9.cloned.1.call-done), kind=kOutput, calls=%fused_computation.22 | convolution fusion | flops 8602516480 | bytes 20975616 | tf_op jit(solution)/shard_map/dot_general | solution.py:236
  218.5 7.0 %fusion.18 = f32[1024,768]{1,0:T(8,128)S(1)} fusion(bf16[3,768,2048]{2,1,0:T(8,128)(2,1)} %all-gather.5.cloned.1.call-done, bf16[1024,2048]{1,0:T(8,128)(2,1)S(1)} %get-tuple-element.31, f32[2048]{0:T(1024)S(1)} %copy-done.17, f32[1024]{0:T(1024)S(1)} %add_rsqrt_fusion.1), kind=kOutput, calls=%fused_computation.33 | convolution fusion | flops 3229614080 | bytes 10498048 | tf_op jit(solution)/shard_map/dot_general | solution.py:241
  225.6 3.9 %multiply_convert_fusion = bf16[1024,768]{1,0:T(8,128)(2,1)S(1)} fusion(f32[1024,768]{1,0:T(8,128)S(1)} %fusion.18, bf16[3,768,2048]{2,1,0:T(8,128)(2,1)S(1)} %bitcast.120, bf16[1024,2048]{1,0:T(8,128)(2,1)S(1)} %get-tuple-element.31, f32[2048]{0:T(1024)S(1)} %copy-done.17, f32[1024]{0:T(1024)S(1)} %add_rsqrt_fusion.1), kind=kOutput, calls=%fused_computation.37 | convolution fusion | flops 3234332672 | bytes 12070912 | tf_op jit(solution)/shard_map/dot_general | solution.py:240
  229.5 5.7 %fusion.16 = f32[1024,2048]{1,0:T(8,128)} fusion(bf16[1024,768]{1,0:T(8,128)(2,1)S(1)} %multiply_convert_fusion, bf16[3,768,2048]{2,1,0:T(8,128)(2,1)S(1)} %bitcast.120), kind=kOutput, calls=%fused_computation.31 | convolution fusion | flops 3221225472 | bytes 13107200 | tf_op jit(solution)/shard_map/dot_general | solution.py:245
  235.2 2.4 fusion.14
  239.7 5.2 %collective-permute-done.1 = f32[16,2048]{1,0:T(8,128)S(1)} collective-permute-done((f32[16,2048]{1,0:T(8,128)S(1)}, f32[16,2048]{1,0:T(8,128)S(1)}, u32[]{:S(2)}, u32[]{:S(2)}) %collective-permute-start.1) | collective-permute-done | bytes 131104 | tf_op jit(solution)/shard_map/ppermute | solution.py:81
  246.7 6.8 %collective-permute-done.2 = f32[16,2048]{1,0:T(8,128)S(1)} collective-permute-done((f32[16,2048]{1,0:T(8,128)S(1)}, f32[16,2048]{1,0:T(8,128)S(1)}, u32[]{:S(2)}, u32[]{:S(2)}) %collective-permute-start.2) | collective-permute-done | bytes 131104 | tf_op jit(solution)/shard_map/ppermute | solution.py:81
  254.6 2.8 collective-permute-start.5
  263.9 3.0 collective-permute-start.8
  268.2 3.4 %collective-permute-done.8 = bf16[36,2048]{1,0:T(8,128)(2,1)S(1)} collective-permute-done((bf16[36,2048]{1,0:T(8,128)(2,1)S(1)}, bf16[36,2048]{1,0:T(8,128)(2,1)S(1)}, u32[]{:S(2)}, u32[]{:S(2)}) %collective-permute-start.8) | collective-permute-done | bytes 147488 | tf_op jit(solution)/shard_map/ppermute | solution.py:106
  274.6 4.3 %convolution_reduce_fusion = f32[144]{0:T(256)S(1)} fusion(bf16[144,2048]{1,0:T(8,128)(2,1)S(1)} %reshape.451, bf16[2048,1187]{0,1:T(8,128)(2,1)} %param.41), kind=kOutput, calls=%fused_computation.48 | convolution fusion | flops 700291840 | bytes 5452352 | tf_op jit(solution)/shard_map/dot_general | solution.py:252
  280.5 3.3 collective-permute-done.10
  285.4 3.5 %collective-permute-done.11 = f32[144]{0:T(256)S(1)} collective-permute-done((f32[144]{0:T(256)S(1)}, f32[144]{0:T(256)S(1)}, u32[]{:S(2)}, u32[]{:S(2)}) %collective-permute-start.11) | collective-permute-done | bytes 608 | tf_op jit(solution)/shard_map/ppermute | solution.py:81
  295.4 2.4 collective-permute-start.17
  300.3 2.6 collective-permute-done.16
  307.1 19.8 %all_to_all.29 = bf16[128,2,1024]{2,1,0:T(2,128)(2,1)S(1)} all-to-all(bf16[128,2,1024]{2,1,0:T(2,128)(2,1)S(1)} %reshape.511), channel_id=1, replica_groups=mesh['req'=16,'kv'=8] {'req','kv'}, dimensions={0} | all-to-all | bytes 1048576 | tf_op jit(solution)/shard_map/all_to_all | solution.py:133
  327.3 2.4 scatter_custom_fusion.1
  (156 shorter events, 58.0 us)
Async XLA Ops:
  7.2 35.8 %copy-start = (bf16[384,2048]{1,0:T(8,128)(2,1)S(1)}, bf16[384,2048]{1,0:T(8,128)(2,1)}, u32[]{:S(2)}) copy-start(bf16[384,2048]{1,0:T(8,128)(2,1)} %param.39) | copy-start | bytes 4718596
  13.4 24.7 %all-to-all-start = ((bf16[128,2,1024]{2,1,0:T(2,128)(2,1)}), bf16[128,2,1024]{2,1,0:T(2,128)(2,1)S(1)}, u32[]{:S(2)}, u32[]{:S(2)}) async-start(bf16[128,2,1024]{2,1,0:T(2,128)(2,1)} %reshape.509), calls=%async_computation | async-start | bytes 1048576 | tf_op jit(solution)/shard_map/all_to_all | solution.py:133
  24.5 60.7 %all-gather.9.cloned.1.call-start = ((), (), s32[]{:S(2)}) async-start(), calls=%async_computation.7 | async-start | bytes 4718592 | tf_op jit(solution)/shard_map/all_gather | solution.py:171
  40.6 129.3 %all-gather.5.cloned.1.call-start = ((), (), s32[]{:S(2)}) async-start(), calls=%async_computation.4 | async-start | bytes 10027008 | tf_op jit(solution)/shard_map/all_gather | solution.py:185
  49.5 107.9 %all-to-all-start.1 = ((bf16[8,256,2048]{2,1,0:T(8,128)(2,1)}), bf16[8,256,2048]{2,1,0:T(8,128)(2,1)}, u32[]{:S(2)}, u32[]{:S(2)}) async-start(bf16[8,256,2048]{2,1,0:T(8,128)(2,1)} %broadcast_in_dim.46), calls=%async_computation.1 | async-start | bytes 16777216 | tf_op jit(solution)/shard_map/all_to_all | solution.py:173
  54.7 149.2 %all-gather.7.cloned.1.call-start = ((), (), s32[]{:S(2)}) async-start(), calls=%async_computation.5 | async-start | bytes 4718592 | tf_op jit(solution)/shard_map/all_gather | solution.py:234
  55.6 32.9 %copy-start.9 = (f32[2048]{0:T(1024)S(1)}, f32[2048]{0:T(1024)}, u32[]{:S(2)}) copy-start(f32[2048]{0:T(1024)} %param.29) | copy-start | bytes 24580
  108.1 15.9 %copy-start.16 = (bf16[1,2048,128]{2,1,0:T(8,128)(2,1)S(1)}, bf16[1,2048,128]{2,1,0:T(8,128)(2,1)}, u32[]{:S(2)}) copy-start(bf16[1,2048,128]{2,1,0:T(8,128)(2,1)} %param.28) | copy-start | bytes 1572868
  170.9 47.5 %copy-start.17 = (f32[2048]{0:T(1024)S(1)}, f32[2048]{0:T(1024)}, u32[]{:S(2)}) copy-start(f32[2048]{0:T(1024)} %param.36) | copy-start | bytes 24580
  171.0 132.5 %reduce-scatter.2.cloned.1.call-start = ((), (), s32[]{:S(2)}) async-start(), calls=%async_computation.6 | async-start | bytes 9437184 | tf_op jit(solution)/shard_map/reduce_scatter | solution.py:246
  203.9 21.6 %slice-start = ((s8[9437184]{0:T(1024)(128)(4,1)}), s8[1048576]{0:T(1024)(128)(4,1)S(1)}, s32[]{:S(2)}) async-start(s8[9437184]{0:T(1024)(128)(4,1)} %bitcast.119), calls=%async_computation.8 | async-start | bytes 2097152
  203.9 21.6 %slice-start.1 = ((s8[9437184]{0:T(1024)(128)(4,1)}), s8[4194304]{0:T(1024)(128)(4,1)S(1)}, s32[]{:S(2)}) async-start(s8[9437184]{0:T(1024)(128)(4,1)} %bitcast.119), calls=%async_computation.9 | async-start | bytes 8388608
  235.2 19.3 %copy-start.8 = (f32[2048]{0:T(1024)S(1)}, f32[2048]{0:T(1024)}, u32[]{:S(2)}) copy-start(f32[2048]{0:T(1024)} %param.40) | copy-start | bytes 24580
  237.6 1.3 collective-permute-start
  239.0 5.9 %collective-permute-start.1 = (f32[16,2048]{1,0:T(8,128)S(1)}, f32[16,2048]{1,0:T(8,128)S(1)}, u32[]{:S(2)}, u32[]{:S(2)}) collective-permute-start(f32[16,2048]{1,0:T(8,128)S(1)} %add.188), channel_id=1, source_target_pairs={{0,2},{1,3},{2,0},{3,1},{4,6},{5,7},{6,4},{7,5},{8,10},{9,11},{10,... | collective-permute-start | bytes 393224 | tf_op jit(solution)/shard_map/ppermute | solution.py:81
  244.9 8.6 %collective-permute-start.2 = (f32[16,2048]{1,0:T(8,128)S(1)}, f32[16,2048]{1,0:T(8,128)S(1)}, u32[]{:S(2)}, u32[]{:S(2)}) collective-permute-start(f32[16,2048]{1,0:T(8,128)S(1)} %add.189), channel_id=1, source_target_pairs={{0,4},{1,5},{2,6},{3,7},{4,0},{5,1},{6,2},{7,3},{8,12},{9,13},{10,... | collective-permute-start | bytes 393224 | tf_op jit(solution)/shard_map/ppermute | solution.py:81
  254.6 6.3 %collective-permute-start.5 = (bf16[9,2048]{1,0:T(8,128)(2,1)S(1)}, bf16[9,2048]{1,0:T(8,128)(2,1)S(1)}, u32[]{:S(2)}, u32[]{:S(2)}) collective-permute-start(bf16[9,2048]{1,0:T(8,128)(2,1)S(1)} %fusion.56), channel_id=1, source_target_pairs={{0,24},{8,16},{16,8},{24,0},{32,56},{40,48},{48,40},{56,32},{64,88... | collective-permute-start | bytes 110600 | tf_op jit(solution)/shard_map/ppermute | solution.py:106
  257.4 5.8 %collective-permute-start.4 = (bf16[9,2048]{1,0:T(8,128)(2,1)S(1)}, bf16[9,2048]{1,0:T(8,128)(2,1)S(1)}, u32[]{:S(2)}, u32[]{:S(2)}) collective-permute-start(bf16[9,2048]{1,0:T(8,128)(2,1)S(1)} %fusion.56), channel_id=1, source_target_pairs={{0,16},{8,24},{16,0},{24,8},{32,48},{40,56},{48,32},{56,40},{64,80... | collective-permute-start | bytes 110600 | tf_op jit(solution)/shard_map/ppermute | solution.py:106
  258.2 5.0 %collective-permute-start.3 = (bf16[9,2048]{1,0:T(8,128)(2,1)S(1)}, bf16[9,2048]{1,0:T(8,128)(2,1)S(1)}, u32[]{:S(2)}, u32[]{:S(2)}) collective-permute-start(bf16[9,2048]{1,0:T(8,128)(2,1)S(1)} %fusion.56), channel_id=1, source_target_pairs={{0,8},{8,0},{16,24},{24,16},{32,40},{40,32},{48,56},{56,48},{64,72... | collective-permute-start | bytes 110600 | tf_op jit(solution)/shard_map/ppermute | solution.py:106
  263.9 7.7 %collective-permute-start.8 = (bf16[36,2048]{1,0:T(8,128)(2,1)S(1)}, bf16[36,2048]{1,0:T(8,128)(2,1)S(1)}, u32[]{:S(2)}, u32[]{:S(2)}) collective-permute-start(bf16[36,2048]{1,0:T(8,128)(2,1)S(1)} %reshape.450), channel_id=1, source_target_pairs={{0,96},{8,104},{16,112},{24,120},{32,64},{40,72},{48,80},{56,88},{... | collective-permute-start | bytes 442376 | tf_op jit(solution)/shard_map/ppermute | solution.py:106
  266.9 6.8 %collective-permute-start.7 = (bf16[36,2048]{1,0:T(8,128)(2,1)S(1)}, bf16[36,2048]{1,0:T(8,128)(2,1)S(1)}, u32[]{:S(2)}, u32[]{:S(2)}) collective-permute-start(bf16[36,2048]{1,0:T(8,128)(2,1)S(1)} %reshape.450), channel_id=1, source_target_pairs={{0,64},{8,72},{16,80},{24,88},{32,96},{40,104},{48,112},{56,120},{... | collective-permute-start | bytes 442376 | tf_op jit(solution)/shard_map/ppermute | solution.py:106
  267.6 6.2 %collective-permute-start.6 = (bf16[36,2048]{1,0:T(8,128)(2,1)S(1)}, bf16[36,2048]{1,0:T(8,128)(2,1)S(1)}, u32[]{:S(2)}, u32[]{:S(2)}) collective-permute-start(bf16[36,2048]{1,0:T(8,128)(2,1)S(1)} %reshape.450), channel_id=1, source_target_pairs={{0,32},{8,40},{16,48},{24,56},{32,0},{40,8},{48,16},{56,24},{64,96... | collective-permute-start | bytes 442376 | tf_op jit(solution)/shard_map/ppermute | solution.py:106
  278.9 1.2 collective-permute-start.9
  280.1 3.7 %collective-permute-start.10 = (f32[144]{0:T(256)S(1)}, f32[144]{0:T(256)S(1)}, u32[]{:S(2)}, u32[]{:S(2)}) collective-permute-start(f32[144]{0:T(256)S(1)} %max.31), channel_id=1, source_target_pairs={{0,2},{1,3},{2,0},{3,1},{4,6},{5,7},{6,4},{7,5},{8,10},{9,11},{10,... | collective-permute-start | bytes 1736 | tf_op jit(solution)/shard_map/ppermute | solution.py:81
  283.8 5.2 %collective-permute-start.11 = (f32[144]{0:T(256)S(1)}, f32[144]{0:T(256)S(1)}, u32[]{:S(2)}, u32[]{:S(2)}) collective-permute-start(f32[144]{0:T(256)S(1)} %max.32), channel_id=1, source_target_pairs={{0,4},{1,5},{2,6},{3,7},{4,0},{5,1},{6,2},{7,3},{8,12},{9,13},{10,... | collective-permute-start | bytes 1736 | tf_op jit(solution)/shard_map/ppermute | solution.py:81
  288.9 4.8 %collective-permute-start.14 = (f32[144]{0:T(256)S(1)}, f32[144]{0:T(256)S(1)}, u32[]{:S(2)}, u32[]{:S(2)}) collective-permute-start(f32[144]{0:T(256)S(1)} %max.33), channel_id=1, source_target_pairs={{0,24},{8,16},{16,8},{24,0},{32,56},{40,48},{48,40},{56,32},{64,88... | collective-permute-start | bytes 1736 | tf_op jit(solution)/shard_map/ppermute | solution.py:106
  290.3 5.1 %collective-permute-start.13 = (f32[144]{0:T(256)S(1)}, f32[144]{0:T(256)S(1)}, u32[]{:S(2)}, u32[]{:S(2)}) collective-permute-start(f32[144]{0:T(256)S(1)} %max.33), channel_id=1, source_target_pairs={{0,16},{8,24},{16,0},{24,8},{32,48},{40,56},{48,32},{56,40},{64,80... | collective-permute-start | bytes 1736 | tf_op jit(solution)/shard_map/ppermute | solution.py:106
  291.2 4.2 %collective-permute-start.12 = (f32[144]{0:T(256)S(1)}, f32[144]{0:T(256)S(1)}, u32[]{:S(2)}, u32[]{:S(2)}) collective-permute-start(f32[144]{0:T(256)S(1)} %max.33), channel_id=1, source_target_pairs={{0,8},{8,0},{16,24},{24,16},{32,40},{40,32},{48,56},{56,48},{64,72... | collective-permute-start | bytes 1736 | tf_op jit(solution)/shard_map/ppermute | solution.py:106
  295.4 4.9 %collective-permute-start.17 = (f32[144]{0:T(256)S(1)}, f32[144]{0:T(256)S(1)}, u32[]{:S(2)}, u32[]{:S(2)}) collective-permute-start(f32[144]{0:T(256)S(1)} %maximum_maximum_fusion.1), channel_id=1, source_target_pairs={{0,96},{8,104},{16,112},{24,120},{32,64},{40,72},{48,80},{56,88},{... | collective-permute-start | bytes 1736 | tf_op jit(solution)/shard_map/ppermute | solution.py:106
  297.8 5.1 %collective-permute-start.16 = (f32[144]{0:T(256)S(1)}, f32[144]{0:T(256)S(1)}, u32[]{:S(2)}, u32[]{:S(2)}) collective-permute-start(f32[144]{0:T(256)S(1)} %maximum_maximum_fusion.1), channel_id=1, source_target_pairs={{0,64},{8,72},{16,80},{24,88},{32,96},{40,104},{48,112},{56,120},{... | collective-permute-start | bytes 1736 | tf_op jit(solution)/shard_map/ppermute | solution.py:106
  298.4 4.4 %collective-permute-start.15 = (f32[144]{0:T(256)S(1)}, f32[144]{0:T(256)S(1)}, u32[]{:S(2)}, u32[]{:S(2)}) collective-permute-start(f32[144]{0:T(256)S(1)} %maximum_maximum_fusion.1), channel_id=1, source_target_pairs={{0,32},{8,40},{16,48},{24,56},{32,0},{40,8},{48,16},{56,24},{64,96... | collective-permute-start | bytes 1736 | tf_op jit(solution)/shard_map/ppermute | solution.py:106
  302.9 26.8 %copy-start.1 = (bf16[384,2048]{1,0:T(8,128)(2,1)S(1)}, bf16[384,2048]{1,0:T(8,128)(2,1)}, u32[]{:S(2)}) copy-start(bf16[384,2048]{1,0:T(8,128)(2,1)} %param.39) | copy-start | bytes 4718596
  (13 other events, 56.0 us)
Sparse Core Ops, SparseCore 0:
  40.7 44.5 all-gather.8
  87.4 82.4 all-gather.4
  172.2 31.6 all-gather.6
  235.3 55.1 reduce-scatter.1

commit v12 on v11

--- a/solution.py
+++ b/solution.py
@@ -125,6 +125,20 @@
         got = radix_exchange(value, axis, step, radix)
         order = jnp.arange(radix, dtype=jnp.int32) ^ ((me // step) % radix)
         value = jnp.stack(got)[order].reshape((radix * value.shape[0],) + value.shape[1:])
+        step *= radix
+    return value
+
+
+def mixed_reduce(value, axis, combine, radices):
+    me = lax.axis_index(axis)
+    step = 1
+    for radix in radices:
+        got = radix_exchange(value, axis, step, radix)
+        order = jnp.arange(radix, dtype=jnp.int32) ^ ((me // step) % radix)
+        members = jnp.stack(got)[order]
+        while members.shape[0] > 1:
+            members = combine(members[0::2], members[1::2])
+        value = members[0]
         step *= radix
     return value
 
@@ -245,7 +259,7 @@
     down_part = jnp.dot(hidden_act, down_w, preferred_element_type=jnp.float32)
     ffn_part = lax.psum_scatter(down_part, "kv", scatter_dimension=0, tiled=True)
     tail_part = jnp.dot(hidden_act[tok_req - tail_pad :], down_w, preferred_element_type=jnp.float32)
-    tail_sum = butterfly(tail_part, "kv", jnp.add)[tail_pad - tail_count :]
+    tail_sum = mixed_reduce(tail_part, "kv", jnp.add, (2, 4))[tail_pad - tail_count :]
     tail_out = (resid[fresh_count - 1 :].astype(jnp.float32) + tail_sum).astype(jnp.bfloat16)
     tail_rows = norm_rows(tail_out, final_gain).astype(jnp.bfloat16)
     local_peaks = jnp.max(
@@ -256,7 +270,7 @@
         ),
         axis=1,
     )
-    max_logit = radix_reduce(butterfly(local_peaks, "kv", jnp.maximum), "req", jnp.maximum, 4)
+    max_logit = radix_reduce(mixed_reduce(local_peaks, "kv", jnp.maximum, (2, 4)), "req", jnp.maximum, 4)
     ffn_part, max_logit = lax.optimization_barrier((ffn_part, max_logit))
     mine = lax.dynamic_slice_in_dim(resid, kv_index * rows_dev, rows_dev, axis=0)
     out_rows = (mine.astype(jnp.float32) + ffn_part).astype(jnp.bfloat16)

time: 342 us -> 341 us (level)
  waiting for transfers between devices: 139 us -> 131 us
  starting transfers between devices: 38.1 us -> 42.4 us
    ppermute x6 -> x0, waiting for transfers between devices: 20.9 us -> none  [butterfly(): value = combine(value, lax.ppermute(value, axis, pairs))]
    ppermute x12 -> x20, waiting for transfers between devices: 15.6 us -> 28.7 us  [radix_exchange(): got.append(lax.ppermute(value, axis, pairs))]
    ppermute x12 -> x20, starting transfers between devices: 16.6 us -> 25.5 us  [radix_exchange(): got.append(lax.ppermute(value, axis, pairs))]
    ppermute x6 -> x0, starting transfers between devices: 4.92 us -> none  [butterfly(): value = combine(value, lax.ppermute(value, axis, pairs))]
  transfers between devices with their start and end apart: 24 -> 26, of which waited for: 19 -> 20; matrix products, arithmetic and copies ran while one was open for 22% -> 23% of each run, Pallas kernels for 0% -> 0%
where the time goes in v12:
time: 341 us; the launch traced here: 336 us
  waiting for transfers between devices  131 us (38%)
  matrix products  78 us (23%)
  starting transfers between devices  42.4 us (12%)
  local copies, waits for them, and re-layouts  26.3 us (8%)
  other arithmetic  22.3 us (7%)
  blocking collectives  20.2 us (6%)
  between operations  15.3 us (4%)
    all_gather x1, waiting for transfers between devices, shards(): lax.all_gather(pieces.reshape(tok_req, q_cols), 'kv', axis=1, tiled=True)  32.9 us
    ppermute x20, waiting for transfers between devices, radix_exchange(): got.append(lax.ppermute(value, axis, pairs))  28.7 us
    ppermute x20, starting transfers between devices, radix_exchange(): got.append(lax.ppermute(value, axis, pairs))  25.5 us
    all_gather x1, waiting for transfers between devices, shards(): rows_all = lax.all_gather(owner_rows, 'kv', axis=0, tiled=True)  23.3 us
    all_to_all x1, waiting for transfers between devices, shards(): lax.all_to_all(jnp.broadcast_to(o_proj[None], (kv_count,) + o_proj.shape)...  21.1 us
    all_to_all x1, blocking collectives, regroup(): lax.all_to_all(rows_in, ('req', 'kv'), split_axis=0, concat_axis=0, tiled...  20.2 us
    sub x1, matrix products, prefill_full(): expd = jnp.exp(scores - row_peak)  15.9 us
    dot_general x1, matrix products, shards(): jnp.dot(attended, o_full, preferred_element_type=jnp.float32)  14.5 us
  transfers between devices with their start and end apart: 26, of which 20 were waited for; matrix products, arithmetic and copies ran while one was open for 23% of the time, Pallas kernels for 0%

profile of v12, /device:TPU:0, one launch (start us, length us, event | category | flops | bytes accessed | tf_op | source)
XLA Modules:
  0.0 335.8 jit_solution(1163954709671219122)
XLA Ops:
  8.3 2.6 gather_fusion
  13.5 11.1 %all-to-all-start = ((bf16[128,2,1024]{2,1,0:T(2,128)(2,1)}), bf16[128,2,1024]{2,1,0:T(2,128)(2,1)S(1)}, u32[]{:S(2)}, u32[]{:S(2)}) async-start(bf16[128,2,1024]{2,1,0:T(2,128)(2,1)} %reshape.574), calls=%async_computation | async-start | bytes 1048576 | tf_op jit(solution)/shard_map/all_to_all | solution.py:147
  25.5 12.8 %all-to-all-done = bf16[128,2,1024]{2,1,0:T(2,128)(2,1)S(1)} async-done(((bf16[128,2,1024]{2,1,0:T(2,128)(2,1)}), bf16[128,2,1024]{2,1,0:T(2,128)(2,1)S(1)}, u32[]{:S(2)}, u32[]{:S(2)}) %all-to-all-start) | async-done | bytes 524320 | tf_op jit(solution)/shard_map/all_to_all | solution.py:147
  44.1 5.6 %broadcast_in_dim.46 = bf16[8,256,2048]{2,1,0:T(8,128)(2,1)} broadcast(bf16[256,2048]{1,0:T(8,128)(2,1)} %param.35), dimensions={1,2} | broadcast | bytes 9437184 | tf_op jit(solution)/shard_map/broadcast_in_dim | solution.py:188
  49.7 5.1 %all-to-all-start.1 = ((bf16[8,256,2048]{2,1,0:T(8,128)(2,1)}), bf16[8,256,2048]{2,1,0:T(8,128)(2,1)}, u32[]{:S(2)}, u32[]{:S(2)}) async-start(bf16[8,256,2048]{2,1,0:T(8,128)(2,1)} %broadcast_in_dim.46), calls=%async_computation.1 | async-start | bytes 16777216 | tf_op jit(solution)/shard_map/all_to_all | solution.py:187
  58.1 4.0 %fusion.4 = pred[1016,3064]{1,0:T(8,128)(4,1)} fusion(s32[3064]{0:T(1024)S(1)} %iota_add_fusion, pred[3064]{0:T(1024)(128)(4,1)S(1)} %get-tuple-element.34, pred[3064]{0:T(1024)(128)(4,1)S(1)} %get-tuple-element.35), kind=kLoop, calls=%fused_computation.21 | loop fusion | flops 6226048 | bytes 3131408 | tf_op jit(solution)/shard_map/jit(_where)/select_n | solution.py:45
  62.1 23.3 %all-gather.9.cloned.1.call-done = bf16[1024,2048]{1,0:T(8,128)(2,1)} async-done(((bf16[128,2048]{1,0:T(8,128)(2,1)}), bf16[1024,2048]{1,0:T(8,128)(2,1)}) %all-gather.9.cloned.1.call-update) | async-done | bytes 4194320 | tf_op jit(solution)/shard_map/all_gather | solution.py:185
  85.4 3.2 fusion.10
  90.1 2.3 multiply_reduce_fusion
  94.0 3.7 %multiply_reduce_fusion.1 = (f32[1024]{0:T(1024)S(1)}, f32[1024,128]{0,1:T(8,128)S(1)}) fusion(bf16[1024,2048]{1,0:T(8,128)(2,1)} %copy-done.3, bf16[2048,128]{1,0:T(8,128)(2,1)S(1)} %copy-done.6), kind=kOutput, calls=%fused_computation.77 | convolution fusion | flops 537132032 | bytes 5246976 | tf_op jit(solution)/shard_map/dot_general | solution.py:206
  103.5 3.9 %convolution_convert_fusion = bf16[1024,128]{1,0:T(8,128)(2,1)S(1)} fusion(bf16[1024,2048]{1,0:T(8,128)(2,1)} %copy-done.3, bf16[2048,128]{1,0:T(8,128)(2,1)S(1)} %copy-done.14), kind=kOutput, calls=%fused_computation.51 | convolution fusion | flops 537001984 | bytes 4980736 | tf_op jit(solution)/shard_map/dot_general | solution.py:207
  108.2 15.9 %fusion.96 = (f32[2,1016]{1,0:T(2,128)S(1)}, f32[2,1016,3064]{2,1,0:T(8,128)}) fusion(pred[1016,3064]{1,0:T(8,128)(4,1)} %fusion.4, bf16[1016,128]{1,0:T(8,128)(2,1)S(1)} %copy.49, bf16[2048,128]{1,0:T(8,128)(2,1)S(1)} %bitcast.175, bf16[1024,2,64]{2,0,1:T(8,128)(2,1)S(1)} %get-tuple-element.14, bf16[1024,2,64]{2,0,1:T(8,128)(2,1)S(1)} %get-tuple-element.15), kind=kOutput, calls=%fused_computation.188 | convolution fusion | flops 1621384704 | bytes 29334016 | tf_op jit(solution)/shard_map/sub | solution.py:48
  124.1 12.3 %fusion.32 = bf16[1016,2,128]{2,0,1:T(8,128)(2,1)S(1)} fusion(f32[2,1016,3064]{2,1,0:T(8,128)} %get-tuple-element.31, f32[2,1016]{1,0:T(2,128)S(1)} %get-tuple-element.30, bf16[1016,128]{1,0:T(8,128)(2,1)S(1)} %slice.142, bf16[2048,128]{1,0:T(8,128)(2,1)S(1)} %bitcast.176), kind=kOutput, calls=%fused_computation.50 | convolution fusion | flops 1608149248 | bytes 26216896 | tf_op jit(solution)/shard_map/gck,kd->cgd/dot_general | solution.py:50
  136.5 21.1 %all-to-all-done.1 = bf16[8,256,2048]{2,1,0:T(8,128)(2,1)} async-done(((bf16[8,256,2048]{2,1,0:T(8,128)(2,1)}), bf16[8,256,2048]{2,1,0:T(8,128)(2,1)}, u32[]{:S(2)}, u32[]{:S(2)}) %all-to-all-start.1) | async-done | bytes 8388640 | tf_op jit(solution)/shard_map/all_to_all | solution.py:187
  157.6 12.5 %all-gather.5.cloned.1.call-done = bf16[3,768,2048]{2,1,0:T(8,128)(2,1)} async-done(((bf16[3,48,2048]{2,1,0:T(8,128)(2,1)}), bf16[3,768,2048]{2,1,0:T(8,128)(2,1)}) %all-gather.5.cloned.1.call-update) | async-done | bytes 9437200 | tf_op jit(solution)/shard_map/all_gather | solution.py:199
  171.2 32.9 %all-gather.7.cloned.1.call-done = bf16[1024,2048]{0,1:T(8,128)(2,1)} async-done(((bf16[1024,256]{0,1:T(8,128)(2,1)}), bf16[1024,2048]{0,1:T(8,128)(2,1)}) %all-gather.7.cloned.1.call-update) | async-done | bytes 4194320 | tf_op jit(solution)/shard_map/all_gather | solution.py:248
  204.1 14.5 %fusion.7 = (f32[1024]{0:T(1024)S(1)}, bf16[1024,2048]{1,0:T(8,128)(2,1)S(1)}) fusion(bf16[1024,2048]{0,1:T(8,128)(2,1)} %all-gather.7.cloned.1.call-done, bf16[2048,2048]{1,0:T(8,128)(2,1)} %bitcast.25, bf16[1024,2048]{1,0:T(8,128)(2,1)} %all-gather.9.cloned.1.call-done), kind=kOutput, calls=%fused_computation.26 | convolution fusion | flops 8602516480 | bytes 20975616 | tf_op jit(solution)/shard_map/dot_general | solution.py:250
  218.6 7.0 %fusion.18 = f32[1024,768]{1,0:T(8,128)S(1)} fusion(bf16[3,768,2048]{2,1,0:T(8,128)(2,1)} %all-gather.5.cloned.1.call-done, bf16[1024,2048]{1,0:T(8,128)(2,1)S(1)} %get-tuple-element.33, f32[2048]{0:T(1024)S(1)} %copy-done.17, f32[1024]{0:T(1024)S(1)} %add_rsqrt_fusion.1), kind=kOutput, calls=%fused_computation.37 | convolution fusion | flops 3229614080 | bytes 10498048 | tf_op jit(solution)/shard_map/dot_general | solution.py:255
  225.7 3.9 %multiply_convert_fusion = bf16[1024,768]{1,0:T(8,128)(2,1)S(1)} fusion(f32[1024,768]{1,0:T(8,128)S(1)} %fusion.18, bf16[3,768,2048]{2,1,0:T(8,128)(2,1)S(1)} %bitcast.145, bf16[1024,2048]{1,0:T(8,128)(2,1)S(1)} %get-tuple-element.33, f32[2048]{0:T(1024)S(1)} %copy-done.17, f32[1024]{0:T(1024)S(1)} %add_rsqrt_fusion.1), kind=kOutput, calls=%fused_computation.41 | convolution fusion | flops 3234332672 | bytes 12070912 | tf_op jit(solution)/shard_map/dot_general | solution.py:254
  229.6 5.6 %fusion.16 = f32[1024,2048]{1,0:T(8,128)} fusion(bf16[1024,768]{1,0:T(8,128)(2,1)S(1)} %multiply_convert_fusion, bf16[3,768,2048]{2,1,0:T(8,128)(2,1)S(1)} %bitcast.145), kind=kOutput, calls=%fused_computation.35 | convolution fusion | flops 3221225472 | bytes 13107200 | tf_op jit(solution)/shard_map/dot_general | solution.py:259
  235.4 2.4 fusion.14
  244.1 6.8 %collective-permute-done.3 = f32[16,2048]{1,0:T(8,128)S(1)} collective-permute-done((f32[16,2048]{1,0:T(8,128)S(1)}, f32[16,2048]{1,0:T(8,128)S(1)}, u32[]{:S(2)}, u32[]{:S(2)}) %collective-permute-start.3) | collective-permute-done | bytes 131104 | tf_op jit(solution)/shard_map/ppermute | solution.py:106
  254.6 2.8 collective-permute-start.6
  260.9 2.3 collective-permute-done.5
  263.9 3.0 collective-permute-start.9
  268.2 3.4 %collective-permute-done.9 = bf16[36,2048]{1,0:T(8,128)(2,1)S(1)} collective-permute-done((bf16[36,2048]{1,0:T(8,128)(2,1)S(1)}, bf16[36,2048]{1,0:T(8,128)(2,1)S(1)}, u32[]{:S(2)}, u32[]{:S(2)}) %collective-permute-start.9) | collective-permute-done | bytes 147488 | tf_op jit(solution)/shard_map/ppermute | solution.py:106
  274.6 4.3 %convolution_reduce_fusion = f32[144]{0:T(256)S(1)} fusion(bf16[144,2048]{1,0:T(8,128)(2,1)S(1)} %reshape.484, bf16[2048,1187]{0,1:T(8,128)(2,1)} %param.41), kind=kOutput, calls=%fused_computation.52 | convolution fusion | flops 700291840 | bytes 5452352 | tf_op jit(solution)/shard_map/dot_general | solution.py:266
  294.3 2.4 collective-permute-start.19
  299.1 2.6 collective-permute-done.18
  302.3 2.3 scatter_custom_fusion
  306.0 20.2 %all_to_all.29 = bf16[128,2,1024]{2,1,0:T(2,128)(2,1)S(1)} all-to-all(bf16[128,2,1024]{2,1,0:T(2,128)(2,1)S(1)} %reshape.576), channel_id=1, replica_groups=mesh['req'=16,'kv'=8] {'req','kv'}, dimensions={0} | all-to-all | bytes 1048576 | tf_op jit(solution)/shard_map/all_to_all | solution.py:147
  326.7 2.4 scatter_custom_fusion.1
  (176 shorter events, 62.1 us)
Async XLA Ops:
  7.2 35.9 %copy-start = (bf16[384,2048]{1,0:T(8,128)(2,1)S(1)}, bf16[384,2048]{1,0:T(8,128)(2,1)}, u32[]{:S(2)}) copy-start(bf16[384,2048]{1,0:T(8,128)(2,1)} %param.39) | copy-start | bytes 4718596
  13.5 24.7 %all-to-all-start = ((bf16[128,2,1024]{2,1,0:T(2,128)(2,1)}), bf16[128,2,1024]{2,1,0:T(2,128)(2,1)S(1)}, u32[]{:S(2)}, u32[]{:S(2)}) async-start(bf16[128,2,1024]{2,1,0:T(2,128)(2,1)} %reshape.574), calls=%async_computation | async-start | bytes 1048576 | tf_op jit(solution)/shard_map/all_to_all | solution.py:147
  24.7 60.7 %all-gather.9.cloned.1.call-start = ((), (), s32[]{:S(2)}) async-start(), calls=%async_computation.7 | async-start | bytes 4718592 | tf_op jit(solution)/shard_map/all_gather | solution.py:185
  40.7 129.3 %all-gather.5.cloned.1.call-start = ((), (), s32[]{:S(2)}) async-start(), calls=%async_computation.4 | async-start | bytes 10027008 | tf_op jit(solution)/shard_map/all_gather | solution.py:199
  49.7 107.9 %all-to-all-start.1 = ((bf16[8,256,2048]{2,1,0:T(8,128)(2,1)}), bf16[8,256,2048]{2,1,0:T(8,128)(2,1)}, u32[]{:S(2)}, u32[]{:S(2)}) async-start(bf16[8,256,2048]{2,1,0:T(8,128)(2,1)} %broadcast_in_dim.46), calls=%async_computation.1 | async-start | bytes 16777216 | tf_op jit(solution)/shard_map/all_to_all | solution.py:187
  54.8 149.3 %all-gather.7.cloned.1.call-start = ((), (), s32[]{:S(2)}) async-start(), calls=%async_computation.5 | async-start | bytes 4718592 | tf_op jit(solution)/shard_map/all_gather | solution.py:248
  56.1 32.6 %copy-start.9 = (f32[2048]{0:T(1024)S(1)}, f32[2048]{0:T(1024)}, u32[]{:S(2)}) copy-start(f32[2048]{0:T(1024)} %param.29) | copy-start | bytes 24580
  171.1 47.5 %copy-start.17 = (f32[2048]{0:T(1024)S(1)}, f32[2048]{0:T(1024)}, u32[]{:S(2)}) copy-start(f32[2048]{0:T(1024)} %param.36) | copy-start | bytes 24580
  171.1 131.2 %reduce-scatter.2.cloned.1.call-start = ((), (), s32[]{:S(2)}) async-start(), calls=%async_computation.6 | async-start | bytes 9437184 | tf_op jit(solution)/shard_map/reduce_scatter | solution.py:260
  204.1 21.6 %slice-start = ((s8[9437184]{0:T(1024)(128)(4,1)}), s8[1048576]{0:T(1024)(128)(4,1)S(1)}, s32[]{:S(2)}) async-start(s8[9437184]{0:T(1024)(128)(4,1)} %bitcast.144), calls=%async_computation.8 | async-start | bytes 2097152
  204.1 21.6 %slice-start.1 = ((s8[9437184]{0:T(1024)(128)(4,1)}), s8[4194304]{0:T(1024)(128)(4,1)S(1)}, s32[]{:S(2)}) async-start(s8[9437184]{0:T(1024)(128)(4,1)} %bitcast.144), calls=%async_computation.9 | async-start | bytes 8388608
  237.8 1.5 collective-permute-start
  239.9 11.0 %collective-permute-start.3 = (f32[16,2048]{1,0:T(8,128)S(1)}, f32[16,2048]{1,0:T(8,128)S(1)}, u32[]{:S(2)}, u32[]{:S(2)}) collective-permute-start(f32[16,2048]{1,0:T(8,128)S(1)} %fusion.116), channel_id=1, source_target_pairs={{0,6},{1,7},{2,4},{3,5},{4,2},{5,3},{6,0},{7,1},{8,14},{9,15},{10,... | collective-permute-start | bytes 393224 | tf_op jit(solution)/shard_map/ppermute | solution.py:106
  240.9 10.0 %collective-permute-start.2 = (f32[16,2048]{1,0:T(8,128)S(1)}, f32[16,2048]{1,0:T(8,128)S(1)}, u32[]{:S(2)}, u32[]{:S(2)}) collective-permute-start(f32[16,2048]{1,0:T(8,128)S(1)} %fusion.116), channel_id=1, source_target_pairs={{0,4},{1,5},{2,6},{3,7},{4,0},{5,1},{6,2},{7,3},{8,12},{9,13},{10,... | collective-permute-start | bytes 393224 | tf_op jit(solution)/shard_map/ppermute | solution.py:106
  242.6 10.2 %collective-permute-start.1 = (f32[16,2048]{1,0:T(8,128)S(1)}, f32[16,2048]{1,0:T(8,128)S(1)}, u32[]{:S(2)}, u32[]{:S(2)}) collective-permute-start(f32[16,2048]{1,0:T(8,128)S(1)} %fusion.116), channel_id=1, source_target_pairs={{0,2},{1,3},{2,0},{3,1},{4,6},{5,7},{6,4},{7,5},{8,10},{9,11},{10,... | collective-permute-start | bytes 393224 | tf_op jit(solution)/shard_map/ppermute | solution.py:106
  254.6 6.3 %collective-permute-start.6 = (bf16[9,2048]{1,0:T(8,128)(2,1)S(1)}, bf16[9,2048]{1,0:T(8,128)(2,1)S(1)}, u32[]{:S(2)}, u32[]{:S(2)}) collective-permute-start(bf16[9,2048]{1,0:T(8,128)(2,1)S(1)} %fusion.56), channel_id=1, source_target_pairs={{0,24},{8,16},{16,8},{24,0},{32,56},{40,48},{48,40},{56,32},{64,88... | collective-permute-start | bytes 110600 | tf_op jit(solution)/shard_map/ppermute | solution.py:106
  257.4 5.8 %collective-permute-start.5 = (bf16[9,2048]{1,0:T(8,128)(2,1)S(1)}, bf16[9,2048]{1,0:T(8,128)(2,1)S(1)}, u32[]{:S(2)}, u32[]{:S(2)}) collective-permute-start(bf16[9,2048]{1,0:T(8,128)(2,1)S(1)} %fusion.56), channel_id=1, source_target_pairs={{0,16},{8,24},{16,0},{24,8},{32,48},{40,56},{48,32},{56,40},{64,80... | collective-permute-start | bytes 110600 | tf_op jit(solution)/shard_map/ppermute | solution.py:106
  258.2 5.0 %collective-permute-start.4 = (bf16[9,2048]{1,0:T(8,128)(2,1)S(1)}, bf16[9,2048]{1,0:T(8,128)(2,1)S(1)}, u32[]{:S(2)}, u32[]{:S(2)}) collective-permute-start(bf16[9,2048]{1,0:T(8,128)(2,1)S(1)} %fusion.56), channel_id=1, source_target_pairs={{0,8},{8,0},{16,24},{24,16},{32,40},{40,32},{48,56},{56,48},{64,72... | collective-permute-start | bytes 110600 | tf_op jit(solution)/shard_map/ppermute | solution.py:106
  263.9 7.7 %collective-permute-start.9 = (bf16[36,2048]{1,0:T(8,128)(2,1)S(1)}, bf16[36,2048]{1,0:T(8,128)(2,1)S(1)}, u32[]{:S(2)}, u32[]{:S(2)}) collective-permute-start(bf16[36,2048]{1,0:T(8,128)(2,1)S(1)} %reshape.483), channel_id=1, source_target_pairs={{0,96},{8,104},{16,112},{24,120},{32,64},{40,72},{48,80},{56,88},{... | collective-permute-start | bytes 442376 | tf_op jit(solution)/shard_map/ppermute | solution.py:106
  266.9 6.8 %collective-permute-start.8 = (bf16[36,2048]{1,0:T(8,128)(2,1)S(1)}, bf16[36,2048]{1,0:T(8,128)(2,1)S(1)}, u32[]{:S(2)}, u32[]{:S(2)}) collective-permute-start(bf16[36,2048]{1,0:T(8,128)(2,1)S(1)} %reshape.483), channel_id=1, source_target_pairs={{0,64},{8,72},{16,80},{24,88},{32,96},{40,104},{48,112},{56,120},{... | collective-permute-start | bytes 442376 | tf_op jit(solution)/shard_map/ppermute | solution.py:106
  267.6 6.1 %collective-permute-start.7 = (bf16[36,2048]{1,0:T(8,128)(2,1)S(1)}, bf16[36,2048]{1,0:T(8,128)(2,1)S(1)}, u32[]{:S(2)}, u32[]{:S(2)}) collective-permute-start(bf16[36,2048]{1,0:T(8,128)(2,1)S(1)} %reshape.483), channel_id=1, source_target_pairs={{0,32},{8,40},{16,48},{24,56},{32,0},{40,8},{48,16},{56,24},{64,96... | collective-permute-start | bytes 442376 | tf_op jit(solution)/shard_map/ppermute | solution.py:106
  278.9 1.2 collective-permute-start.10
  280.7 5.0 %collective-permute-start.13 = (f32[144]{0:T(256)S(1)}, f32[144]{0:T(256)S(1)}, u32[]{:S(2)}, u32[]{:S(2)}) collective-permute-start(f32[144]{0:T(256)S(1)} %bitcast.167), channel_id=1, source_target_pairs={{0,6},{1,7},{2,4},{3,5},{4,2},{5,3},{6,0},{7,1},{8,14},{9,15},{10,... | collective-permute-start | bytes 1736 | tf_op jit(solution)/shard_map/ppermute | solution.py:106
  281.1 5.1 %collective-permute-start.12 = (f32[144]{0:T(256)S(1)}, f32[144]{0:T(256)S(1)}, u32[]{:S(2)}, u32[]{:S(2)}) collective-permute-start(f32[144]{0:T(256)S(1)} %bitcast.168), channel_id=1, source_target_pairs={{0,4},{1,5},{2,6},{3,7},{4,0},{5,1},{6,2},{7,3},{8,12},{9,13},{10,... | collective-permute-start | bytes 1736 | tf_op jit(solution)/shard_map/ppermute | solution.py:106
  283.4 3.7 %collective-permute-start.11 = (f32[144]{0:T(256)S(1)}, f32[144]{0:T(256)S(1)}, u32[]{:S(2)}, u32[]{:S(2)}) collective-permute-start(f32[144]{0:T(256)S(1)} %bitcast.169), channel_id=1, source_target_pairs={{0,2},{1,3},{2,0},{3,1},{4,6},{5,7},{6,4},{7,5},{8,10},{9,11},{10,... | collective-permute-start | bytes 1736 | tf_op jit(solution)/shard_map/ppermute | solution.py:106
  287.7 4.8 %collective-permute-start.16 = (f32[144]{0:T(256)S(1)}, f32[144]{0:T(256)S(1)}, u32[]{:S(2)}, u32[]{:S(2)}) collective-permute-start(f32[144]{0:T(256)S(1)} %bitcast.163), channel_id=1, source_target_pairs={{0,24},{8,16},{16,8},{24,0},{32,56},{40,48},{48,40},{56,32},{64,88... | collective-permute-start | bytes 1736 | tf_op jit(solution)/shard_map/ppermute | solution.py:106
  289.2 5.1 %collective-permute-start.15 = (f32[144]{0:T(256)S(1)}, f32[144]{0:T(256)S(1)}, u32[]{:S(2)}, u32[]{:S(2)}) collective-permute-start(f32[144]{0:T(256)S(1)} %bitcast.164), channel_id=1, source_target_pairs={{0,16},{8,24},{16,0},{24,8},{32,48},{40,56},{48,32},{56,40},{64,80... | collective-permute-start | bytes 1736 | tf_op jit(solution)/shard_map/ppermute | solution.py:106
  290.1 4.2 %collective-permute-start.14 = (f32[144]{0:T(256)S(1)}, f32[144]{0:T(256)S(1)}, u32[]{:S(2)}, u32[]{:S(2)}) collective-permute-start(f32[144]{0:T(256)S(1)} %bitcast.165), channel_id=1, source_target_pairs={{0,8},{8,0},{16,24},{24,16},{32,40},{40,32},{48,56},{56,48},{64,72... | collective-permute-start | bytes 1736 | tf_op jit(solution)/shard_map/ppermute | solution.py:106
  294.3 4.9 %collective-permute-start.19 = (f32[144]{0:T(256)S(1)}, f32[144]{0:T(256)S(1)}, u32[]{:S(2)}, u32[]{:S(2)}) collective-permute-start(f32[144]{0:T(256)S(1)} %maximum_maximum_fusion.1), channel_id=1, source_target_pairs={{0,96},{8,104},{16,112},{24,120},{32,64},{40,72},{48,80},{56,88},{... | collective-permute-start | bytes 1736 | tf_op jit(solution)/shard_map/ppermute | solution.py:106
  296.7 5.1 %collective-permute-start.18 = (f32[144]{0:T(256)S(1)}, f32[144]{0:T(256)S(1)}, u32[]{:S(2)}, u32[]{:S(2)}) collective-permute-start(f32[144]{0:T(256)S(1)} %maximum_maximum_fusion.1), channel_id=1, source_target_pairs={{0,64},{8,72},{16,80},{24,88},{32,96},{40,104},{48,112},{56,120},{... | collective-permute-start | bytes 1736 | tf_op jit(solution)/shard_map/ppermute | solution.py:106
  297.3 4.4 %collective-permute-start.17 = (f32[144]{0:T(256)S(1)}, f32[144]{0:T(256)S(1)}, u32[]{:S(2)}, u32[]{:S(2)}) collective-permute-start(f32[144]{0:T(256)S(1)} %maximum_maximum_fusion.1), channel_id=1, source_target_pairs={{0,32},{8,40},{16,48},{24,56},{32,0},{40,8},{48,16},{56,24},{64,96... | collective-permute-start | bytes 1736 | tf_op jit(solution)/shard_map/ppermute | solution.py:106
  301.8 27.3 %copy-start.1 = (bf16[384,2048]{1,0:T(8,128)(2,1)S(1)}, bf16[384,2048]{1,0:T(8,128)(2,1)}, u32[]{:S(2)}) copy-start(bf16[384,2048]{1,0:T(8,128)(2,1)} %param.39) | copy-start | bytes 4718596
  (15 other events, 91.2 us)
Sparse Core Ops, SparseCore 0:
  40.8 44.5 all-gather.8
  87.6 82.4 all-gather.4
  172.4 31.6 all-gather.6
  235.4 54.9 reduce-scatter.1

commit v13 on v12

--- a/solution.py
+++ b/solution.py
@@ -270,8 +270,8 @@
         ),
         axis=1,
     )
+    ffn_part, local_peaks = lax.optimization_barrier((ffn_part, local_peaks))
     max_logit = radix_reduce(mixed_reduce(local_peaks, "kv", jnp.maximum, (2, 4)), "req", jnp.maximum, 4)
-    ffn_part, max_logit = lax.optimization_barrier((ffn_part, max_logit))
     mine = lax.dynamic_slice_in_dim(resid, kv_index * rows_dev, rows_dev, axis=0)
     out_rows = (mine.astype(jnp.float32) + ffn_part).astype(jnp.bfloat16)
     going_back = jnp.zeros_like(out_rows).at[slot_place].set(out_rows)

time: 341 us -> 342 us (level)
  blocking collectives: 20.2 us -> 0 us
  waiting for transfers between devices: 131 us -> 142 us
  starting transfers between devices: 42.4 us -> 51.7 us
    all_to_all x1 -> x0, blocking collectives: 20.2 us -> none  [regroup(): lax.all_to_all(rows_in, ('req', 'kv'), split_axis=0, concat_axis=0, tiled...]
    reduce_scatter x1, waiting for transfers between devices: 0.01 us -> 11.5 us  [shards(): lax.psum_scatter(down_part, 'kv', scatter_dimension=0, tiled=True)]
    all_to_all x1 -> x2, starting transfers between devices: 11.1 us -> 19.8 us  [regroup(): lax.all_to_all(rows_in, ('req', 'kv'), split_axis=0, concat_axis=0, tiled...]
    all_to_all x1 -> x2, waiting for transfers between devices: 12.8 us -> 12.8 us  [regroup(): lax.all_to_all(rows_in, ('req', 'kv'), split_axis=0, concat_axis=0, tiled...]
  transfers between devices with their start and end apart: 26 -> 27, of which waited for: 20 -> 18; matrix products, arithmetic and copies ran while one was open for 23% -> 24% of each run, Pallas kernels for 0% -> 0%
where the time goes in v13:
time: 342 us; the launch traced here: 337 us
  waiting for transfers between devices  142 us (42%)
  matrix products  78 us (23%)
  starting transfers between devices  51.7 us (15%)
  local copies, waits for them, and re-layouts  27 us (8%)
  other arithmetic  22.4 us (7%)
  between operations  15.3 us (4%)
    all_gather x1, waiting for transfers between devices, shards(): lax.all_gather(pieces.reshape(tok_req, q_cols), 'kv', axis=1, tiled=True)  32.9 us
    ppermute x20, waiting for transfers between devices, radix_exchange(): got.append(lax.ppermute(value, axis, pairs))  27.9 us
    ppermute x20, starting transfers between devices, radix_exchange(): got.append(lax.ppermute(value, axis, pairs))  26.2 us
    all_gather x1, waiting for transfers between devices, shards(): rows_all = lax.all_gather(owner_rows, 'kv', axis=0, tiled=True)  23.4 us
    all_to_all x1, waiting for transfers between devices, shards(): lax.all_to_all(jnp.broadcast_to(o_proj[None], (kv_count,) + o_proj.shape)...  21.1 us
    all_to_all x2, starting transfers between devices, regroup(): lax.all_to_all(rows_in, ('req', 'kv'), split_axis=0, concat_axis=0, tiled...  19.8 us
    sub x1, matrix products, prefill_full(): expd = jnp.exp(scores - row_peak)  15.9 us
    dot_general x1, matrix products, shards(): jnp.dot(attended, o_full, preferred_element_type=jnp.float32)  14.5 us
  transfers between devices with their start and end apart: 27, of which 18 were waited for; matrix products, arithmetic and copies ran while one was open for 24% of the time, Pallas kernels for 0%

profile of v13, /device:TPU:0, one launch (start us, length us, event | category | flops | bytes accessed | tf_op | source)
XLA Modules:
  0.0 336.6 jit_solution(2238581659457027961)
XLA Ops:
  8.3 2.6 gather_fusion
  13.5 11.1 %all-to-all-start = ((bf16[128,2,1024]{2,1,0:T(2,128)(2,1)}), bf16[128,2,1024]{2,1,0:T(2,128)(2,1)S(1)}, u32[]{:S(2)}, u32[]{:S(2)}) async-start(bf16[128,2,1024]{2,1,0:T(2,128)(2,1)} %reshape.574), calls=%async_computation | async-start | bytes 1048576 | tf_op jit(solution)/shard_map/all_to_all | solution.py:147
  25.4 12.8 %all-to-all-done = bf16[128,2,1024]{2,1,0:T(2,128)(2,1)S(1)} async-done(((bf16[128,2,1024]{2,1,0:T(2,128)(2,1)}), bf16[128,2,1024]{2,1,0:T(2,128)(2,1)S(1)}, u32[]{:S(2)}, u32[]{:S(2)}) %all-to-all-start) | async-done | bytes 524320 | tf_op jit(solution)/shard_map/all_to_all | solution.py:147
  44.0 5.6 %broadcast_in_dim.46 = bf16[8,256,2048]{2,1,0:T(8,128)(2,1)} broadcast(bf16[256,2048]{1,0:T(8,128)(2,1)} %param.35), dimensions={1,2} | broadcast | bytes 9437184 | tf_op jit(solution)/shard_map/broadcast_in_dim | solution.py:188
  49.7 5.1 %all-to-all-start.1 = ((bf16[8,256,2048]{2,1,0:T(8,128)(2,1)}), bf16[8,256,2048]{2,1,0:T(8,128)(2,1)}, u32[]{:S(2)}, u32[]{:S(2)}) async-start(bf16[8,256,2048]{2,1,0:T(8,128)(2,1)} %broadcast_in_dim.46), calls=%async_computation.1 | async-start | bytes 16777216 | tf_op jit(solution)/shard_map/all_to_all | solution.py:187
  58.0 4.1 %fusion.4 = pred[1016,3064]{1,0:T(8,128)(4,1)} fusion(s32[3064]{0:T(1024)S(1)} %iota_add_fusion, pred[3064]{0:T(1024)(128)(4,1)S(1)} %get-tuple-element.34, pred[3064]{0:T(1024)(128)(4,1)S(1)} %get-tuple-element.35), kind=kLoop, calls=%fused_computation.21 | loop fusion | flops 6226048 | bytes 3131408 | tf_op jit(solution)/shard_map/jit(_where)/select_n | solution.py:45
  62.1 23.4 %all-gather.9.cloned.1.call-done = bf16[1024,2048]{1,0:T(8,128)(2,1)} async-done(((bf16[128,2048]{1,0:T(8,128)(2,1)}), bf16[1024,2048]{1,0:T(8,128)(2,1)}) %all-gather.9.cloned.1.call-update) | async-done | bytes 4194320 | tf_op jit(solution)/shard_map/all_gather | solution.py:185
  85.5 3.2 fusion.10
  94.1 3.7 %multiply_reduce_fusion.1 = (f32[1024]{0:T(1024)S(1)}, f32[1024,128]{0,1:T(8,128)S(1)}) fusion(bf16[1024,2048]{1,0:T(8,128)(2,1)} %copy-done.3, bf16[2048,128]{1,0:T(8,128)(2,1)S(1)} %copy-done.6), kind=kOutput, calls=%fused_computation.77 | convolution fusion | flops 537132032 | bytes 5246976 | tf_op jit(solution)/shard_map/dot_general | solution.py:206
  103.5 3.9 %convolution_convert_fusion = bf16[1024,128]{1,0:T(8,128)(2,1)S(1)} fusion(bf16[1024,2048]{1,0:T(8,128)(2,1)} %copy-done.3, bf16[2048,128]{1,0:T(8,128)(2,1)S(1)} %copy-done.14), kind=kOutput, calls=%fused_computation.51 | convolution fusion | flops 537001984 | bytes 4980736 | tf_op jit(solution)/shard_map/dot_general | solution.py:207
  108.2 15.9 %fusion.96 = (f32[2,1016]{1,0:T(2,128)S(1)}, f32[2,1016,3064]{2,1,0:T(8,128)}) fusion(pred[1016,3064]{1,0:T(8,128)(4,1)} %fusion.4, bf16[1016,128]{1,0:T(8,128)(2,1)S(1)} %copy.49, bf16[2048,128]{1,0:T(8,128)(2,1)S(1)} %bitcast.175, bf16[1024,2,64]{2,0,1:T(8,128)(2,1)S(1)} %get-tuple-element.14, bf16[1024,2,64]{2,0,1:T(8,128)(2,1)S(1)} %get-tuple-element.15), kind=kOutput, calls=%fused_computation.188 | convolution fusion | flops 1621384704 | bytes 29334016 | tf_op jit(solution)/shard_map/sub | solution.py:48
  124.1 12.3 %fusion.32 = bf16[1016,2,128]{2,0,1:T(8,128)(2,1)S(1)} fusion(f32[2,1016,3064]{2,1,0:T(8,128)} %get-tuple-element.31, f32[2,1016]{1,0:T(2,128)S(1)} %get-tuple-element.30, bf16[1016,128]{1,0:T(8,128)(2,1)S(1)} %slice.142, bf16[2048,128]{1,0:T(8,128)(2,1)S(1)} %bitcast.176), kind=kOutput, calls=%fused_computation.50 | convolution fusion | flops 1608149248 | bytes 26216896 | tf_op jit(solution)/shard_map/gck,kd->cgd/dot_general | solution.py:50
  136.5 21.1 %all-to-all-done.1 = bf16[8,256,2048]{2,1,0:T(8,128)(2,1)} async-done(((bf16[8,256,2048]{2,1,0:T(8,128)(2,1)}), bf16[8,256,2048]{2,1,0:T(8,128)(2,1)}, u32[]{:S(2)}, u32[]{:S(2)}) %all-to-all-start.1) | async-done | bytes 8388640 | tf_op jit(solution)/shard_map/all_to_all | solution.py:187
  157.6 12.5 %all-gather.5.cloned.1.call-done = bf16[3,768,2048]{2,1,0:T(8,128)(2,1)} async-done(((bf16[3,48,2048]{2,1,0:T(8,128)(2,1)}), bf16[3,768,2048]{2,1,0:T(8,128)(2,1)}) %all-gather.5.cloned.1.call-update) | async-done | bytes 9437200 | tf_op jit(solution)/shard_map/all_gather | solution.py:199
  171.2 32.9 %all-gather.7.cloned.1.call-done = bf16[1024,2048]{0,1:T(8,128)(2,1)} async-done(((bf16[1024,256]{0,1:T(8,128)(2,1)}), bf16[1024,2048]{0,1:T(8,128)(2,1)}) %all-gather.7.cloned.1.call-update) | async-done | bytes 4194320 | tf_op jit(solution)/shard_map/all_gather | solution.py:248
  204.1 14.5 %fusion.7 = (f32[1024]{0:T(1024)S(1)}, bf16[1024,2048]{1,0:T(8,128)(2,1)S(1)}) fusion(bf16[1024,2048]{0,1:T(8,128)(2,1)} %all-gather.7.cloned.1.call-done, bf16[2048,2048]{1,0:T(8,128)(2,1)} %bitcast.25, bf16[1024,2048]{1,0:T(8,128)(2,1)} %all-gather.9.cloned.1.call-done), kind=kOutput, calls=%fused_computation.26 | convolution fusion | flops 8602516480 | bytes 20975616 | tf_op jit(solution)/shard_map/dot_general | solution.py:250
  218.7 7.0 %fusion.18 = f32[1024,768]{1,0:T(8,128)S(1)} fusion(bf16[3,768,2048]{2,1,0:T(8,128)(2,1)} %all-gather.5.cloned.1.call-done, bf16[1024,2048]{1,0:T(8,128)(2,1)S(1)} %get-tuple-element.33, f32[2048]{0:T(1024)S(1)} %copy-done.17, f32[1024]{0:T(1024)S(1)} %add_rsqrt_fusion.1), kind=kOutput, calls=%fused_computation.37 | convolution fusion | flops 3229614080 | bytes 10498048 | tf_op jit(solution)/shard_map/dot_general | solution.py:255
  225.7 3.9 %multiply_convert_fusion = bf16[1024,768]{1,0:T(8,128)(2,1)S(1)} fusion(f32[1024,768]{1,0:T(8,128)S(1)} %fusion.18, bf16[3,768,2048]{2,1,0:T(8,128)(2,1)S(1)} %bitcast.145, bf16[1024,2048]{1,0:T(8,128)(2,1)S(1)} %get-tuple-element.33, f32[2048]{0:T(1024)S(1)} %copy-done.17, f32[1024]{0:T(1024)S(1)} %add_rsqrt_fusion.1), kind=kOutput, calls=%fused_computation.41 | convolution fusion | flops 3234332672 | bytes 12070912 | tf_op jit(solution)/shard_map/dot_general | solution.py:254
  229.6 5.6 %fusion.16 = f32[1024,2048]{1,0:T(8,128)} fusion(bf16[1024,768]{1,0:T(8,128)(2,1)S(1)} %multiply_convert_fusion, bf16[3,768,2048]{2,1,0:T(8,128)(2,1)S(1)} %bitcast.145), kind=kOutput, calls=%fused_computation.35 | convolution fusion | flops 3221225472 | bytes 13107200 | tf_op jit(solution)/shard_map/dot_general | solution.py:259
  235.4 2.4 fusion.14
  244.1 6.8 %collective-permute-done.3 = f32[16,2048]{1,0:T(8,128)S(1)} collective-permute-done((f32[16,2048]{1,0:T(8,128)S(1)}, f32[16,2048]{1,0:T(8,128)S(1)}, u32[]{:S(2)}, u32[]{:S(2)}) %collective-permute-start.3) | collective-permute-done | bytes 131104 | tf_op jit(solution)/shard_map/ppermute | solution.py:106
  254.6 2.8 collective-permute-start.6
  263.9 3.0 collective-permute-start.9
  268.1 3.4 %collective-permute-done.9 = bf16[36,2048]{1,0:T(8,128)(2,1)S(1)} collective-permute-done((bf16[36,2048]{1,0:T(8,128)(2,1)S(1)}, bf16[36,2048]{1,0:T(8,128)(2,1)S(1)}, u32[]{:S(2)}, u32[]{:S(2)}) %collective-permute-start.9) | collective-permute-done | bytes 147488 | tf_op jit(solution)/shard_map/ppermute | solution.py:106
  274.6 4.3 %convolution_reduce_fusion = f32[144]{0:T(256)S(1)} fusion(bf16[144,2048]{1,0:T(8,128)(2,1)S(1)} %reshape.484, bf16[2048,1187]{0,1:T(8,128)(2,1)} %param.41), kind=kOutput, calls=%fused_computation.52 | convolution fusion | flops 700291840 | bytes 5452352 | tf_op jit(solution)/shard_map/dot_general | solution.py:266
  278.8 11.5 %reduce-scatter.2.cloned.1.call-done = f32[128,2048]{1,0:T(8,128)} async-done(((f32[1024,2048]{1,0:T(8,128)}), f32[128,2048]{1,0:T(8,128)}) %reduce-scatter.2.cloned.1.call-update) | async-done | bytes 1048592 | tf_op jit(solution)/shard_map/reduce_scatter | solution.py:260
  296.4 2.4 scatter_custom_fusion
  301.0 8.6 %all-to-all-start.2 = ((bf16[128,2,1024]{2,1,0:T(2,128)(2,1)}), bf16[128,2,1024]{2,1,0:T(2,128)(2,1)S(1)}, u32[]{:S(2)}, u32[]{:S(2)}) async-start(bf16[128,2,1024]{2,1,0:T(2,128)(2,1)} %reshape.576), calls=%async_computation.3 | async-start | bytes 1048576 | tf_op jit(solution)/shard_map/all_to_all | solution.py:147
  315.3 2.5 collective-permute-done.15
  317.8 3.6 %collective-permute-start.19 = (f32[144]{0:T(256)S(1)}, f32[144]{0:T(256)S(1)}, u32[]{:S(2)}, u32[]{:S(2)}) collective-permute-start(f32[144]{0:T(256)S(1)} %maximum_maximum_fusion.1), channel_id=1, source_target_pairs={{0,96},{8,104},{16,112},{24,120},{32,64},{40,72},{48,80},{56,88},{... | collective-permute-start | bytes 1736 | tf_op jit(solution)/shard_map/ppermute | solution.py:106
  322.9 3.5 %collective-permute-done.18 = f32[144]{0:T(256)S(1)} collective-permute-done((f32[144]{0:T(256)S(1)}, f32[144]{0:T(256)S(1)}, u32[]{:S(2)}, u32[]{:S(2)}) %collective-permute-start.18) | collective-permute-done | bytes 608 | tf_op jit(solution)/shard_map/ppermute | solution.py:106
  327.4 2.4 scatter_custom_fusion.1
  (177 shorter events, 62.8 us)
Async XLA Ops:
  7.2 35.9 %copy-start = (bf16[384,2048]{1,0:T(8,128)(2,1)S(1)}, bf16[384,2048]{1,0:T(8,128)(2,1)}, u32[]{:S(2)}) copy-start(bf16[384,2048]{1,0:T(8,128)(2,1)} %param.39) | copy-start | bytes 4718596
  13.5 24.7 %all-to-all-start = ((bf16[128,2,1024]{2,1,0:T(2,128)(2,1)}), bf16[128,2,1024]{2,1,0:T(2,128)(2,1)S(1)}, u32[]{:S(2)}, u32[]{:S(2)}) async-start(bf16[128,2,1024]{2,1,0:T(2,128)(2,1)} %reshape.574), calls=%async_computation | async-start | bytes 1048576 | tf_op jit(solution)/shard_map/all_to_all | solution.py:147
  24.7 60.8 %all-gather.9.cloned.1.call-start = ((), (), s32[]{:S(2)}) async-start(), calls=%async_computation.7 | async-start | bytes 4718592 | tf_op jit(solution)/shard_map/all_gather | solution.py:185
  40.7 129.4 %all-gather.5.cloned.1.call-start = ((), (), s32[]{:S(2)}) async-start(), calls=%async_computation.4 | async-start | bytes 10027008 | tf_op jit(solution)/shard_map/all_gather | solution.py:199
  49.7 107.9 %all-to-all-start.1 = ((bf16[8,256,2048]{2,1,0:T(8,128)(2,1)}), bf16[8,256,2048]{2,1,0:T(8,128)(2,1)}, u32[]{:S(2)}, u32[]{:S(2)}) async-start(bf16[8,256,2048]{2,1,0:T(8,128)(2,1)} %broadcast_in_dim.46), calls=%async_computation.1 | async-start | bytes 16777216 | tf_op jit(solution)/shard_map/all_to_all | solution.py:187
  54.8 149.3 %all-gather.7.cloned.1.call-start = ((), (), s32[]{:S(2)}) async-start(), calls=%async_computation.5 | async-start | bytes 4718592 | tf_op jit(solution)/shard_map/all_gather | solution.py:248
  56.1 32.6 %copy-start.9 = (f32[2048]{0:T(1024)S(1)}, f32[2048]{0:T(1024)}, u32[]{:S(2)}) copy-start(f32[2048]{0:T(1024)} %param.29) | copy-start | bytes 24580
  171.1 47.5 %copy-start.17 = (f32[2048]{0:T(1024)S(1)}, f32[2048]{0:T(1024)}, u32[]{:S(2)}) copy-start(f32[2048]{0:T(1024)} %param.36) | copy-start | bytes 24580
  171.1 119.3 %reduce-scatter.2.cloned.1.call-start = ((), (), s32[]{:S(2)}) async-start(), calls=%async_computation.6 | async-start | bytes 9437184 | tf_op jit(solution)/shard_map/reduce_scatter | solution.py:260
  204.1 21.6 %slice-start.1 = ((s8[9437184]{0:T(1024)(128)(4,1)}), s8[4194304]{0:T(1024)(128)(4,1)S(1)}, s32[]{:S(2)}) async-start(s8[9437184]{0:T(1024)(128)(4,1)} %bitcast.144), calls=%async_computation.9 | async-start | bytes 8388608
  237.8 1.5 collective-permute-start
  239.9 11.0 %collective-permute-start.3 = (f32[16,2048]{1,0:T(8,128)S(1)}, f32[16,2048]{1,0:T(8,128)S(1)}, u32[]{:S(2)}, u32[]{:S(2)}) collective-permute-start(f32[16,2048]{1,0:T(8,128)S(1)} %fusion.116), channel_id=1, source_target_pairs={{0,6},{1,7},{2,4},{3,5},{4,2},{5,3},{6,0},{7,1},{8,14},{9,15},{10,... | collective-permute-start | bytes 393224 | tf_op jit(solution)/shard_map/ppermute | solution.py:106
  240.9 10.1 %collective-permute-start.2 = (f32[16,2048]{1,0:T(8,128)S(1)}, f32[16,2048]{1,0:T(8,128)S(1)}, u32[]{:S(2)}, u32[]{:S(2)}) collective-permute-start(f32[16,2048]{1,0:T(8,128)S(1)} %fusion.116), channel_id=1, source_target_pairs={{0,4},{1,5},{2,6},{3,7},{4,0},{5,1},{6,2},{7,3},{8,12},{9,13},{10,... | collective-permute-start | bytes 393224 | tf_op jit(solution)/shard_map/ppermute | solution.py:106
  242.5 10.3 %collective-permute-start.1 = (f32[16,2048]{1,0:T(8,128)S(1)}, f32[16,2048]{1,0:T(8,128)S(1)}, u32[]{:S(2)}, u32[]{:S(2)}) collective-permute-start(f32[16,2048]{1,0:T(8,128)S(1)} %fusion.116), channel_id=1, source_target_pairs={{0,2},{1,3},{2,0},{3,1},{4,6},{5,7},{6,4},{7,5},{8,10},{9,11},{10,... | collective-permute-start | bytes 393224 | tf_op jit(solution)/shard_map/ppermute | solution.py:106
  254.6 6.3 %collective-permute-start.6 = (bf16[9,2048]{1,0:T(8,128)(2,1)S(1)}, bf16[9,2048]{1,0:T(8,128)(2,1)S(1)}, u32[]{:S(2)}, u32[]{:S(2)}) collective-permute-start(bf16[9,2048]{1,0:T(8,128)(2,1)S(1)} %fusion.56), channel_id=1, source_target_pairs={{0,24},{8,16},{16,8},{24,0},{32,56},{40,48},{48,40},{56,32},{64,88... | collective-permute-start | bytes 110600 | tf_op jit(solution)/shard_map/ppermute | solution.py:106
  257.4 5.8 %collective-permute-start.5 = (bf16[9,2048]{1,0:T(8,128)(2,1)S(1)}, bf16[9,2048]{1,0:T(8,128)(2,1)S(1)}, u32[]{:S(2)}, u32[]{:S(2)}) collective-permute-start(bf16[9,2048]{1,0:T(8,128)(2,1)S(1)} %fusion.56), channel_id=1, source_target_pairs={{0,16},{8,24},{16,0},{24,8},{32,48},{40,56},{48,32},{56,40},{64,80... | collective-permute-start | bytes 110600 | tf_op jit(solution)/shard_map/ppermute | solution.py:106
  258.2 4.9 %collective-permute-start.4 = (bf16[9,2048]{1,0:T(8,128)(2,1)S(1)}, bf16[9,2048]{1,0:T(8,128)(2,1)S(1)}, u32[]{:S(2)}, u32[]{:S(2)}) collective-permute-start(bf16[9,2048]{1,0:T(8,128)(2,1)S(1)} %fusion.56), channel_id=1, source_target_pairs={{0,8},{8,0},{16,24},{24,16},{32,40},{40,32},{48,56},{56,48},{64,72... | collective-permute-start | bytes 110600 | tf_op jit(solution)/shard_map/ppermute | solution.py:106
  263.9 7.7 %collective-permute-start.9 = (bf16[36,2048]{1,0:T(8,128)(2,1)S(1)}, bf16[36,2048]{1,0:T(8,128)(2,1)S(1)}, u32[]{:S(2)}, u32[]{:S(2)}) collective-permute-start(bf16[36,2048]{1,0:T(8,128)(2,1)S(1)} %reshape.483), channel_id=1, source_target_pairs={{0,96},{8,104},{16,112},{24,120},{32,64},{40,72},{48,80},{56,88},{... | collective-permute-start | bytes 442376 | tf_op jit(solution)/shard_map/ppermute | solution.py:106
  266.9 6.8 %collective-permute-start.8 = (bf16[36,2048]{1,0:T(8,128)(2,1)S(1)}, bf16[36,2048]{1,0:T(8,128)(2,1)S(1)}, u32[]{:S(2)}, u32[]{:S(2)}) collective-permute-start(bf16[36,2048]{1,0:T(8,128)(2,1)S(1)} %reshape.483), channel_id=1, source_target_pairs={{0,64},{8,72},{16,80},{24,88},{32,96},{40,104},{48,112},{56,120},{... | collective-permute-start | bytes 442376 | tf_op jit(solution)/shard_map/ppermute | solution.py:106
  267.6 6.1 %collective-permute-start.7 = (bf16[36,2048]{1,0:T(8,128)(2,1)S(1)}, bf16[36,2048]{1,0:T(8,128)(2,1)S(1)}, u32[]{:S(2)}, u32[]{:S(2)}) collective-permute-start(bf16[36,2048]{1,0:T(8,128)(2,1)S(1)} %reshape.483), channel_id=1, source_target_pairs={{0,32},{8,40},{16,48},{24,56},{32,0},{40,8},{48,16},{56,24},{64,96... | collective-permute-start | bytes 442376 | tf_op jit(solution)/shard_map/ppermute | solution.py:106
  290.4 1.3 collective-permute-start.10
  292.2 17.4 %collective-permute-start.13 = (f32[144]{0:T(256)S(1)}, f32[144]{0:T(256)S(1)}, u32[]{:S(2)}, u32[]{:S(2)}) collective-permute-start(f32[144]{0:T(256)S(1)} %bitcast.167), channel_id=1, source_target_pairs={{0,6},{1,7},{2,4},{3,5},{4,2},{5,3},{6,0},{7,1},{8,14},{9,15},{10,... | collective-permute-start | bytes 1736 | tf_op jit(solution)/shard_map/ppermute | solution.py:106
  293.7 16.0 %collective-permute-start.12 = (f32[144]{0:T(256)S(1)}, f32[144]{0:T(256)S(1)}, u32[]{:S(2)}, u32[]{:S(2)}) collective-permute-start(f32[144]{0:T(256)S(1)} %bitcast.168), channel_id=1, source_target_pairs={{0,4},{1,5},{2,6},{3,7},{4,0},{5,1},{6,2},{7,3},{8,12},{9,13},{10,... | collective-permute-start | bytes 1736 | tf_op jit(solution)/shard_map/ppermute | solution.py:106
  295.4 14.3 %collective-permute-start.11 = (f32[144]{0:T(256)S(1)}, f32[144]{0:T(256)S(1)}, u32[]{:S(2)}, u32[]{:S(2)}) collective-permute-start(f32[144]{0:T(256)S(1)} %bitcast.169), channel_id=1, source_target_pairs={{0,2},{1,3},{2,0},{3,1},{4,6},{5,7},{6,4},{7,5},{8,10},{9,11},{10,... | collective-permute-start | bytes 1736 | tf_op jit(solution)/shard_map/ppermute | solution.py:106
  296.4 33.5 %copy-start.1 = (bf16[384,2048]{1,0:T(8,128)(2,1)S(1)}, bf16[384,2048]{1,0:T(8,128)(2,1)}, u32[]{:S(2)}) copy-start(bf16[384,2048]{1,0:T(8,128)(2,1)} %param.39) | copy-start | bytes 4718596
  301.0 26.0 %all-to-all-start.2 = ((bf16[128,2,1024]{2,1,0:T(2,128)(2,1)}), bf16[128,2,1024]{2,1,0:T(2,128)(2,1)S(1)}, u32[]{:S(2)}, u32[]{:S(2)}) async-start(bf16[128,2,1024]{2,1,0:T(2,128)(2,1)} %reshape.576), calls=%async_computation.3 | async-start | bytes 1048576 | tf_op jit(solution)/shard_map/all_to_all | solution.py:147
  310.3 4.9 %collective-permute-start.16 = (f32[144]{0:T(256)S(1)}, f32[144]{0:T(256)S(1)}, u32[]{:S(2)}, u32[]{:S(2)}) collective-permute-start(f32[144]{0:T(256)S(1)} %bitcast.163), channel_id=1, source_target_pairs={{0,24},{8,16},{16,8},{24,0},{32,56},{40,48},{48,40},{56,32},{64,88... | collective-permute-start | bytes 1736 | tf_op jit(solution)/shard_map/ppermute | solution.py:106
  312.6 5.1 %collective-permute-start.15 = (f32[144]{0:T(256)S(1)}, f32[144]{0:T(256)S(1)}, u32[]{:S(2)}, u32[]{:S(2)}) collective-permute-start(f32[144]{0:T(256)S(1)} %bitcast.164), channel_id=1, source_target_pairs={{0,16},{8,24},{16,0},{24,8},{32,48},{40,56},{48,32},{56,40},{64,80... | collective-permute-start | bytes 1736 | tf_op jit(solution)/shard_map/ppermute | solution.py:106
  313.4 4.3 %collective-permute-start.14 = (f32[144]{0:T(256)S(1)}, f32[144]{0:T(256)S(1)}, u32[]{:S(2)}, u32[]{:S(2)}) collective-permute-start(f32[144]{0:T(256)S(1)} %bitcast.165), channel_id=1, source_target_pairs={{0,8},{8,0},{16,24},{24,16},{32,40},{40,32},{48,56},{56,48},{64,72... | collective-permute-start | bytes 1736 | tf_op jit(solution)/shard_map/ppermute | solution.py:106
  317.8 5.1 %collective-permute-start.19 = (f32[144]{0:T(256)S(1)}, f32[144]{0:T(256)S(1)}, u32[]{:S(2)}, u32[]{:S(2)}) collective-permute-start(f32[144]{0:T(256)S(1)} %maximum_maximum_fusion.1), channel_id=1, source_target_pairs={{0,96},{8,104},{16,112},{24,120},{32,64},{40,72},{48,80},{56,88},{... | collective-permute-start | bytes 1736 | tf_op jit(solution)/shard_map/ppermute | solution.py:106
  321.3 5.1 %collective-permute-start.18 = (f32[144]{0:T(256)S(1)}, f32[144]{0:T(256)S(1)}, u32[]{:S(2)}, u32[]{:S(2)}) collective-permute-start(f32[144]{0:T(256)S(1)} %maximum_maximum_fusion.1), channel_id=1, source_target_pairs={{0,64},{8,72},{16,80},{24,88},{32,96},{40,104},{48,112},{56,120},{... | collective-permute-start | bytes 1736 | tf_op jit(solution)/shard_map/ppermute | solution.py:106
  321.7 4.8 %collective-permute-start.17 = (f32[144]{0:T(256)S(1)}, f32[144]{0:T(256)S(1)}, u32[]{:S(2)}, u32[]{:S(2)}) collective-permute-start(f32[144]{0:T(256)S(1)} %maximum_maximum_fusion.1), channel_id=1, source_target_pairs={{0,32},{8,40},{16,48},{24,56},{32,0},{40,8},{48,16},{56,24},{64,96... | collective-permute-start | bytes 1736 | tf_op jit(solution)/shard_map/ppermute | solution.py:106
  (16 other events, 112.8 us)
Sparse Core Ops, SparseCore 0:
  40.8 44.5 all-gather.8
  87.6 82.4 all-gather.4
  172.4 31.6 all-gather.6
  235.4 54.9 reduce-scatter.1
